TPU v7x, 256 devices: a whole 4x4x8 slice. The times are simulated.
256 devices in a mesh: row: 64 (over z, y, core), col: 4 (over x).
Axes of the slice: x: 4, y: 4, z: 8, core: 2. Of those that a mesh axis runs over, the one named last changes fastest.
Arguments:
- train_points: float32 [16, 3, 64, 128], P(None, None, 'row'), may hold values from -6 to 6
- new_points: float32 [16, 256], replicated, may hold values from -6 to 6
- lengthscales: float32 [16], replicated, may hold values from 2.5 to 6
- factor: float32 [3, 64, 128, 3, 4, 2048], P(None, 'row', None, None, 'col'), may hold values from -0.02734375 to 0.02734375
- diag_inverse: float32 [3, 64, 128, 4, 2048], P(None, 'row', None, 'col'), may hold values from -3 to 3
Outputs:
- solution: float32 [3, 4, 64, 32, 256], P(None, 'col', 'row')
All inputs are finite; a program needn't handle non-finite values.
Results may differ from a plain program's by a relative error of at most 0.0001.
Values sent between devices are 32-bit elements; how exact they have to be, the bound alone decides.
No kernel may reach another device: no remote copies, remote signals or barrier semaphores. Data moves between devices by JAX's collectives and lax.ppermute only.
A program may use at most 128 MiB of HBM per device.

v0:
```python
import functools

import jax
import jax.numpy as jnp
from jax import lax
from jax.experimental import pallas as pl
from jax.experimental.pallas import tpu as pltpu
from jax.sharding import Mesh, PartitionSpec as P

Z, Y, CORE, N_COL = 8, 4, 2, 4
LANES = 128


def shift(value, axis, by, size):
    return lax.ppermute(value, axis, [(i, (i + by) % size) for i in range(size)])


def halves(value):
    high = value.astype(jnp.bfloat16)
    return high, (value - high.astype(jnp.float32)).astype(jnp.bfloat16)


def dot3(left, right, contract):
    left_high, left_low = left
    right_high, right_low = right
    dot = functools.partial(
        lax.dot_general,
        dimension_numbers=(contract, ((), ())),
        preferred_element_type=jnp.float32,
    )
    return dot(left_low, right_high) + dot(left_high, right_low) + dot(left_high, right_high)


def split_kernel(n_blocks, place, *refs):
    block_refs, extra_refs, outs, flat = refs[:n_blocks], refs[n_blocks : -Y - 1], refs[-Y - 1 : -1], refs[-1]
    y = place[1]
    rows, columns = flat.shape
    half = columns // (Z * Y)
    for at, block_ref in enumerate(block_refs):
        flat[...] = block_ref[...].reshape(rows, columns)
        left = lax.broadcasted_iota(jnp.int32, (rows, LANES), 1) < half
        for e in range(Y):
            to = lax.rem(y + e, Y)
            odd = lax.rem(to, 2) == 1
            for pair in range(Z // 2):
                tiles = []
                for z in (2 * pair, 2 * pair + 1):
                    start = pl.multiple_of((z * 2 + to // 2) * LANES, LANES)
                    tiles.append(flat[:, pl.ds(start, LANES)])
                first, second = tiles
                value = jnp.where(
                    left,
                    jnp.where(odd, pltpu.roll(first, half, axis=1), first),
                    jnp.where(odd, second, pltpu.roll(second, half, axis=1)),
                )
                outs[e][at, :rows, pair * LANES : (pair + 1) * LANES] = value
    for points_ref in extra_refs:
        more = points_ref.shape[0] // 2
        points = points_ref[...].reshape(2 * more, LANES)
        for out_ref in outs:
            out_ref[0, rows:, :] = jnp.zeros((more, out_ref.shape[2]), jnp.float32)
            out_ref[0, rows:, :LANES] = points[:more]
            out_ref[0, rows:, LANES : 2 * LANES] = points[more:]


def split_columns(place, blocks, extra=None):
    specs, arrays = [], []
    rows, columns = blocks[0][0].shape[2], blocks[0][0].shape[-1]
    for array, at in blocks:
        arrays.append(array)
        if array.ndim == 5:
            specs.append(
                pl.BlockSpec((None, None, rows, None, columns), lambda i, place, at=at: (at[0], 0, 0, 0, 0))
            )
        else:
            specs.append(
                pl.BlockSpec(
                    (None, None, rows, None, None, columns),
                    lambda i, place, at=at: (at[0], 0, 0, at[1], 0, 0),
                )
            )
    more = 0
    if extra is not None:
        arrays.append(extra)
        dims, _, _, width = extra.shape
        specs.append(pl.BlockSpec((dims, None, None, width), lambda i, place: (0, 0, 0, 0)))
        more = dims // 2
    out = jax.ShapeDtypeStruct((len(blocks), rows + more, columns // Y), jnp.float32)
    return pl.pallas_call(
        functools.partial(split_kernel, len(blocks)),
        out_shape=[out] * Y,
        grid_spec=pltpu.PrefetchScalarGridSpec(
            num_scalar_prefetch=1,
            grid=(1,),
            in_specs=specs,
            out_specs=[pl.BlockSpec(out.shape, lambda i, place: (0, 0, 0))] * Y,
            scratch_shapes=[pltpu.VMEM((rows, columns), jnp.float32)],
        ),
        cost_estimate=pl.CostEstimate(
            flops=len(blocks) * rows * columns,
            bytes_accessed=len(blocks) * rows * columns * 8,
            transcendentals=0,
        ),
        compiler_params=pltpu.CompilerParams(vmem_limit_bytes=54 << 20),
    )(place, *arrays)


def inverse_kernel(place, *refs):
    residuals, blocks = refs[:Y], refs[Y : 2 * Y]
    keep_ref, send_ref, high, low, product = refs[2 * Y :]
    core = place[2]
    rows = blocks[0].shape[0]
    parts = [halves(ref[...]) for ref in residuals]
    residual = tuple(jnp.concatenate([part[i] for part in parts]) for i in range(2))
    for e in range(Y):
        high[e * rows : (e + 1) * rows, :], low[e * rows : (e + 1) * rows, :] = halves(blocks[e][...])
    columns = high.shape[1]
    step = 256
    for start in range(0, columns, step):
        part = slice(start, start + step)
        product[part, :] = dot3((high[:, part], low[:, part]), residual, ((0,), (0,)))
    share = keep_ref.shape[1]
    for z in range(Z):
        for out_ref, owner in ((send_ref, 1 - core), (keep_ref, core)):
            start = pl.multiple_of((z * CORE + owner) * share, share)
            out_ref[z] = product[pl.ds(start, share), :]


def apply_inverse(place, residuals, blocks):
    rows, new = residuals[0].shape
    columns = blocks[0].shape[-1]
    out = jax.ShapeDtypeStruct((Z, columns // (Z * CORE), new), jnp.float32)
    return pl.pallas_call(
        inverse_kernel,
        out_shape=(out, out),
        grid_spec=pltpu.PrefetchScalarGridSpec(
            num_scalar_prefetch=1,
            grid=(1,),
            in_specs=[pl.BlockSpec((rows, new), lambda i, place: (0, 0))] * Y
            + [pl.BlockSpec((None, rows, columns), lambda i, place: (0, 0, 0))] * Y,
            out_specs=[pl.BlockSpec(out.shape, lambda i, place: (0, 0, 0))] * 2,
            scratch_shapes=[pltpu.VMEM((Y * rows, columns), jnp.bfloat16)] * 2
            + [pltpu.VMEM((columns, new), jnp.float32)],
        ),
        cost_estimate=pl.CostEstimate(
            flops=6 * Y * rows * columns * new, bytes_accessed=4 << 20, transcendentals=0
        ),
        compiler_params=pltpu.CompilerParams(vmem_limit_bytes=32 << 20),
    )(place, *residuals, *blocks)


def halve_kernel(block_ref, high_ref, low_ref, flat):
    flat[...] = block_ref[...]
    step = 16

    def part(i, carry):
        where = pl.ds(pl.multiple_of(i * step, step), step)
        high_ref[where, :], low_ref[where, :] = halves(flat[where, :])
        return carry

    lax.fori_loop(0, flat.shape[0] // step, part, 0)


def halve_block(factor, row, column):
    rows, columns = factor.shape[2], factor.shape[5]
    out = jax.ShapeDtypeStruct((rows, columns), jnp.bfloat16)
    return pl.pallas_call(
        halve_kernel,
        out_shape=(out, out),
        grid=(1,),
        in_specs=[
            pl.BlockSpec(
                (None, None, rows, None, None, columns), lambda i: (row, 0, 0, column, 0, 0)
            )
        ],
        out_specs=[pl.BlockSpec(out.shape, lambda i: (0, 0))] * 2,
        scratch_shapes=[pltpu.VMEM(out.shape, jnp.float32)],
        cost_estimate=pl.CostEstimate(
            flops=4 * rows * columns, bytes_accessed=8 * rows * columns, transcendentals=0
        ),
        compiler_params=pltpu.CompilerParams(vmem_limit_bytes=56 << 20),
    )(factor)


def factor_kernel(place, block_high, block_low, *refs):
    pieces, rest, (out_ref, high, low) = refs[: Y + 1], refs[Y + 1], refs[Y + 2 :]
    y, core = place[1], place[2]
    share = pieces[0].shape[1]

    def put(z, carry):
        for at, owner in enumerate((core, 1 - core)):
            for e in range(Y):
                row = (z * Y + lax.rem(y + Y - e, Y)) * CORE + owner
                where = pl.ds(pl.multiple_of(row * share, share), share)
                piece = rest[e - 1, z] if at and e else pieces[at * Y + e][z]
                high[where, :], low[where, :] = halves(piece)
        return carry

    lax.fori_loop(0, Z, put, 0)
    out_ref[...] = dot3(
        (block_high[...], block_low[...]), (high[...], low[...]), ((1,), (0,))
    )


def apply_factor(place, block, pieces):
    rows, columns = block[0].shape
    new = pieces[0].shape[-1]
    return pl.pallas_call(
        factor_kernel,
        out_shape=jax.ShapeDtypeStruct((rows, new), jnp.float32),
        grid_spec=pltpu.PrefetchScalarGridSpec(
            num_scalar_prefetch=1,
            grid=(1,),
            in_specs=[pl.BlockSpec((rows, columns), lambda i, place: (0, 0))] * 2
            + [pl.BlockSpec(pieces[0].shape, lambda i, place: (0, 0, 0))] * (Y + 1)
            + [pl.BlockSpec(pieces[-1].shape, lambda i, place: (0, 0, 0, 0))],
            out_specs=pl.BlockSpec((rows, new), lambda i, place: (0, 0)),
            scratch_shapes=[pltpu.VMEM((columns, new), jnp.bfloat16)] * 2,
        ),
        cost_estimate=pl.CostEstimate(
            flops=6 * rows * columns * new, bytes_accessed=3 << 20, transcendentals=0
        ),
        compiler_params=pltpu.CompilerParams(vmem_limit_bytes=32 << 20),
    )(place, *block, *pieces)


def spread(arrays, steps=(2, 1, 3)):
    return {e: shift(arrays[e], "y", e, Y) for e in steps}


def in_order(own, arrived):
    return [own] + [arrived[e] for e in range(1, Y)]


def kernel_rows(scaled_train, scaled_new):
    inner_products = jnp.dot(scaled_train.T, scaled_new, precision=lax.Precision.HIGHEST)
    sqdist = (
        jnp.sum(scaled_train * scaled_train, axis=0)[:, None]
        + jnp.sum(scaled_new * scaled_new, axis=0)[None, :]
        - 2.0 * inner_products
    )
    return jnp.exp(-0.5 * sqdist)


def on_device(train_points, new_points, lengthscales, factor, diag_inverse):
    dims, panels, _, block_rows = train_points.shape
    new_count = new_points.shape[1]
    place = jnp.stack([lax.axis_index(axis) for axis in ("z", "y", "core")]).astype(jnp.int32)
    scaled_new = new_points / lengthscales[:, None]

    w0 = split_columns(place, [(diag_inverse, (0,))], train_points)
    w0 = in_order(w0[0], spread(w0))
    w1 = split_columns(place, [(diag_inverse, (1,))])
    w2 = split_columns(place, [(diag_inverse, (2,))])
    l10, l20, l21 = (halve_block(factor, *at) for at in ((1, 0), (2, 0), (2, 1)))
    w0, w1, l10, l20 = lax.optimization_barrier((w0, w1, l10, l20))

    own_points = (train_points[:, 1:, 0] / lengthscales[:, None, None]).reshape(dims, -1)
    kernel = kernel_rows(own_points, scaled_new).reshape(panels - 1, block_rows, new_count)

    both = jnp.concatenate([part[0, block_rows:, : 2 * block_rows] for part in w0]).reshape(
        Y, dims // 2, 2, block_rows
    )
    line_points = both.transpose(2, 1, 0, 3).reshape(dims, Y, block_rows)
    line_points = (line_points / lengthscales[:, None, None]).reshape(dims, -1)
    residuals = kernel_rows(line_points, scaled_new).reshape(Y, block_rows, new_count)
    residuals = [residuals[e] for e in range(Y)]

    def reduce(keep, send):
        chip = keep + shift(send, "core", 1, CORE)
        return jnp.sum(lax.all_to_all(chip, "z", 0, 0), axis=0)

    def gather_z(rows):
        return lax.all_to_all(jnp.broadcast_to(rows[None], (Z,) + rows.shape), "z", 0, 0)

    def gather(line):
        mine = in_order(line, spread({e: line for e in range(1, Y)}))
        rest = shift(jnp.stack(mine[1:]), "core", 1, CORE)
        return mine + [shift(line, "core", 1, CORE), rest]

    def residual_rows(panel, own):
        arrived = [shift(own, "col", by, N_COL) for by in (2, 1, 3)]
        rest = kernel[panel - 1] - (own + arrived[0] + arrived[1] + arrived[2])
        return in_order(rest, spread({e: rest for e in range(1, Y)}))

    def solve(residuals, blocks, later, during_sum, during_gather):
        rows = reduce(*apply_inverse(place, residuals, blocks))
        far = spread(later, (2,))
        rows, far, later, during_sum = lax.optimization_barrier((rows, far, later, during_sum))
        line = gather_z(rows)
        near = spread(later, (1, 3))
        line, near, during_gather = lax.optimization_barrier((line, near, during_gather))
        return rows, line, in_order(later[0], {**far, **near}), during_sum, during_gather

    rows_0, line, w1, w2, l21 = solve(residuals, w0, w1, w2, l21)
    pieces = gather(line)
    residuals = residual_rows(1, apply_factor(place, l10, pieces))
    early = apply_factor(place, l20, pieces)

    residuals, w2, early = lax.optimization_barrier((residuals, w2, early))
    rows_1, line, w2, _, _ = solve(residuals, w1, w2, (), ())
    pieces = gather(line)
    residuals = residual_rows(2, early + apply_factor(place, l21, pieces))

    rows_2 = reduce(*apply_inverse(place, residuals, w2))
    return jnp.stack([rows_0, rows_1, rows_2])[:, None, None]


def solution(mesh):
    split = Mesh(
        mesh.devices.reshape(Z, Y, CORE, mesh.devices.shape[1]), ("z", "y", "core", "col")
    )
    row = ("z", "y", "core")
    return jax.shard_map(
        on_device,
        mesh=split,
        in_specs=(
            P(None, None, row, None),
            P(),
            P(),
            P(None, row, None, None, "col", None),
            P(None, row, None, "col", None),
        ),
        out_specs=P(None, "col", row, None, None),
        check_vma=False,
    )
```

profile of v0, /device:TPU:2, one launch (start us, length us, event | category | flops | bytes accessed | tf_op | source)
XLA Modules:
  0.0 196.6 jit_solution(16161796940772120464)
XLA Ops:
  0.6 3.6 %shard_map.55 = (f32[1,136,512]{2,1,0:T(8,128)}, f32[1,136,512]{2,1,0:T(8,128)}, f32[1,136,512]{2,1,0:T(8,128)}, f32[1,136,512]{2,1,0:T(8,128)}) custom-call(s32[3]{0:T(128)} %pad_add_fusion.place, f32[3,1,128,1,2048]{4,3,2,1,0:T(1,128)} %refs_0_.5, f32[16,3,1,128]{3,2,1,0:T(1,128)} %refs_1_.1), custom_call_target="tpu_custom_call" | custom-call | flops 262144 | bytes 2097152 | tf_op jit(solution)/shard_map/pallas_call | solution.py:89
  4.3 1.6 collective-permute-start
  5.9 2.9 %collective-permute-start.1 = (f32[1,136,512]{2,1,0:T(8,128)}, f32[1,136,512]{2,1,0:T(8,128)S(1)}, u32[]{:S(2)}, u32[]{:S(2)}) collective-permute-start(f32[1,136,512]{2,1,0:T(8,128)} %get-tuple-element.74), channel_id=1, source_target_pairs={{0,16},{8,24},{16,0},{24,8},{1,17},{9,25},{17,1},{25,9},{2,18},{10... | collective-permute-start | bytes 835592 | tf_op jit(solution)/shard_map/ppermute | solution.py:15
  10.1 3.6 %shard_map.56 = (f32[1,128,512]{2,1,0:T(8,128)}, f32[1,128,512]{2,1,0:T(8,128)}, f32[1,128,512]{2,1,0:T(8,128)}, f32[1,128,512]{2,1,0:T(8,128)}) custom-call(s32[3]{0:T(128)} %pad_add_fusion.place, f32[3,1,128,1,2048]{4,3,2,1,0:T(1,128)} %refs_0_.5), custom_call_target="tpu_custom_call" | custom-call | flops 262144 | bytes 2097152 | tf_op jit(solution)/shard_map/pallas_call | solution.py:89
  14.5 2.6 %shard_map.57 = (bf16[128,2048]{1,0:T(8,128)(2,1)}, bf16[128,2048]{1,0:T(8,128)(2,1)}) custom-call(f32[3,1,128,3,1,2048]{5,4,3,2,1,0:T(1,128)} %block_ref.5), custom_call_target="tpu_custom_call" | custom-call | flops 1048576 | bytes 2097152 | tf_op jit(solution)/shard_map/pallas_call | solution.py:167
  17.0 2.6 %shard_map.58 = (bf16[128,2048]{1,0:T(8,128)(2,1)}, bf16[128,2048]{1,0:T(8,128)(2,1)}) custom-call(f32[3,1,128,3,1,2048]{5,4,3,2,1,0:T(1,128)} %block_ref.5), custom_call_target="tpu_custom_call" | custom-call | flops 1048576 | bytes 2097152 | tf_op jit(solution)/shard_map/pallas_call | solution.py:167
  19.7 1.6 collective-permute-done.1.refs_6_
  23.6 1.5 collective-permute-done.3
  25.9 8.5 %all-to-all-start = ((f32[8,32,256]{2,1,0:T(8,128)}), f32[8,32,256]{2,1,0:T(8,128)S(1)}, u32[]{:S(2)}, u32[]{:S(2)}) async-start(f32[8,32,256]{2,1,0:T(8,128)} %add.64), calls=%async_computation | async-start | bytes 524288 | tf_op jit(solution)/shard_map/all_to_all | solution.py:271
  34.4 2.7 %collective-permute-start.4 = (f32[1,128,512]{2,1,0:T(8,128)S(1)}, f32[1,128,512]{2,1,0:T(8,128)S(1)}, u32[]{:S(2)}, u32[]{:S(2)}) collective-permute-start(f32[1,128,512]{2,1,0:T(8,128)S(1)} %copy-done.22), channel_id=1, source_target_pairs={{0,16},{8,24},{16,0},{24,8},{1,17},{9,25},{17,1},{25,9},{2,18},{10... | collective-permute-start | bytes 786440 | tf_op jit(solution)/shard_map/ppermute | solution.py:15
  37.0 3.6 %shard_map.60 = (f32[1,128,512]{2,1,0:T(8,128)}, f32[1,128,512]{2,1,0:T(8,128)}, f32[1,128,512]{2,1,0:T(8,128)}, f32[1,128,512]{2,1,0:T(8,128)}) custom-call(s32[3]{0:T(128)} %pad_add_fusion.place, f32[3,1,128,1,2048]{4,3,2,1,0:T(1,128)} %refs_0_.5), custom_call_target="tpu_custom_call" | custom-call | flops 262144 | bytes 2097152 | tf_op jit(solution)/shard_map/pallas_call | solution.py:89
  40.6 5.9 %all-to-all-done = f32[8,32,256]{2,1,0:T(8,128)S(1)} async-done(((f32[8,32,256]{2,1,0:T(8,128)}), f32[8,32,256]{2,1,0:T(8,128)S(1)}, u32[]{:S(2)}, u32[]{:S(2)}) %all-to-all-start) | async-done | bytes 262176 | tf_op jit(solution)/shard_map/all_to_all | solution.py:271
  47.4 4.4 %all-to-all-start.1 = ((f32[8,32,256]{2,1,0:T(8,128)}), f32[8,32,256]{2,1,0:T(8,128)S(1)}, u32[]{:S(2)}, u32[]{:S(2)}) async-start(f32[8,32,256]{2,1,0:T(8,128)} %broadcast_in_dim.6), calls=%async_computation.1 | async-start | bytes 524288 | tf_op jit(solution)/shard_map/all_to_all | solution.py:274
  52.9 2.1 %collective-permute-start.6 = (f32[1,128,512]{2,1,0:T(8,128)}, f32[1,128,512]{2,1,0:T(8,128)S(1)}, u32[]{:S(2)}, u32[]{:S(2)}) collective-permute-start(f32[1,128,512]{2,1,0:T(8,128)} %get-tuple-element.102), channel_id=1, source_target_pairs={{0,24},{8,0},{16,8},{24,16},{1,25},{9,1},{17,9},{25,17},{2,26},{10... | collective-permute-start | bytes 786440 | tf_op jit(solution)/shard_map/ppermute | solution.py:15
  55.0 2.5 %shard_map.61 = (bf16[128,2048]{1,0:T(8,128)(2,1)}, bf16[128,2048]{1,0:T(8,128)(2,1)}) custom-call(f32[3,1,128,3,1,2048]{5,4,3,2,1,0:T(1,128)} %block_ref.5), custom_call_target="tpu_custom_call" | custom-call | flops 1048576 | bytes 2097152 | tf_op jit(solution)/shard_map/pallas_call | solution.py:167
  57.5 2.3 %collective-permute-done.5.refs_5_ = f32[1,128,512]{2,1,0:T(8,128)S(1)} collective-permute-done((f32[1,128,512]{2,1,0:T(8,128)}, f32[1,128,512]{2,1,0:T(8,128)S(1)}, u32[]{:S(2)}, u32[]{:S(2)}) %collective-permute-start.5) | collective-permute-done | bytes 262176 | tf_op jit(solution)/shard_map/ppermute | solution.py:15
  63.7 2.4 %collective-permute-start.8 = (f32[8,32,256]{2,1,0:T(8,128)S(1)}, f32[8,32,256]{2,1,0:T(8,128)S(1)}, u32[]{:S(2)}, u32[]{:S(2)}) collective-permute-start(f32[8,32,256]{2,1,0:T(8,128)S(1)} %all-to-all-done.1.refs_0_), channel_id=1, source_target_pairs={{0,16},{8,24},{16,0},{24,8},{1,17},{9,25},{17,1},{25,9},{2,18},{10... | collective-permute-start | bytes 786440 | tf_op jit(solution)/shard_map/ppermute | solution.py:15
  66.1 1.7 collective-permute-start.9
  67.7 4.3 %collective-permute-done.7.refs_1_ = f32[8,32,256]{2,1,0:T(8,128)S(1)} collective-permute-done((f32[8,32,256]{2,1,0:T(8,128)S(1)}, f32[8,32,256]{2,1,0:T(8,128)S(1)}, u32[]{:S(2)}, u32[]{:S(2)}) %collective-permute-start.7) | collective-permute-done | bytes 262176 | tf_op jit(solution)/shard_map/ppermute | solution.py:15
  72.0 2.8 %collective-permute-done.8.refs_2_ = f32[8,32,256]{2,1,0:T(8,128)S(1)} collective-permute-done((f32[8,32,256]{2,1,0:T(8,128)S(1)}, f32[8,32,256]{2,1,0:T(8,128)S(1)}, u32[]{:S(2)}, u32[]{:S(2)}) %collective-permute-start.8) | collective-permute-done | bytes 262176 | tf_op jit(solution)/shard_map/ppermute | solution.py:15
  76.1 2.0 %collective-permute-done.10.refs_4_ = f32[8,32,256]{2,1,0:T(8,128)S(1)} collective-permute-done((f32[8,32,256]{2,1,0:T(8,128)S(1)}, f32[8,32,256]{2,1,0:T(8,128)S(1)}, u32[]{:S(2)}, u32[]{:S(2)}) %collective-permute-start.10) | collective-permute-done | bytes 262176 | tf_op jit(solution)/shard_map/ppermute | solution.py:15
  78.2 1.5 shard_map.62
  79.7 2.2 %collective-permute-start.12 = (f32[128,256]{1,0:T(8,128)S(1)}, f32[128,256]{1,0:T(8,128)S(1)}, u32[]{:S(2)}, u32[]{:S(2)}) collective-permute-start(f32[128,256]{1,0:T(8,128)S(1)} %shard_map.62), channel_id=1, source_target_pairs={{0,2},{1,3},{2,0},{3,1},{4,6},{5,7},{6,4},{7,5},{8,10},{9,11},{10,... | collective-permute-start | bytes 393224 | tf_op jit(solution)/shard_map/ppermute | solution.py:15
  81.9 2.0 %collective-permute-start.14 = (f32[128,256]{1,0:T(8,128)S(1)}, f32[128,256]{1,0:T(8,128)S(1)}, u32[]{:S(2)}, u32[]{:S(2)}) collective-permute-start(f32[128,256]{1,0:T(8,128)S(1)} %shard_map.62), channel_id=1, source_target_pairs={{0,3},{1,0},{2,1},{3,2},{4,7},{5,4},{6,5},{7,6},{8,11},{9,8},{10,9... | collective-permute-start | bytes 393224 | tf_op jit(solution)/shard_map/ppermute | solution.py:15
  84.4 3.2 %collective-permute-done.12 = f32[128,256]{1,0:T(8,128)S(1)} collective-permute-done((f32[128,256]{1,0:T(8,128)S(1)}, f32[128,256]{1,0:T(8,128)S(1)}, u32[]{:S(2)}, u32[]{:S(2)}) %collective-permute-start.12) | collective-permute-done | bytes 131104 | tf_op jit(solution)/shard_map/ppermute | solution.py:15
  87.6 2.0 %collective-permute-done.13 = f32[128,256]{1,0:T(8,128)S(1)} collective-permute-done((f32[128,256]{1,0:T(8,128)S(1)}, f32[128,256]{1,0:T(8,128)S(1)}, u32[]{:S(2)}, u32[]{:S(2)}) %collective-permute-start.13) | collective-permute-done | bytes 131104 | tf_op jit(solution)/shard_map/ppermute | solution.py:15
  89.7 1.8 collective-permute-start.15
  91.5 2.4 %collective-permute-start.16 = (f32[128,256]{1,0:T(8,128)S(1)}, f32[128,256]{1,0:T(8,128)S(1)}, u32[]{:S(2)}, u32[]{:S(2)}) collective-permute-start(f32[128,256]{1,0:T(8,128)S(1)} %slice_subtract_fusion.1.refs_0_), channel_id=1, source_target_pairs={{0,16},{8,24},{16,0},{24,8},{1,17},{9,25},{17,1},{25,9},{2,18},{10... | collective-permute-start | bytes 393224 | tf_op jit(solution)/shard_map/ppermute | solution.py:15
  96.6 3.5 %collective-permute-done.16.refs_2_ = f32[128,256]{1,0:T(8,128)S(1)} collective-permute-done((f32[128,256]{1,0:T(8,128)S(1)}, f32[128,256]{1,0:T(8,128)S(1)}, u32[]{:S(2)}, u32[]{:S(2)}) %collective-permute-start.16) | collective-permute-done | bytes 131104 | tf_op jit(solution)/shard_map/ppermute | solution.py:15
  101.4 1.5 collective-permute-done.18
  103.6 6.0 %all-to-all-start.2 = ((f32[8,32,256]{2,1,0:T(8,128)}), f32[8,32,256]{2,1,0:T(8,128)S(1)}, u32[]{:S(2)}, u32[]{:S(2)}) async-start(f32[8,32,256]{2,1,0:T(8,128)} %add.72), calls=%async_computation.2 | async-start | bytes 524288 | tf_op jit(solution)/shard_map/all_to_all | solution.py:271
  110.8 11.1 %all-to-all-done.2 = f32[8,32,256]{2,1,0:T(8,128)S(1)} async-done(((f32[8,32,256]{2,1,0:T(8,128)}), f32[8,32,256]{2,1,0:T(8,128)S(1)}, u32[]{:S(2)}, u32[]{:S(2)}) %all-to-all-start.2) | async-done | bytes 262176 | tf_op jit(solution)/shard_map/all_to_all | solution.py:271
  122.6 4.5 %all-to-all-start.3 = ((f32[8,32,256]{2,1,0:T(8,128)}), f32[8,32,256]{2,1,0:T(8,128)S(1)}, u32[]{:S(2)}, u32[]{:S(2)}) async-start(f32[8,32,256]{2,1,0:T(8,128)} %broadcast_in_dim.7), calls=%async_computation.3 | async-start | bytes 524288 | tf_op jit(solution)/shard_map/all_to_all | solution.py:274
  127.6 2.7 %collective-permute-start.21 = (f32[1,128,512]{2,1,0:T(8,128)}, f32[1,128,512]{2,1,0:T(8,128)S(1)}, u32[]{:S(2)}, u32[]{:S(2)}) collective-permute-start(f32[1,128,512]{2,1,0:T(8,128)} %get-tuple-element.131), channel_id=1, source_target_pairs={{0,24},{8,0},{16,8},{24,16},{1,25},{9,1},{17,9},{25,17},{2,26},{10... | collective-permute-start | bytes 786440 | tf_op jit(solution)/shard_map/ppermute | solution.py:15
  130.3 4.8 %collective-permute-done.20.refs_5_ = f32[1,128,512]{2,1,0:T(8,128)S(1)} collective-permute-done((f32[1,128,512]{2,1,0:T(8,128)}, f32[1,128,512]{2,1,0:T(8,128)S(1)}, u32[]{:S(2)}, u32[]{:S(2)}) %collective-permute-start.20) | collective-permute-done | bytes 262176 | tf_op jit(solution)/shard_map/ppermute | solution.py:15
  135.1 2.7 %all-to-all-done.3.refs_0_ = f32[8,32,256]{2,1,0:T(8,128)S(1)} async-done(((f32[8,32,256]{2,1,0:T(8,128)}), f32[8,32,256]{2,1,0:T(8,128)S(1)}, u32[]{:S(2)}, u32[]{:S(2)}) %all-to-all-start.3) | async-done | bytes 262176 | tf_op jit(solution)/shard_map/all_to_all | solution.py:274
  138.3 3.4 %collective-permute-start.23 = (f32[8,32,256]{2,1,0:T(8,128)S(1)}, f32[8,32,256]{2,1,0:T(8,128)S(1)}, u32[]{:S(2)}, u32[]{:S(2)}) collective-permute-start(f32[8,32,256]{2,1,0:T(8,128)S(1)} %all-to-all-done.3.refs_0_), channel_id=1, source_target_pairs={{0,16},{8,24},{16,0},{24,8},{1,17},{9,25},{17,1},{25,9},{2,18},{10... | collective-permute-start | bytes 786440 | tf_op jit(solution)/shard_map/ppermute | solution.py:15
  141.7 5.9 %collective-permute-done.22.refs_1_ = f32[8,32,256]{2,1,0:T(8,128)S(1)} collective-permute-done((f32[8,32,256]{2,1,0:T(8,128)S(1)}, f32[8,32,256]{2,1,0:T(8,128)S(1)}, u32[]{:S(2)}, u32[]{:S(2)}) %collective-permute-start.22) | collective-permute-done | bytes 262176 | tf_op jit(solution)/shard_map/ppermute | solution.py:15
  147.6 2.8 %collective-permute-done.23.refs_2_ = f32[8,32,256]{2,1,0:T(8,128)S(1)} collective-permute-done((f32[8,32,256]{2,1,0:T(8,128)S(1)}, f32[8,32,256]{2,1,0:T(8,128)S(1)}, u32[]{:S(2)}, u32[]{:S(2)}) %collective-permute-start.23) | collective-permute-done | bytes 262176 | tf_op jit(solution)/shard_map/ppermute | solution.py:15
  151.3 2.1 %collective-permute-done.25.refs_4_ = f32[8,32,256]{2,1,0:T(8,128)S(1)} collective-permute-done((f32[8,32,256]{2,1,0:T(8,128)S(1)}, f32[8,32,256]{2,1,0:T(8,128)S(1)}, u32[]{:S(2)}, u32[]{:S(2)}) %collective-permute-start.25) | collective-permute-done | bytes 262176 | tf_op jit(solution)/shard_map/ppermute | solution.py:15
  155.0 1.7 collective-permute-start.27
  156.9 1.9 collective-permute-start.29
  158.8 4.2 %collective-permute-done.27 = f32[128,256]{1,0:T(8,128)S(1)} collective-permute-done((f32[128,256]{1,0:T(8,128)S(1)}, f32[128,256]{1,0:T(8,128)S(1)}, u32[]{:S(2)}, u32[]{:S(2)}) %collective-permute-start.27) | collective-permute-done | bytes 131104 | tf_op jit(solution)/shard_map/ppermute | solution.py:15
  165.5 3.6 %collective-permute-start.31 = (f32[128,256]{1,0:T(8,128)S(1)}, f32[128,256]{1,0:T(8,128)S(1)}, u32[]{:S(2)}, u32[]{:S(2)}) collective-permute-start(f32[128,256]{1,0:T(8,128)S(1)} %slice_subtract_fusion.refs_0_), channel_id=1, source_target_pairs={{0,16},{8,24},{16,0},{24,8},{1,17},{9,25},{17,1},{25,9},{2,18},{10... | collective-permute-start | bytes 393224 | tf_op jit(solution)/shard_map/ppermute | solution.py:15
  169.1 2.7 %collective-permute-done.30.refs_1_ = f32[128,256]{1,0:T(8,128)S(1)} collective-permute-done((f32[128,256]{1,0:T(8,128)S(1)}, f32[128,256]{1,0:T(8,128)S(1)}, u32[]{:S(2)}, u32[]{:S(2)}) %collective-permute-start.30) | collective-permute-done | bytes 131104 | tf_op jit(solution)/shard_map/ppermute | solution.py:15
  171.8 3.5 %collective-permute-done.31.refs_2_ = f32[128,256]{1,0:T(8,128)S(1)} collective-permute-done((f32[128,256]{1,0:T(8,128)S(1)}, f32[128,256]{1,0:T(8,128)S(1)}, u32[]{:S(2)}, u32[]{:S(2)}) %collective-permute-start.31) | collective-permute-done | bytes 131104 | tf_op jit(solution)/shard_map/ppermute | solution.py:15
  177.6 1.5 collective-permute-done.33
  179.2 16.8 %all_to_all.25 = f32[8,32,256]{2,1,0:T(8,128)S(1)} all-to-all(f32[8,32,256]{2,1,0:T(8,128)S(1)} %add.77), channel_id=1, replica_groups=mesh['z'=8,'y'=4,'core'=2,'col'=4] {'z'}, dimensions={0} | all-to-all | bytes 524288 | tf_op jit(solution)/shard_map/all_to_all | solution.py:271
  (111 shorter events, 29.1 us)
Async XLA Ops:
  4.3 15.4 %collective-permute-start = (f32[1,136,512]{2,1,0:T(8,128)}, f32[1,136,512]{2,1,0:T(8,128)S(1)}, u32[]{:S(2)}, u32[]{:S(2)}) collective-permute-start(f32[1,136,512]{2,1,0:T(8,128)} %get-tuple-element.73), channel_id=1, source_target_pairs={{0,8},{8,16},{16,24},{24,0},{1,9},{9,17},{17,25},{25,1},{2,10},{10... | collective-permute-start | bytes 835592 | tf_op jit(solution)/shard_map/ppermute | solution.py:15
  5.9 15.5 %collective-permute-start.1 = (f32[1,136,512]{2,1,0:T(8,128)}, f32[1,136,512]{2,1,0:T(8,128)S(1)}, u32[]{:S(2)}, u32[]{:S(2)}) collective-permute-start(f32[1,136,512]{2,1,0:T(8,128)} %get-tuple-element.74), channel_id=1, source_target_pairs={{0,16},{8,24},{16,0},{24,8},{1,17},{9,25},{17,1},{25,9},{2,18},{10... | collective-permute-start | bytes 835592 | tf_op jit(solution)/shard_map/ppermute | solution.py:15
  8.8 12.6 %collective-permute-start.2 = (f32[1,136,512]{2,1,0:T(8,128)}, f32[1,136,512]{2,1,0:T(8,128)S(1)}, u32[]{:S(2)}, u32[]{:S(2)}) collective-permute-start(f32[1,136,512]{2,1,0:T(8,128)} %get-tuple-element.75), channel_id=1, source_target_pairs={{0,24},{8,0},{16,8},{24,16},{1,25},{9,1},{17,9},{25,17},{2,26},{10... | collective-permute-start | bytes 835592 | tf_op jit(solution)/shard_map/ppermute | solution.py:15
  22.2 53.8 %copy-start.19 = (f32[16,3,1,128]{3,2,1,0:T(1,128)S(1)}, f32[16,3,1,128]{3,2,1,0:T(1,128)}, u32[]{:S(2)}) copy-start(f32[16,3,1,128]{3,2,1,0:T(1,128)} %refs_1_.1) | copy-start | bytes 73732
  22.2 55.9 %copy-start.4 = (bf16[128,2048]{1,0:T(8,128)(2,1)S(1)}, bf16[128,2048]{1,0:T(8,128)(2,1)}, u32[]{:S(2)}) copy-start(bf16[128,2048]{1,0:T(8,128)(2,1)} %get-tuple-element.99.block_high) | copy-start | bytes 1572868
  22.2 55.9 %copy-start.5 = (bf16[128,2048]{1,0:T(8,128)(2,1)S(1)}, bf16[128,2048]{1,0:T(8,128)(2,1)}, u32[]{:S(2)}) copy-start(bf16[128,2048]{1,0:T(8,128)(2,1)} %get-tuple-element.100.block_low) | copy-start | bytes 1572868
  22.2 55.9 %copy-start.16 = (s32[3]{0:T(128)S(1)}, s32[3]{0:T(128)}, u32[]{:S(2)}) copy-start(s32[3]{0:T(128)} %pad_add_fusion.place) | copy-start | bytes 40
  23.5 1.6 collective-permute-start.3
  25.9 20.7 %all-to-all-start = ((f32[8,32,256]{2,1,0:T(8,128)}), f32[8,32,256]{2,1,0:T(8,128)S(1)}, u32[]{:S(2)}, u32[]{:S(2)}) async-start(f32[8,32,256]{2,1,0:T(8,128)} %add.64), calls=%async_computation | async-start | bytes 524288 | tf_op jit(solution)/shard_map/all_to_all | solution.py:271
  34.4 60.7 %copy-start.2 = (bf16[128,2048]{1,0:T(8,128)(2,1)S(1)}, bf16[128,2048]{1,0:T(8,128)(2,1)}, u32[]{:S(2)}) copy-start(bf16[128,2048]{1,0:T(8,128)(2,1)} %get-tuple-element.110.block_high) | copy-start | bytes 1572868
  34.4 60.7 %copy-start.3 = (bf16[128,2048]{1,0:T(8,128)(2,1)S(1)}, bf16[128,2048]{1,0:T(8,128)(2,1)}, u32[]{:S(2)}) copy-start(bf16[128,2048]{1,0:T(8,128)(2,1)} %get-tuple-element.111.block_low) | copy-start | bytes 1572868
  34.4 12.2 %collective-permute-start.4 = (f32[1,128,512]{2,1,0:T(8,128)S(1)}, f32[1,128,512]{2,1,0:T(8,128)S(1)}, u32[]{:S(2)}, u32[]{:S(2)}) collective-permute-start(f32[1,128,512]{2,1,0:T(8,128)S(1)} %copy-done.22), channel_id=1, source_target_pairs={{0,16},{8,24},{16,0},{24,8},{1,17},{9,25},{17,1},{25,9},{2,18},{10... | collective-permute-start | bytes 786440 | tf_op jit(solution)/shard_map/ppermute | solution.py:15
  47.4 15.1 %all-to-all-start.1 = ((f32[8,32,256]{2,1,0:T(8,128)}), f32[8,32,256]{2,1,0:T(8,128)S(1)}, u32[]{:S(2)}, u32[]{:S(2)}) async-start(f32[8,32,256]{2,1,0:T(8,128)} %broadcast_in_dim.6), calls=%async_computation.1 | async-start | bytes 524288 | tf_op jit(solution)/shard_map/all_to_all | solution.py:274
  51.7 8.0 %collective-permute-start.5 = (f32[1,128,512]{2,1,0:T(8,128)}, f32[1,128,512]{2,1,0:T(8,128)S(1)}, u32[]{:S(2)}, u32[]{:S(2)}) collective-permute-start(f32[1,128,512]{2,1,0:T(8,128)} %get-tuple-element.101), channel_id=1, source_target_pairs={{0,8},{8,16},{16,24},{24,0},{1,9},{9,17},{17,25},{25,1},{2,10},{10... | collective-permute-start | bytes 786440 | tf_op jit(solution)/shard_map/ppermute | solution.py:15
  52.9 7.6 %collective-permute-start.6 = (f32[1,128,512]{2,1,0:T(8,128)}, f32[1,128,512]{2,1,0:T(8,128)S(1)}, u32[]{:S(2)}, u32[]{:S(2)}) collective-permute-start(f32[1,128,512]{2,1,0:T(8,128)} %get-tuple-element.102), channel_id=1, source_target_pairs={{0,24},{8,0},{16,8},{24,16},{1,25},{9,1},{17,9},{25,17},{2,26},{10... | collective-permute-start | bytes 786440 | tf_op jit(solution)/shard_map/ppermute | solution.py:15
  57.5 96.0 %copy-start = (bf16[128,2048]{1,0:T(8,128)(2,1)S(1)}, bf16[128,2048]{1,0:T(8,128)(2,1)}, u32[]{:S(2)}) copy-start(bf16[128,2048]{1,0:T(8,128)(2,1)} %get-tuple-element.128.block_high) | copy-start | bytes 1572868
  57.5 96.0 %copy-start.1 = (bf16[128,2048]{1,0:T(8,128)(2,1)S(1)}, bf16[128,2048]{1,0:T(8,128)(2,1)}, u32[]{:S(2)}) copy-start(bf16[128,2048]{1,0:T(8,128)(2,1)} %get-tuple-element.129.block_low) | copy-start | bytes 1572868
  62.4 37.6 %copy-start.14 = (f32[1,128,512]{2,1,0:T(8,128)S(1)}, f32[1,128,512]{2,1,0:T(8,128)}, u32[]{:S(2)}) copy-start(f32[1,128,512]{2,1,0:T(8,128)} %copy-done.13) | copy-start | bytes 786436
  62.5 9.5 %collective-permute-start.7 = (f32[8,32,256]{2,1,0:T(8,128)S(1)}, f32[8,32,256]{2,1,0:T(8,128)S(1)}, u32[]{:S(2)}, u32[]{:S(2)}) collective-permute-start(f32[8,32,256]{2,1,0:T(8,128)S(1)} %all-to-all-done.1.refs_0_), channel_id=1, source_target_pairs={{0,8},{8,16},{16,24},{24,0},{1,9},{9,17},{17,25},{25,1},{2,10},{10... | collective-permute-start | bytes 786440 | tf_op jit(solution)/shard_map/ppermute | solution.py:15
  63.7 11.2 %collective-permute-start.8 = (f32[8,32,256]{2,1,0:T(8,128)S(1)}, f32[8,32,256]{2,1,0:T(8,128)S(1)}, u32[]{:S(2)}, u32[]{:S(2)}) collective-permute-start(f32[8,32,256]{2,1,0:T(8,128)S(1)} %all-to-all-done.1.refs_0_), channel_id=1, source_target_pairs={{0,16},{8,24},{16,0},{24,8},{1,17},{9,25},{17,1},{25,9},{2,18},{10... | collective-permute-start | bytes 786440 | tf_op jit(solution)/shard_map/ppermute | solution.py:15
  66.1 9.1 %collective-permute-start.9 = (f32[8,32,256]{2,1,0:T(8,128)S(1)}, f32[8,32,256]{2,1,0:T(8,128)S(1)}, u32[]{:S(2)}, u32[]{:S(2)}) collective-permute-start(f32[8,32,256]{2,1,0:T(8,128)S(1)} %all-to-all-done.1.refs_0_), channel_id=1, source_target_pairs={{0,24},{8,0},{16,8},{24,16},{1,25},{9,1},{17,9},{25,17},{2,26},{10... | collective-permute-start | bytes 786440 | tf_op jit(solution)/shard_map/ppermute | solution.py:15
  75.2 2.9 %collective-permute-start.11 = (f32[3,8,32,256]{3,2,1,0:T(8,128)S(1)}, f32[3,8,32,256]{3,2,1,0:T(8,128)S(1)}, u32[]{:S(2)}, u32[]{:S(2)}) collective-permute-start(f32[3,8,32,256]{3,2,1,0:T(8,128)S(1)} %pad_maximum_fusion), channel_id=1, source_target_pairs={{0,4},{4,0},{1,5},{5,1},{2,6},{6,2},{3,7},{7,3},{8,12},{12,8},{9,1... | collective-permute-start | bytes 2359304 | tf_op jit(solution)/shard_map/ppermute | solution.py:15
  75.5 2.6 %collective-permute-start.10 = (f32[8,32,256]{2,1,0:T(8,128)S(1)}, f32[8,32,256]{2,1,0:T(8,128)S(1)}, u32[]{:S(2)}, u32[]{:S(2)}) collective-permute-start(f32[8,32,256]{2,1,0:T(8,128)S(1)} %all-to-all-done.1.refs_0_), channel_id=1, source_target_pairs={{0,4},{4,0},{1,5},{5,1},{2,6},{6,2},{3,7},{7,3},{8,12},{12,8},{9,1... | collective-permute-start | bytes 786440 | tf_op jit(solution)/shard_map/ppermute | solution.py:15
  79.7 116.3 %copy-start.18 = (f32[32,256]{1,0:T(8,128)S(1)}, f32[32,256]{1,0:T(8,128)}, u32[]{:S(2)}) copy-start(f32[32,256]{1,0:T(8,128)} %copy-done.17) | copy-start | bytes 98308
  79.7 8.0 %collective-permute-start.12 = (f32[128,256]{1,0:T(8,128)S(1)}, f32[128,256]{1,0:T(8,128)S(1)}, u32[]{:S(2)}, u32[]{:S(2)}) collective-permute-start(f32[128,256]{1,0:T(8,128)S(1)} %shard_map.62), channel_id=1, source_target_pairs={{0,2},{1,3},{2,0},{3,1},{4,6},{5,7},{6,4},{7,5},{8,10},{9,11},{10,... | collective-permute-start | bytes 393224 | tf_op jit(solution)/shard_map/ppermute | solution.py:15
  81.9 7.8 %collective-permute-start.13 = (f32[128,256]{1,0:T(8,128)S(1)}, f32[128,256]{1,0:T(8,128)S(1)}, u32[]{:S(2)}, u32[]{:S(2)}) collective-permute-start(f32[128,256]{1,0:T(8,128)S(1)} %shard_map.62), channel_id=1, source_target_pairs={{0,1},{1,2},{2,3},{3,0},{4,5},{5,6},{6,7},{7,4},{8,9},{9,10},{10,1... | collective-permute-start | bytes 393224 | tf_op jit(solution)/shard_map/ppermute | solution.py:15
  81.9 7.8 %collective-permute-start.14 = (f32[128,256]{1,0:T(8,128)S(1)}, f32[128,256]{1,0:T(8,128)S(1)}, u32[]{:S(2)}, u32[]{:S(2)}) collective-permute-start(f32[128,256]{1,0:T(8,128)S(1)} %shard_map.62), channel_id=1, source_target_pairs={{0,3},{1,0},{2,1},{3,2},{4,7},{5,4},{6,5},{7,6},{8,11},{9,8},{10,9... | collective-permute-start | bytes 393224 | tf_op jit(solution)/shard_map/ppermute | solution.py:15
  89.7 6.8 %collective-permute-start.15 = (f32[128,256]{1,0:T(8,128)S(1)}, f32[128,256]{1,0:T(8,128)S(1)}, u32[]{:S(2)}, u32[]{:S(2)}) collective-permute-start(f32[128,256]{1,0:T(8,128)S(1)} %slice_subtract_fusion.1.refs_0_), channel_id=1, source_target_pairs={{0,8},{8,16},{16,24},{24,0},{1,9},{9,17},{17,25},{25,1},{2,10},{10... | collective-permute-start | bytes 393224 | tf_op jit(solution)/shard_map/ppermute | solution.py:15
  91.5 8.5 %collective-permute-start.16 = (f32[128,256]{1,0:T(8,128)S(1)}, f32[128,256]{1,0:T(8,128)S(1)}, u32[]{:S(2)}, u32[]{:S(2)}) collective-permute-start(f32[128,256]{1,0:T(8,128)S(1)} %slice_subtract_fusion.1.refs_0_), channel_id=1, source_target_pairs={{0,16},{8,24},{16,0},{24,8},{1,17},{9,25},{17,1},{25,9},{2,18},{10... | collective-permute-start | bytes 393224 | tf_op jit(solution)/shard_map/ppermute | solution.py:15
  93.9 6.1 %collective-permute-start.17 = (f32[128,256]{1,0:T(8,128)S(1)}, f32[128,256]{1,0:T(8,128)S(1)}, u32[]{:S(2)}, u32[]{:S(2)}) collective-permute-start(f32[128,256]{1,0:T(8,128)S(1)} %slice_subtract_fusion.1.refs_0_), channel_id=1, source_target_pairs={{0,24},{8,0},{16,8},{24,16},{1,25},{9,1},{17,9},{25,17},{2,26},{10... | collective-permute-start | bytes 393224 | tf_op jit(solution)/shard_map/ppermute | solution.py:15
  101.3 1.6 collective-permute-start.18
  103.6 18.2 %all-to-all-start.2 = ((f32[8,32,256]{2,1,0:T(8,128)}), f32[8,32,256]{2,1,0:T(8,128)S(1)}, u32[]{:S(2)}, u32[]{:S(2)}) async-start(f32[8,32,256]{2,1,0:T(8,128)} %add.72), calls=%async_computation.2 | async-start | bytes 524288 | tf_op jit(solution)/shard_map/all_to_all | solution.py:271
  109.7 12.2 %collective-permute-start.19 = (f32[1,128,512]{2,1,0:T(8,128)}, f32[1,128,512]{2,1,0:T(8,128)S(1)}, u32[]{:S(2)}, u32[]{:S(2)}) collective-permute-start(f32[1,128,512]{2,1,0:T(8,128)} %get-tuple-element.122), channel_id=1, source_target_pairs={{0,16},{8,24},{16,0},{24,8},{1,17},{9,25},{17,1},{25,9},{2,18},{10... | collective-permute-start | bytes 786440 | tf_op jit(solution)/shard_map/ppermute | solution.py:15
  122.6 15.2 %all-to-all-start.3 = ((f32[8,32,256]{2,1,0:T(8,128)}), f32[8,32,256]{2,1,0:T(8,128)S(1)}, u32[]{:S(2)}, u32[]{:S(2)}) async-start(f32[8,32,256]{2,1,0:T(8,128)} %broadcast_in_dim.7), calls=%async_computation.3 | async-start | bytes 524288 | tf_op jit(solution)/shard_map/all_to_all | solution.py:274
  127.1 8.0 %collective-permute-start.20 = (f32[1,128,512]{2,1,0:T(8,128)}, f32[1,128,512]{2,1,0:T(8,128)S(1)}, u32[]{:S(2)}, u32[]{:S(2)}) collective-permute-start(f32[1,128,512]{2,1,0:T(8,128)} %get-tuple-element.130), channel_id=1, source_target_pairs={{0,8},{8,16},{16,24},{24,0},{1,9},{9,17},{17,25},{25,1},{2,10},{10... | collective-permute-start | bytes 786440 | tf_op jit(solution)/shard_map/ppermute | solution.py:15
  127.6 7.5 %collective-permute-start.21 = (f32[1,128,512]{2,1,0:T(8,128)}, f32[1,128,512]{2,1,0:T(8,128)S(1)}, u32[]{:S(2)}, u32[]{:S(2)}) collective-permute-start(f32[1,128,512]{2,1,0:T(8,128)} %get-tuple-element.131), channel_id=1, source_target_pairs={{0,24},{8,0},{16,8},{24,16},{1,25},{9,1},{17,9},{25,17},{2,26},{10... | collective-permute-start | bytes 786440 | tf_op jit(solution)/shard_map/ppermute | solution.py:15
  137.8 9.8 %collective-permute-start.22 = (f32[8,32,256]{2,1,0:T(8,128)S(1)}, f32[8,32,256]{2,1,0:T(8,128)S(1)}, u32[]{:S(2)}, u32[]{:S(2)}) collective-permute-start(f32[8,32,256]{2,1,0:T(8,128)S(1)} %all-to-all-done.3.refs_0_), channel_id=1, source_target_pairs={{0,8},{8,16},{16,24},{24,0},{1,9},{9,17},{17,25},{25,1},{2,10},{10... | collective-permute-start | bytes 786440 | tf_op jit(solution)/shard_map/ppermute | solution.py:15
  138.3 12.2 %collective-permute-start.23 = (f32[8,32,256]{2,1,0:T(8,128)S(1)}, f32[8,32,256]{2,1,0:T(8,128)S(1)}, u32[]{:S(2)}, u32[]{:S(2)}) collective-permute-start(f32[8,32,256]{2,1,0:T(8,128)S(1)} %all-to-all-done.3.refs_0_), channel_id=1, source_target_pairs={{0,16},{8,24},{16,0},{24,8},{1,17},{9,25},{17,1},{25,9},{2,18},{10... | collective-permute-start | bytes 786440 | tf_op jit(solution)/shard_map/ppermute | solution.py:15
  141.7 8.8 %collective-permute-start.24 = (f32[8,32,256]{2,1,0:T(8,128)S(1)}, f32[8,32,256]{2,1,0:T(8,128)S(1)}, u32[]{:S(2)}, u32[]{:S(2)}) collective-permute-start(f32[8,32,256]{2,1,0:T(8,128)S(1)} %all-to-all-done.3.refs_0_), channel_id=1, source_target_pairs={{0,24},{8,0},{16,8},{24,16},{1,25},{9,1},{17,9},{25,17},{2,26},{10... | collective-permute-start | bytes 786440 | tf_op jit(solution)/shard_map/ppermute | solution.py:15
  150.5 3.0 %collective-permute-start.26 = (f32[3,8,32,256]{3,2,1,0:T(8,128)S(1)}, f32[3,8,32,256]{3,2,1,0:T(8,128)S(1)}, u32[]{:S(2)}, u32[]{:S(2)}) collective-permute-start(f32[3,8,32,256]{3,2,1,0:T(8,128)S(1)} %pad_maximum_fusion.1), channel_id=1, source_target_pairs={{0,4},{4,0},{1,5},{5,1},{2,6},{6,2},{3,7},{7,3},{8,12},{12,8},{9,1... | collective-permute-start | bytes 2359304 | tf_op jit(solution)/shard_map/ppermute | solution.py:15
  150.8 2.6 %collective-permute-start.25 = (f32[8,32,256]{2,1,0:T(8,128)S(1)}, f32[8,32,256]{2,1,0:T(8,128)S(1)}, u32[]{:S(2)}, u32[]{:S(2)}) collective-permute-start(f32[8,32,256]{2,1,0:T(8,128)S(1)} %all-to-all-done.3.refs_0_), channel_id=1, source_target_pairs={{0,4},{4,0},{1,5},{5,1},{2,6},{6,2},{3,7},{7,3},{8,12},{12,8},{9,1... | collective-permute-start | bytes 786440 | tf_op jit(solution)/shard_map/ppermute | solution.py:15
  155.0 8.0 %collective-permute-start.27 = (f32[128,256]{1,0:T(8,128)S(1)}, f32[128,256]{1,0:T(8,128)S(1)}, u32[]{:S(2)}, u32[]{:S(2)}) collective-permute-start(f32[128,256]{1,0:T(8,128)S(1)} %add.73), channel_id=1, source_target_pairs={{0,2},{1,3},{2,0},{3,1},{4,6},{5,7},{6,4},{7,5},{8,10},{9,11},{10,... | collective-permute-start | bytes 393224 | tf_op jit(solution)/shard_map/ppermute | solution.py:15
  156.7 6.7 %collective-permute-start.28 = (f32[128,256]{1,0:T(8,128)S(1)}, f32[128,256]{1,0:T(8,128)S(1)}, u32[]{:S(2)}, u32[]{:S(2)}) collective-permute-start(f32[128,256]{1,0:T(8,128)S(1)} %add.73), channel_id=1, source_target_pairs={{0,1},{1,2},{2,3},{3,0},{4,5},{5,6},{6,7},{7,4},{8,9},{9,10},{10,1... | collective-permute-start | bytes 393224 | tf_op jit(solution)/shard_map/ppermute | solution.py:15
  156.9 8.0 %collective-permute-start.29 = (f32[128,256]{1,0:T(8,128)S(1)}, f32[128,256]{1,0:T(8,128)S(1)}, u32[]{:S(2)}, u32[]{:S(2)}) collective-permute-start(f32[128,256]{1,0:T(8,128)S(1)} %add.73), channel_id=1, source_target_pairs={{0,3},{1,0},{2,1},{3,2},{4,7},{5,4},{6,5},{7,6},{8,11},{9,8},{10,9... | collective-permute-start | bytes 393224 | tf_op jit(solution)/shard_map/ppermute | solution.py:15
  165.0 6.8 %collective-permute-start.30 = (f32[128,256]{1,0:T(8,128)S(1)}, f32[128,256]{1,0:T(8,128)S(1)}, u32[]{:S(2)}, u32[]{:S(2)}) collective-permute-start(f32[128,256]{1,0:T(8,128)S(1)} %slice_subtract_fusion.refs_0_), channel_id=1, source_target_pairs={{0,8},{8,16},{16,24},{24,0},{1,9},{9,17},{17,25},{25,1},{2,10},{10... | collective-permute-start | bytes 393224 | tf_op jit(solution)/shard_map/ppermute | solution.py:15
  165.5 9.8 %collective-permute-start.31 = (f32[128,256]{1,0:T(8,128)S(1)}, f32[128,256]{1,0:T(8,128)S(1)}, u32[]{:S(2)}, u32[]{:S(2)}) collective-permute-start(f32[128,256]{1,0:T(8,128)S(1)} %slice_subtract_fusion.refs_0_), channel_id=1, source_target_pairs={{0,16},{8,24},{16,0},{24,8},{1,17},{9,25},{17,1},{25,9},{2,18},{10... | collective-permute-start | bytes 393224 | tf_op jit(solution)/shard_map/ppermute | solution.py:15
  169.1 6.2 %collective-permute-start.32 = (f32[128,256]{1,0:T(8,128)S(1)}, f32[128,256]{1,0:T(8,128)S(1)}, u32[]{:S(2)}, u32[]{:S(2)}) collective-permute-start(f32[128,256]{1,0:T(8,128)S(1)} %slice_subtract_fusion.refs_0_), channel_id=1, source_target_pairs={{0,24},{8,0},{16,8},{24,16},{1,25},{9,1},{17,9},{25,17},{2,26},{10... | collective-permute-start | bytes 393224 | tf_op jit(solution)/shard_map/ppermute | solution.py:15
  177.5 1.6 collective-permute-start.33
  (13 other events, 166.7 us)
where the time goes:
time: 197 us
  waiting for transfers between devices  75.6 us (38%)
  starting transfers between devices  67.9 us (34%)
  Pallas kernels  26.6 us (14%)
  blocking collectives  16.8 us (9%)
  local copies, waits for them, and re-layouts  4.75 us (2%)
  other arithmetic  3.36 us (2%)
    ppermute x34, waiting for transfers between devices, shift(): lax.ppermute(value, axis, [(i, (i + by) % size) for i in range(size)])  54.7 us
    ppermute x34, starting transfers between devices, shift(): lax.ppermute(value, axis, [(i, (i + by) % size) for i in range(size)])  44.5 us
    all_to_all x2, waiting for transfers between devices, reduce(): return jnp.sum(lax.all_to_all(chip, 'z', 0, 0), axis=0)  17 us
    all_to_all x1, blocking collectives, reduce(): return jnp.sum(lax.all_to_all(chip, 'z', 0, 0), axis=0)  16.8 us
    all_to_all x2, starting transfers between devices, reduce(): return jnp.sum(lax.all_to_all(chip, 'z', 0, 0), axis=0)  14.5 us
    pallas_call x3, Pallas kernels, split_columns(): pl.pallas_call(functools.partial(split_kernel, len(blocks)), out_shape=[o...  10.8 us
    all_to_all x2, starting transfers between devices, gather_z(): lax.all_to_all(jnp.broadcast_to(rows[None], (Z,) + rows.shape), 'z', 0, 0)  8.86 us
    pallas_call x3, Pallas kernels, halve_block(): pl.pallas_call(halve_kernel, out_shape=(out, out), grid=(1,), in_specs=[p...  7.65 us
  transfers between devices with their start and end apart: 38, of which 25 were waited for; matrix products, arithmetic and copies ran while one was open for 1% of the time, Pallas kernels for 8%

commit v1 on v0

--- a/solution.py
+++ b/solution.py
@@ -149,76 +149,96 @@
     )(place, *residuals, *blocks)
 
 
-def halve_kernel(block_ref, high_ref, low_ref, flat):
-    flat[...] = block_ref[...]
-    step = 16
-
-    def part(i, carry):
-        where = pl.ds(pl.multiple_of(i * step, step), step)
-        high_ref[where, :], low_ref[where, :] = halves(flat[where, :])
-        return carry
-
-    lax.fori_loop(0, flat.shape[0] // step, part, 0)
-
-
-def halve_block(factor, row, column):
+def cores_kernel(n_blocks, place, *refs):
+    block_refs, (own_ref, other_ref, flat) = refs[:n_blocks], refs[n_blocks:]
+    core = place[2]
+    rows, columns = flat.shape
+    share = columns // (Z * Y * CORE)
+    group = lax.broadcasted_iota(jnp.int32, (rows, LANES), 1) // share
+    for at, block_ref in enumerate(block_refs):
+        flat[...] = block_ref[...]
+        for tile in range(columns // LANES // 2):
+            first = flat[:, 2 * tile * LANES : (2 * tile + 1) * LANES]
+            second = flat[:, (2 * tile + 1) * LANES : (2 * tile + 2) * LANES]
+
+            def turned(value, groups):
+                return pltpu.roll(value, groups % 4 * share, axis=1) if groups % 4 else value
+
+            parts = [
+                jnp.where(
+                    group < 2,
+                    jnp.where(group == 0, turned(first, -h), turned(first, -1 - h)),
+                    jnp.where(group == 2, turned(second, 2 - h), turned(second, 1 - h)),
+                )
+                for h in range(CORE)
+            ]
+            where = slice(tile * LANES, (tile + 1) * LANES)
+            own_ref[at, :, where] = jnp.where(core == 0, parts[0], parts[1])
+            other_ref[at, :, where] = jnp.where(core == 0, parts[1], parts[0])
+
+
+def split_cores(place, factor, blocks):
     rows, columns = factor.shape[2], factor.shape[5]
-    out = jax.ShapeDtypeStruct((rows, columns), jnp.bfloat16)
+    out = jax.ShapeDtypeStruct((len(blocks), rows, columns // CORE), jnp.float32)
     return pl.pallas_call(
-        halve_kernel,
+        functools.partial(cores_kernel, len(blocks)),
         out_shape=(out, out),
-        grid=(1,),
-        in_specs=[
-            pl.BlockSpec(
-                (None, None, rows, None, None, columns), lambda i: (row, 0, 0, column, 0, 0)
-            )
-        ],
-        out_specs=[pl.BlockSpec(out.shape, lambda i: (0, 0))] * 2,
-        scratch_shapes=[pltpu.VMEM(out.shape, jnp.float32)],
-        cost_estimate=pl.CostEstimate(
-            flops=4 * rows * columns, bytes_accessed=8 * rows * columns, transcendentals=0
-        ),
-        compiler_params=pltpu.CompilerParams(vmem_limit_bytes=56 << 20),
-    )(factor)
-
-
-def factor_kernel(place, block_high, block_low, *refs):
-    pieces, rest, (out_ref, high, low) = refs[: Y + 1], refs[Y + 1], refs[Y + 2 :]
-    y, core = place[1], place[2]
-    share = pieces[0].shape[1]
-
-    def put(z, carry):
-        for at, owner in enumerate((core, 1 - core)):
-            for e in range(Y):
-                row = (z * Y + lax.rem(y + Y - e, Y)) * CORE + owner
-                where = pl.ds(pl.multiple_of(row * share, share), share)
-                piece = rest[e - 1, z] if at and e else pieces[at * Y + e][z]
-                high[where, :], low[where, :] = halves(piece)
-        return carry
-
-    lax.fori_loop(0, Z, put, 0)
-    out_ref[...] = dot3(
-        (block_high[...], block_low[...]), (high[...], low[...]), ((1,), (0,))
-    )
-
-
-def apply_factor(place, block, pieces):
-    rows, columns = block[0].shape
-    new = pieces[0].shape[-1]
-    return pl.pallas_call(
-        factor_kernel,
-        out_shape=jax.ShapeDtypeStruct((rows, new), jnp.float32),
         grid_spec=pltpu.PrefetchScalarGridSpec(
             num_scalar_prefetch=1,
             grid=(1,),
-            in_specs=[pl.BlockSpec((rows, columns), lambda i, place: (0, 0))] * 2
-            + [pl.BlockSpec(pieces[0].shape, lambda i, place: (0, 0, 0))] * (Y + 1)
-            + [pl.BlockSpec(pieces[-1].shape, lambda i, place: (0, 0, 0, 0))],
-            out_specs=pl.BlockSpec((rows, new), lambda i, place: (0, 0)),
+            in_specs=[
+                pl.BlockSpec(
+                    (None, None, rows, None, None, columns),
+                    lambda i, place, at=at: (at[0], 0, 0, at[1], 0, 0),
+                )
+                for at in blocks
+            ],
+            out_specs=[pl.BlockSpec(out.shape, lambda i, place: (0, 0, 0))] * 2,
+            scratch_shapes=[pltpu.VMEM((rows, columns), jnp.float32)],
+        ),
+        cost_estimate=pl.CostEstimate(
+            flops=8 * len(blocks) * rows * columns,
+            bytes_accessed=8 * len(blocks) * rows * columns,
+            transcendentals=0,
+        ),
+        compiler_params=pltpu.CompilerParams(vmem_limit_bytes=56 << 20),
+    )(place, *[factor] * len(blocks))
+
+
+def factor_kernel(place, own_ref, other_ref, *refs):
+    pieces, (mine_ref, theirs_ref, high, low) = refs[:Y], refs[Y:]
+    y = place[1]
+    share = pieces[0].shape[1]
+
+    def put(z, carry):
+        for e in range(Y):
+            row = z * Y + lax.rem(y + Y - e, Y)
+            where = pl.ds(pl.multiple_of(row * share, share), share)
+            high[where, :], low[where, :] = halves(pieces[e][z])
+        return carry
+
+    lax.fori_loop(0, Z, put, 0)
+    for block_ref, out_ref in ((other_ref, theirs_ref), (own_ref, mine_ref)):
+        out_ref[...] = dot3(halves(block_ref[...]), (high[...], low[...]), ((1,), (0,)))
+
+
+def apply_factor(place, at, block, pieces):
+    rows, columns = block[0].shape[1:]
+    new = pieces[0].shape[-1]
+    out = jax.ShapeDtypeStruct((rows, new), jnp.float32)
+    return pl.pallas_call(
+        factor_kernel,
+        out_shape=(out, out),
+        grid_spec=pltpu.PrefetchScalarGridSpec(
+            num_scalar_prefetch=1,
+            grid=(1,),
+            in_specs=[pl.BlockSpec((None, rows, columns), lambda i, place: (at, 0, 0))] * 2
+            + [pl.BlockSpec(pieces[0].shape, lambda i, place: (0, 0, 0))] * Y,
+            out_specs=[pl.BlockSpec((rows, new), lambda i, place: (0, 0))] * 2,
             scratch_shapes=[pltpu.VMEM((columns, new), jnp.bfloat16)] * 2,
         ),
         cost_estimate=pl.CostEstimate(
-            flops=6 * rows * columns * new, bytes_accessed=3 << 20, transcendentals=0
+            flops=12 * rows * columns * new, bytes_accessed=3 << 20, transcendentals=0
         ),
         compiler_params=pltpu.CompilerParams(vmem_limit_bytes=32 << 20),
     )(place, *block, *pieces)
@@ -252,8 +272,10 @@
     w0 = in_order(w0[0], spread(w0))
     w1 = split_columns(place, [(diag_inverse, (1,))])
     w2 = split_columns(place, [(diag_inverse, (2,))])
-    l10, l20, l21 = (halve_block(factor, *at) for at in ((1, 0), (2, 0), (2, 1)))
-    w0, w1, l10, l20 = lax.optimization_barrier((w0, w1, l10, l20))
+    own_a, other_a = split_cores(place, factor, [(1, 0), (2, 0)])
+    own_b, other_b = split_cores(place, factor, [(2, 1)])
+    w0, w1, own_a, other_a = lax.optimization_barrier((w0, w1, own_a, other_a))
+    other_a = shift(other_a, "core", 1, CORE)
 
     own_points = (train_points[:, 1:, 0] / lengthscales[:, None, None]).reshape(dims, -1)
     kernel = kernel_rows(own_points, scaled_new).reshape(panels - 1, block_rows, new_count)
@@ -274,11 +296,10 @@
         return lax.all_to_all(jnp.broadcast_to(rows[None], (Z,) + rows.shape), "z", 0, 0)
 
     def gather(line):
-        mine = in_order(line, spread({e: line for e in range(1, Y)}))
-        rest = shift(jnp.stack(mine[1:]), "core", 1, CORE)
-        return mine + [shift(line, "core", 1, CORE), rest]
-
-    def residual_rows(panel, own):
+        return in_order(line, spread({e: line for e in range(1, Y)}))
+
+    def residual_rows(panel, mine, theirs):
+        own = mine + shift(theirs, "core", 1, CORE)
         arrived = [shift(own, "col", by, N_COL) for by in (2, 1, 3)]
         rest = kernel[panel - 1] - (own + arrived[0] + arrived[1] + arrived[2])
         return in_order(rest, spread({e: rest for e in range(1, Y)}))
@@ -292,15 +313,19 @@
         line, near, during_gather = lax.optimization_barrier((line, near, during_gather))
         return rows, line, in_order(later[0], {**far, **near}), during_sum, during_gather
 
-    rows_0, line, w1, w2, l21 = solve(residuals, w0, w1, w2, l21)
+    rows_0, line, w1, (w2, other_a), (own_b, other_b) = solve(
+        residuals, w0, w1, (w2, other_a), (own_b, other_b)
+    )
+    blocks = (own_a, other_a)
     pieces = gather(line)
-    residuals = residual_rows(1, apply_factor(place, l10, pieces))
-    early = apply_factor(place, l20, pieces)
-
-    residuals, w2, early = lax.optimization_barrier((residuals, w2, early))
-    rows_1, line, w2, _, _ = solve(residuals, w1, w2, (), ())
-    pieces = gather(line)
-    residuals = residual_rows(2, early + apply_factor(place, l21, pieces))
+    residuals = residual_rows(1, *apply_factor(place, 0, blocks, pieces))
+    early = apply_factor(place, 1, blocks, pieces)
+
+    residuals, w2, early, other_b = lax.optimization_barrier((residuals, w2, early, other_b))
+    other_b = shift(other_b, "core", 1, CORE)
+    rows_1, line, w2, other_b, _ = solve(residuals, w1, w2, other_b, ())
+    change = apply_factor(place, 0, (own_b, other_b), gather(line))
+    residuals = residual_rows(2, early[0] + change[0], early[1] + change[1])
 
     rows_2 = reduce(*apply_inverse(place, residuals, w2))
     return jnp.stack([rows_0, rows_1, rows_2])[:, None, None]

time: 197 us -> 200 us (1.015)
  starting transfers between devices: 67.9 us -> 63.8 us
  other arithmetic: 3.36 us -> 5.85 us
    ppermute x34, starting transfers between devices: 44.5 us -> 41 us  [shift(): lax.ppermute(value, axis, [(i, (i + by) % size) for i in range(size)])]
    unnamed x46 -> x40, local copies, waits for them, and re-layouts: 2.47 us -> 4.32 us
    pallas_call x6 -> x5, Pallas kernels: 12.1 us -> 12.5 us  [the longest x2 8.47 us: split_cores(): pl.pallas_call(functools.partial(cores_kernel, len(blocks)), out_shape=(o...]
  transfers between devices with their start and end apart: 38 -> 38, of which waited for: 25 -> 26; matrix products, arithmetic and copies ran while one was open for 1% -> 3% of each run, Pallas kernels for 8% -> 9%
where the time goes in v1:
time: 200 us; the launch traced here: 199 us
  waiting for transfers between devices  76.8 us (38%)
  starting transfers between devices  63.8 us (32%)
  Pallas kernels  26.9 us (13%)
  blocking collectives  16.7 us (8%)
  local copies, waits for them, and re-layouts  6.58 us (3%)
  other arithmetic  5.85 us (3%)
    ppermute x34, waiting for transfers between devices, shift(): lax.ppermute(value, axis, [(i, (i + by) % size) for i in range(size)])  55.5 us
    ppermute x34, starting transfers between devices, shift(): lax.ppermute(value, axis, [(i, (i + by) % size) for i in range(size)])  41 us
    all_to_all x2, waiting for transfers between devices, reduce(): return jnp.sum(lax.all_to_all(chip, 'z', 0, 0), axis=0)  17.5 us
    all_to_all x1, blocking collectives, reduce(): return jnp.sum(lax.all_to_all(chip, 'z', 0, 0), axis=0)  16.7 us
    all_to_all x2, starting transfers between devices, reduce(): return jnp.sum(lax.all_to_all(chip, 'z', 0, 0), axis=0)  14 us
    pallas_call x3, Pallas kernels, split_columns(): pl.pallas_call(functools.partial(split_kernel, len(blocks)), out_shape=[o...  10.7 us
    all_to_all x2, starting transfers between devices, gather_z(): lax.all_to_all(jnp.broadcast_to(rows[None], (Z,) + rows.shape), 'z', 0, 0)  8.78 us
    pallas_call x2, Pallas kernels, split_cores(): pl.pallas_call(functools.partial(cores_kernel, len(blocks)), out_shape=(o...  8.47 us
  transfers between devices with their start and end apart: 38, of which 26 were waited for; matrix products, arithmetic and copies ran while one was open for 3% of the time, Pallas kernels for 9%

profile of v1, /device:TPU:2, one launch (start us, length us, event | category | flops | bytes accessed | tf_op | source)
XLA Modules:
  0.0 198.9 jit_solution(4129857292813562459)
XLA Ops:
  0.6 3.6 %shard_map.55 = (f32[1,136,512]{2,1,0:T(8,128)}, f32[1,136,512]{2,1,0:T(8,128)}, f32[1,136,512]{2,1,0:T(8,128)}, f32[1,136,512]{2,1,0:T(8,128)}) custom-call(s32[3]{0:T(128)} %pad_add_fusion.place, f32[3,1,128,1,2048]{4,3,2,1,0:T(1,128)} %refs_0_.8, f32[16,3,1,128]{3,2,1,0:T(1,128)} %refs_1_.2), custom_call_target="tpu_custom_call" | custom-call | flops 262144 | bytes 2097152 | tf_op jit(solution)/shard_map/pallas_call | solution.py:89
  4.2 1.6 collective-permute-start
  5.8 2.9 %collective-permute-start.1 = (f32[1,136,512]{2,1,0:T(8,128)}, f32[1,136,512]{2,1,0:T(8,128)S(1)}, u32[]{:S(2)}, u32[]{:S(2)}) collective-permute-start(f32[1,136,512]{2,1,0:T(8,128)} %get-tuple-element.80), channel_id=1, source_target_pairs={{0,16},{8,24},{16,0},{24,8},{1,17},{9,25},{17,1},{25,9},{2,18},{10... | collective-permute-start | bytes 835592 | tf_op jit(solution)/shard_map/ppermute | solution.py:15
  8.7 1.3 collective-permute-start.2
  10.0 3.6 %shard_map.56 = (f32[1,128,512]{2,1,0:T(8,128)}, f32[1,128,512]{2,1,0:T(8,128)}, f32[1,128,512]{2,1,0:T(8,128)}, f32[1,128,512]{2,1,0:T(8,128)}) custom-call(s32[3]{0:T(128)} %pad_add_fusion.place, f32[3,1,128,1,2048]{4,3,2,1,0:T(1,128)} %refs_0_.8), custom_call_target="tpu_custom_call" | custom-call | flops 262144 | bytes 2097152 | tf_op jit(solution)/shard_map/pallas_call | solution.py:89
  14.4 4.9 %shard_map.57 = (f32[2,128,1024]{2,1,0:T(8,128)}, f32[2,128,1024]{2,1,0:T(8,128)}) custom-call(s32[3]{0:T(128)} %pad_add_fusion.place, f32[3,1,128,3,1,2048]{5,4,3,2,1,0:T(1,128)} %refs_0_.9, f32[3,1,128,3,1,2048]{5,4,3,2,1,0:T(1,128)} %refs_0_.9), custom_call_target="tpu_custom_call" | custom-call | flops 4194304 | bytes 4194304 | tf_op jit(solution)/shard_map/pallas_call | solution.py:183
  19.4 1.8 collective-permute-done.1.refs_6_
  25.9 8.5 %all-to-all-start = ((f32[8,32,256]{2,1,0:T(8,128)}), f32[8,32,256]{2,1,0:T(8,128)S(1)}, u32[]{:S(2)}, u32[]{:S(2)}) async-start(f32[8,32,256]{2,1,0:T(8,128)} %add.73), calls=%async_computation | async-start | bytes 524288 | tf_op jit(solution)/shard_map/all_to_all | solution.py:293
  34.4 2.7 %collective-permute-start.4 = (f32[1,128,512]{2,1,0:T(8,128)S(1)}, f32[1,128,512]{2,1,0:T(8,128)S(1)}, u32[]{:S(2)}, u32[]{:S(2)}) collective-permute-start(f32[1,128,512]{2,1,0:T(8,128)S(1)} %copy-done.19), channel_id=1, source_target_pairs={{0,16},{8,24},{16,0},{24,8},{1,17},{9,25},{17,1},{25,9},{2,18},{10... | collective-permute-start | bytes 786440 | tf_op jit(solution)/shard_map/ppermute | solution.py:15
  37.0 3.6 %shard_map.59 = (f32[1,128,512]{2,1,0:T(8,128)}, f32[1,128,512]{2,1,0:T(8,128)}, f32[1,128,512]{2,1,0:T(8,128)}, f32[1,128,512]{2,1,0:T(8,128)}) custom-call(s32[3]{0:T(128)} %pad_add_fusion.place, f32[3,1,128,1,2048]{4,3,2,1,0:T(1,128)} %refs_0_.8), custom_call_target="tpu_custom_call" | custom-call | flops 262144 | bytes 2097152 | tf_op jit(solution)/shard_map/pallas_call | solution.py:89
  40.6 6.2 %all-to-all-done = f32[8,32,256]{2,1,0:T(8,128)S(1)} async-done(((f32[8,32,256]{2,1,0:T(8,128)}), f32[8,32,256]{2,1,0:T(8,128)S(1)}, u32[]{:S(2)}, u32[]{:S(2)}) %all-to-all-start) | async-done | bytes 262176 | tf_op jit(solution)/shard_map/all_to_all | solution.py:293
  47.6 4.3 %all-to-all-start.1 = ((f32[8,32,256]{2,1,0:T(8,128)}), f32[8,32,256]{2,1,0:T(8,128)S(1)}, u32[]{:S(2)}, u32[]{:S(2)}) async-start(f32[8,32,256]{2,1,0:T(8,128)} %broadcast_in_dim.6), calls=%async_computation.1 | async-start | bytes 524288 | tf_op jit(solution)/shard_map/all_to_all | solution.py:296
  53.0 2.1 %collective-permute-start.7 = (f32[1,128,512]{2,1,0:T(8,128)}, f32[1,128,512]{2,1,0:T(8,128)S(1)}, u32[]{:S(2)}, u32[]{:S(2)}) collective-permute-start(f32[1,128,512]{2,1,0:T(8,128)} %get-tuple-element.107), channel_id=1, source_target_pairs={{0,24},{8,0},{16,8},{24,16},{1,25},{9,1},{17,9},{25,17},{2,26},{10... | collective-permute-start | bytes 786440 | tf_op jit(solution)/shard_map/ppermute | solution.py:15
  55.1 3.5 %shard_map.60 = (f32[1,128,1024]{2,1,0:T(8,128)}, f32[1,128,1024]{2,1,0:T(8,128)}) custom-call(s32[3]{0:T(128)} %pad_add_fusion.place, f32[3,1,128,3,1,2048]{5,4,3,2,1,0:T(1,128)} %refs_0_.9), custom_call_target="tpu_custom_call" | custom-call | flops 2097152 | bytes 2097152 | tf_op jit(solution)/shard_map/pallas_call | solution.py:183
  58.6 2.0 %collective-permute-done.6.refs_5_ = f32[1,128,512]{2,1,0:T(8,128)S(1)} collective-permute-done((f32[1,128,512]{2,1,0:T(8,128)}, f32[1,128,512]{2,1,0:T(8,128)S(1)}, u32[]{:S(2)}, u32[]{:S(2)}) %collective-permute-start.6) | collective-permute-done | bytes 262176 | tf_op jit(solution)/shard_map/ppermute | solution.py:15
  63.2 2.1 %collective-permute-start.10 = (f32[8,32,256]{2,1,0:T(8,128)S(1)}, f32[8,32,256]{2,1,0:T(8,128)S(1)}, u32[]{:S(2)}, u32[]{:S(2)}) collective-permute-start(f32[8,32,256]{2,1,0:T(8,128)S(1)} %all-to-all-done.1.refs_0_), channel_id=1, source_target_pairs={{0,24},{8,0},{16,8},{24,16},{1,25},{9,1},{17,9},{25,17},{2,26},{10... | collective-permute-start | bytes 786440 | tf_op jit(solution)/shard_map/ppermute | solution.py:15
  65.3 2.5 %collective-permute-start.9 = (f32[8,32,256]{2,1,0:T(8,128)S(1)}, f32[8,32,256]{2,1,0:T(8,128)S(1)}, u32[]{:S(2)}, u32[]{:S(2)}) collective-permute-start(f32[8,32,256]{2,1,0:T(8,128)S(1)} %all-to-all-done.1.refs_0_), channel_id=1, source_target_pairs={{0,16},{8,24},{16,0},{24,8},{1,17},{9,25},{17,1},{25,9},{2,18},{10... | collective-permute-start | bytes 786440 | tf_op jit(solution)/shard_map/ppermute | solution.py:15
  67.8 6.9 %collective-permute-done.10.refs_3_ = f32[8,32,256]{2,1,0:T(8,128)S(1)} collective-permute-done((f32[8,32,256]{2,1,0:T(8,128)S(1)}, f32[8,32,256]{2,1,0:T(8,128)S(1)}, u32[]{:S(2)}, u32[]{:S(2)}) %collective-permute-start.10) | collective-permute-done | bytes 262176 | tf_op jit(solution)/shard_map/ppermute | solution.py:15
  74.7 3.2 %collective-permute-done.8.refs_1_ = f32[8,32,256]{2,1,0:T(8,128)S(1)} collective-permute-done((f32[8,32,256]{2,1,0:T(8,128)S(1)}, f32[8,32,256]{2,1,0:T(8,128)S(1)}, u32[]{:S(2)}, u32[]{:S(2)}) %collective-permute-start.8) | collective-permute-done | bytes 262176 | tf_op jit(solution)/shard_map/ppermute | solution.py:15
  77.9 1.3 shard_map.61
  80.7 2.2 %collective-permute-start.12 = (f32[128,256]{1,0:T(8,128)S(1)}, f32[128,256]{1,0:T(8,128)S(1)}, u32[]{:S(2)}, u32[]{:S(2)}) collective-permute-start(f32[128,256]{1,0:T(8,128)S(1)} %add.78), channel_id=1, source_target_pairs={{0,2},{1,3},{2,0},{3,1},{4,6},{5,7},{6,4},{7,5},{8,10},{9,11},{10,... | collective-permute-start | bytes 393224 | tf_op jit(solution)/shard_map/ppermute | solution.py:15
  82.9 2.0 %collective-permute-start.14 = (f32[128,256]{1,0:T(8,128)S(1)}, f32[128,256]{1,0:T(8,128)S(1)}, u32[]{:S(2)}, u32[]{:S(2)}) collective-permute-start(f32[128,256]{1,0:T(8,128)S(1)} %add.78), channel_id=1, source_target_pairs={{0,3},{1,0},{2,1},{3,2},{4,7},{5,4},{6,5},{7,6},{8,11},{9,8},{10,9... | collective-permute-start | bytes 393224 | tf_op jit(solution)/shard_map/ppermute | solution.py:15
  86.2 2.5 %collective-permute-done.12 = f32[128,256]{1,0:T(8,128)S(1)} collective-permute-done((f32[128,256]{1,0:T(8,128)S(1)}, f32[128,256]{1,0:T(8,128)S(1)}, u32[]{:S(2)}, u32[]{:S(2)}) %collective-permute-start.12) | collective-permute-done | bytes 131104 | tf_op jit(solution)/shard_map/ppermute | solution.py:15
  88.7 2.1 %collective-permute-done.13 = f32[128,256]{1,0:T(8,128)S(1)} collective-permute-done((f32[128,256]{1,0:T(8,128)S(1)}, f32[128,256]{1,0:T(8,128)S(1)}, u32[]{:S(2)}, u32[]{:S(2)}) %collective-permute-start.13) | collective-permute-done | bytes 131104 | tf_op jit(solution)/shard_map/ppermute | solution.py:15
  90.9 1.9 collective-permute-start.16
  92.8 1.3 collective-permute-start.17
  94.1 1.3 shard_map.62
  95.4 4.8 %collective-permute-done.15.refs_1_ = f32[128,256]{1,0:T(8,128)S(1)} collective-permute-done((f32[128,256]{1,0:T(8,128)S(1)}, f32[128,256]{1,0:T(8,128)S(1)}, u32[]{:S(2)}, u32[]{:S(2)}) %collective-permute-start.15) | collective-permute-done | bytes 131104 | tf_op jit(solution)/shard_map/ppermute | solution.py:15
  107.3 5.5 %all-to-all-start.2 = ((f32[8,32,256]{2,1,0:T(8,128)}), f32[8,32,256]{2,1,0:T(8,128)S(1)}, u32[]{:S(2)}, u32[]{:S(2)}) async-start(f32[8,32,256]{2,1,0:T(8,128)} %add.82), calls=%async_computation.2 | async-start | bytes 524288 | tf_op jit(solution)/shard_map/all_to_all | solution.py:293
  113.7 11.3 %all-to-all-done.2 = f32[8,32,256]{2,1,0:T(8,128)S(1)} async-done(((f32[8,32,256]{2,1,0:T(8,128)}), f32[8,32,256]{2,1,0:T(8,128)S(1)}, u32[]{:S(2)}, u32[]{:S(2)}) %all-to-all-start.2) | async-done | bytes 262176 | tf_op jit(solution)/shard_map/all_to_all | solution.py:293
  125.8 4.5 %all-to-all-start.3 = ((f32[8,32,256]{2,1,0:T(8,128)}), f32[8,32,256]{2,1,0:T(8,128)S(1)}, u32[]{:S(2)}, u32[]{:S(2)}) async-start(f32[8,32,256]{2,1,0:T(8,128)} %broadcast_in_dim.7), calls=%async_computation.3 | async-start | bytes 524288 | tf_op jit(solution)/shard_map/all_to_all | solution.py:296
  130.5 3.0 %collective-permute-start.22 = (f32[1,128,512]{2,1,0:T(8,128)}, f32[1,128,512]{2,1,0:T(8,128)S(1)}, u32[]{:S(2)}, u32[]{:S(2)}) collective-permute-start(f32[1,128,512]{2,1,0:T(8,128)} %get-tuple-element.140), channel_id=1, source_target_pairs={{0,24},{8,0},{16,8},{24,16},{1,25},{9,1},{17,9},{25,17},{2,26},{10... | collective-permute-start | bytes 786440 | tf_op jit(solution)/shard_map/ppermute | solution.py:15
  133.5 4.8 %collective-permute-done.21.refs_5_ = f32[1,128,512]{2,1,0:T(8,128)S(1)} collective-permute-done((f32[1,128,512]{2,1,0:T(8,128)}, f32[1,128,512]{2,1,0:T(8,128)S(1)}, u32[]{:S(2)}, u32[]{:S(2)}) %collective-permute-start.21) | collective-permute-done | bytes 262176 | tf_op jit(solution)/shard_map/ppermute | solution.py:15
  138.3 2.7 %all-to-all-done.3.refs_0_ = f32[8,32,256]{2,1,0:T(8,128)S(1)} async-done(((f32[8,32,256]{2,1,0:T(8,128)}), f32[8,32,256]{2,1,0:T(8,128)S(1)}, u32[]{:S(2)}, u32[]{:S(2)}) %all-to-all-start.3) | async-done | bytes 262176 | tf_op jit(solution)/shard_map/all_to_all | solution.py:296
  141.2 3.6 %collective-permute-start.24 = (f32[8,32,256]{2,1,0:T(8,128)S(1)}, f32[8,32,256]{2,1,0:T(8,128)S(1)}, u32[]{:S(2)}, u32[]{:S(2)}) collective-permute-start(f32[8,32,256]{2,1,0:T(8,128)S(1)} %all-to-all-done.3.refs_0_), channel_id=1, source_target_pairs={{0,16},{8,24},{16,0},{24,8},{1,17},{9,25},{17,1},{25,9},{2,18},{10... | collective-permute-start | bytes 786440 | tf_op jit(solution)/shard_map/ppermute | solution.py:15
  144.8 5.9 %collective-permute-done.23.refs_1_ = f32[8,32,256]{2,1,0:T(8,128)S(1)} collective-permute-done((f32[8,32,256]{2,1,0:T(8,128)S(1)}, f32[8,32,256]{2,1,0:T(8,128)S(1)}, u32[]{:S(2)}, u32[]{:S(2)}) %collective-permute-start.23) | collective-permute-done | bytes 262176 | tf_op jit(solution)/shard_map/ppermute | solution.py:15
  150.7 2.8 %collective-permute-done.24.refs_2_ = f32[8,32,256]{2,1,0:T(8,128)S(1)} collective-permute-done((f32[8,32,256]{2,1,0:T(8,128)S(1)}, f32[8,32,256]{2,1,0:T(8,128)S(1)}, u32[]{:S(2)}, u32[]{:S(2)}) %collective-permute-start.24) | collective-permute-done | bytes 262176 | tf_op jit(solution)/shard_map/ppermute | solution.py:15
  153.6 1.3 shard_map.64
  155.1 1.3 collective-permute-done.26
  157.4 1.7 collective-permute-start.27
  159.2 1.9 collective-permute-start.29
  161.1 4.2 %collective-permute-done.27 = f32[128,256]{1,0:T(8,128)S(1)} collective-permute-done((f32[128,256]{1,0:T(8,128)S(1)}, f32[128,256]{1,0:T(8,128)S(1)}, u32[]{:S(2)}, u32[]{:S(2)}) %collective-permute-start.27) | collective-permute-done | bytes 131104 | tf_op jit(solution)/shard_map/ppermute | solution.py:15
  165.8 1.5 collective-permute-done.29
  168.6 3.9 %collective-permute-start.31 = (f32[128,256]{1,0:T(8,128)S(1)}, f32[128,256]{1,0:T(8,128)S(1)}, u32[]{:S(2)}, u32[]{:S(2)}) collective-permute-start(f32[128,256]{1,0:T(8,128)S(1)} %slice_subtract_fusion.refs_0_), channel_id=1, source_target_pairs={{0,16},{8,24},{16,0},{24,8},{1,17},{9,25},{17,1},{25,9},{2,18},{10... | collective-permute-start | bytes 393224 | tf_op jit(solution)/shard_map/ppermute | solution.py:15
  172.4 2.7 %collective-permute-done.30.refs_1_ = f32[128,256]{1,0:T(8,128)S(1)} collective-permute-done((f32[128,256]{1,0:T(8,128)S(1)}, f32[128,256]{1,0:T(8,128)S(1)}, u32[]{:S(2)}, u32[]{:S(2)}) %collective-permute-start.30) | collective-permute-done | bytes 131104 | tf_op jit(solution)/shard_map/ppermute | solution.py:15
  175.1 3.5 %collective-permute-done.31.refs_2_ = f32[128,256]{1,0:T(8,128)S(1)} collective-permute-done((f32[128,256]{1,0:T(8,128)S(1)}, f32[128,256]{1,0:T(8,128)S(1)}, u32[]{:S(2)}, u32[]{:S(2)}) %collective-permute-start.31) | collective-permute-done | bytes 131104 | tf_op jit(solution)/shard_map/ppermute | solution.py:15
  179.9 1.5 collective-permute-done.33
  181.5 16.7 %all_to_all.25 = f32[8,32,256]{2,1,0:T(8,128)S(1)} all-to-all(f32[8,32,256]{2,1,0:T(8,128)S(1)} %add.89), channel_id=1, replica_groups=mesh['z'=8,'y'=4,'core'=2,'col'=4] {'z'}, dimensions={0} | all-to-all | bytes 524288 | tf_op jit(solution)/shard_map/all_to_all | solution.py:293
  (104 shorter events, 27.5 us)
Async XLA Ops:
  4.2 15.2 %collective-permute-start = (f32[1,136,512]{2,1,0:T(8,128)}, f32[1,136,512]{2,1,0:T(8,128)S(1)}, u32[]{:S(2)}, u32[]{:S(2)}) collective-permute-start(f32[1,136,512]{2,1,0:T(8,128)} %get-tuple-element.79), channel_id=1, source_target_pairs={{0,8},{8,16},{16,24},{24,0},{1,9},{9,17},{17,25},{25,1},{2,10},{10... | collective-permute-start | bytes 835592 | tf_op jit(solution)/shard_map/ppermute | solution.py:15
  5.8 15.5 %collective-permute-start.1 = (f32[1,136,512]{2,1,0:T(8,128)}, f32[1,136,512]{2,1,0:T(8,128)S(1)}, u32[]{:S(2)}, u32[]{:S(2)}) collective-permute-start(f32[1,136,512]{2,1,0:T(8,128)} %get-tuple-element.80), channel_id=1, source_target_pairs={{0,16},{8,24},{16,0},{24,8},{1,17},{9,25},{17,1},{25,9},{2,18},{10... | collective-permute-start | bytes 835592 | tf_op jit(solution)/shard_map/ppermute | solution.py:15
  8.7 12.6 %collective-permute-start.2 = (f32[1,136,512]{2,1,0:T(8,128)}, f32[1,136,512]{2,1,0:T(8,128)S(1)}, u32[]{:S(2)}, u32[]{:S(2)}) collective-permute-start(f32[1,136,512]{2,1,0:T(8,128)} %get-tuple-element.81), channel_id=1, source_target_pairs={{0,24},{8,0},{16,8},{24,16},{1,25},{9,1},{17,9},{25,17},{2,26},{10... | collective-permute-start | bytes 835592 | tf_op jit(solution)/shard_map/ppermute | solution.py:15
  14.3 7.8 %copy-start.12 = (s32[3]{0:T(128)S(1)}, s32[3]{0:T(128)}, u32[]{:S(2)}) copy-start(s32[3]{0:T(128)} %pad_add_fusion.place) | copy-start | bytes 40
  14.3 20.0 %copy-start.19 = (f32[1,128,512]{2,1,0:T(8,128)S(1)}, f32[1,128,512]{2,1,0:T(8,128)}, u32[]{:S(2)}) copy-start(f32[1,128,512]{2,1,0:T(8,128)} %get-tuple-element.94) | copy-start | bytes 786436
  19.3 58.6 %copy-start = (f32[2,128,1024]{2,1,0:T(8,128)S(1)}, f32[2,128,1024]{2,1,0:T(8,128)}, u32[]{:S(2)}) copy-start(f32[2,128,1024]{2,1,0:T(8,128)} %get-tuple-element.104.own_ref) | copy-start | bytes 3145732
  19.3 58.6 %copy-start.13 = (s32[3]{0:T(128)S(1)}, s32[3]{0:T(128)}, u32[]{:S(2)}) copy-start(s32[3]{0:T(128)} %pad_add_fusion.place) | copy-start | bytes 40
  21.2 25.6 %collective-permute-start.5 = (f32[2,128,1024]{2,1,0:T(8,128)}, f32[2,128,1024]{2,1,0:T(8,128)S(1)}, u32[]{:S(2)}, u32[]{:S(2)}) collective-permute-start(f32[2,128,1024]{2,1,0:T(8,128)} %get-tuple-element.102), channel_id=1, source_target_pairs={{0,4},{4,0},{1,5},{5,1},{2,6},{6,2},{3,7},{7,3},{8,12},{12,8},{9,1... | collective-permute-start | bytes 3145736 | tf_op jit(solution)/shard_map/ppermute | solution.py:15
  23.4 1.7 collective-permute-start.3
  25.9 20.9 %all-to-all-start = ((f32[8,32,256]{2,1,0:T(8,128)}), f32[8,32,256]{2,1,0:T(8,128)S(1)}, u32[]{:S(2)}, u32[]{:S(2)}) async-start(f32[8,32,256]{2,1,0:T(8,128)} %add.73), calls=%async_computation | async-start | bytes 524288 | tf_op jit(solution)/shard_map/all_to_all | solution.py:293
  34.4 12.4 %collective-permute-start.4 = (f32[1,128,512]{2,1,0:T(8,128)S(1)}, f32[1,128,512]{2,1,0:T(8,128)S(1)}, u32[]{:S(2)}, u32[]{:S(2)}) collective-permute-start(f32[1,128,512]{2,1,0:T(8,128)S(1)} %copy-done.19), channel_id=1, source_target_pairs={{0,16},{8,24},{16,0},{24,8},{1,17},{9,25},{17,1},{25,9},{2,18},{10... | collective-permute-start | bytes 786440 | tf_op jit(solution)/shard_map/ppermute | solution.py:15
  40.6 60.2 %copy-start.4 = (f32[1,128,512]{2,1,0:T(8,128)S(1)}, f32[1,128,512]{2,1,0:T(8,128)}, u32[]{:S(2)}) copy-start(f32[1,128,512]{2,1,0:T(8,128)} %get-tuple-element.124.refs_4_) | copy-start | bytes 786436
  46.8 31.1 %copy-start.14 = (f32[32,256]{1,0:T(8,128)}, f32[32,256]{1,0:T(8,128)S(1)}, u32[]{:S(2)}) copy-start(f32[32,256]{1,0:T(8,128)S(1)} %reduce_sum.60) | copy-start | bytes 98308
  47.6 15.6 %all-to-all-start.1 = ((f32[8,32,256]{2,1,0:T(8,128)}), f32[8,32,256]{2,1,0:T(8,128)S(1)}, u32[]{:S(2)}, u32[]{:S(2)}) async-start(f32[8,32,256]{2,1,0:T(8,128)} %broadcast_in_dim.6), calls=%async_computation.1 | async-start | bytes 524288 | tf_op jit(solution)/shard_map/all_to_all | solution.py:296
  51.9 8.8 %collective-permute-start.6 = (f32[1,128,512]{2,1,0:T(8,128)}, f32[1,128,512]{2,1,0:T(8,128)S(1)}, u32[]{:S(2)}, u32[]{:S(2)}) collective-permute-start(f32[1,128,512]{2,1,0:T(8,128)} %get-tuple-element.106), channel_id=1, source_target_pairs={{0,8},{8,16},{16,24},{24,0},{1,9},{9,17},{17,25},{25,1},{2,10},{10... | collective-permute-start | bytes 786440 | tf_op jit(solution)/shard_map/ppermute | solution.py:15
  53.0 8.4 %collective-permute-start.7 = (f32[1,128,512]{2,1,0:T(8,128)}, f32[1,128,512]{2,1,0:T(8,128)S(1)}, u32[]{:S(2)}, u32[]{:S(2)}) collective-permute-start(f32[1,128,512]{2,1,0:T(8,128)} %get-tuple-element.107), channel_id=1, source_target_pairs={{0,24},{8,0},{16,8},{24,16},{1,25},{9,1},{17,9},{25,17},{2,26},{10... | collective-permute-start | bytes 786440 | tf_op jit(solution)/shard_map/ppermute | solution.py:15
  58.6 95.0 %copy-start.1 = (f32[1,128,1024]{2,1,0:T(8,128)S(1)}, f32[1,128,1024]{2,1,0:T(8,128)}, u32[]{:S(2)}) copy-start(f32[1,128,1024]{2,1,0:T(8,128)} %get-tuple-element.137.own_ref) | copy-start | bytes 1572868
  58.6 120.0 %copy-start.3 = (f32[1,128,512]{2,1,0:T(8,128)S(1)}, f32[1,128,512]{2,1,0:T(8,128)}, u32[]{:S(2)}) copy-start(f32[1,128,512]{2,1,0:T(8,128)} %get-tuple-element.145.refs_4_) | copy-start | bytes 786436
  63.2 11.5 %collective-permute-start.10 = (f32[8,32,256]{2,1,0:T(8,128)S(1)}, f32[8,32,256]{2,1,0:T(8,128)S(1)}, u32[]{:S(2)}, u32[]{:S(2)}) collective-permute-start(f32[8,32,256]{2,1,0:T(8,128)S(1)} %all-to-all-done.1.refs_0_), channel_id=1, source_target_pairs={{0,24},{8,0},{16,8},{24,16},{1,25},{9,1},{17,9},{25,17},{2,26},{10... | collective-permute-start | bytes 786440 | tf_op jit(solution)/shard_map/ppermute | solution.py:15
  65.3 12.6 %collective-permute-start.8 = (f32[8,32,256]{2,1,0:T(8,128)S(1)}, f32[8,32,256]{2,1,0:T(8,128)S(1)}, u32[]{:S(2)}, u32[]{:S(2)}) collective-permute-start(f32[8,32,256]{2,1,0:T(8,128)S(1)} %all-to-all-done.1.refs_0_), channel_id=1, source_target_pairs={{0,8},{8,16},{16,24},{24,0},{1,9},{9,17},{17,25},{25,1},{2,10},{10... | collective-permute-start | bytes 786440 | tf_op jit(solution)/shard_map/ppermute | solution.py:15
  65.3 12.6 %collective-permute-start.9 = (f32[8,32,256]{2,1,0:T(8,128)S(1)}, f32[8,32,256]{2,1,0:T(8,128)S(1)}, u32[]{:S(2)}, u32[]{:S(2)}) collective-permute-start(f32[8,32,256]{2,1,0:T(8,128)S(1)} %all-to-all-done.1.refs_0_), channel_id=1, source_target_pairs={{0,16},{8,24},{16,0},{24,8},{1,17},{9,25},{17,1},{25,9},{2,18},{10... | collective-permute-start | bytes 786440 | tf_op jit(solution)/shard_map/ppermute | solution.py:15
  79.2 1.4 collective-permute-start.11
  80.7 8.0 %collective-permute-start.12 = (f32[128,256]{1,0:T(8,128)S(1)}, f32[128,256]{1,0:T(8,128)S(1)}, u32[]{:S(2)}, u32[]{:S(2)}) collective-permute-start(f32[128,256]{1,0:T(8,128)S(1)} %add.78), channel_id=1, source_target_pairs={{0,2},{1,3},{2,0},{3,1},{4,6},{5,7},{6,4},{7,5},{8,10},{9,11},{10,... | collective-permute-start | bytes 393224 | tf_op jit(solution)/shard_map/ppermute | solution.py:15
  82.9 7.8 %collective-permute-start.13 = (f32[128,256]{1,0:T(8,128)S(1)}, f32[128,256]{1,0:T(8,128)S(1)}, u32[]{:S(2)}, u32[]{:S(2)}) collective-permute-start(f32[128,256]{1,0:T(8,128)S(1)} %add.78), channel_id=1, source_target_pairs={{0,1},{1,2},{2,3},{3,0},{4,5},{5,6},{6,7},{7,4},{8,9},{9,10},{10,1... | collective-permute-start | bytes 393224 | tf_op jit(solution)/shard_map/ppermute | solution.py:15
  82.9 7.8 %collective-permute-start.14 = (f32[128,256]{1,0:T(8,128)S(1)}, f32[128,256]{1,0:T(8,128)S(1)}, u32[]{:S(2)}, u32[]{:S(2)}) collective-permute-start(f32[128,256]{1,0:T(8,128)S(1)} %add.78), channel_id=1, source_target_pairs={{0,3},{1,0},{2,1},{3,2},{4,7},{5,4},{6,5},{7,6},{8,11},{9,8},{10,9... | collective-permute-start | bytes 393224 | tf_op jit(solution)/shard_map/ppermute | solution.py:15
  90.8 9.4 %collective-permute-start.15 = (f32[128,256]{1,0:T(8,128)S(1)}, f32[128,256]{1,0:T(8,128)S(1)}, u32[]{:S(2)}, u32[]{:S(2)}) collective-permute-start(f32[128,256]{1,0:T(8,128)S(1)} %slice_subtract_fusion.1.refs_0_), channel_id=1, source_target_pairs={{0,8},{8,16},{16,24},{24,0},{1,9},{9,17},{17,25},{25,1},{2,10},{10... | collective-permute-start | bytes 393224 | tf_op jit(solution)/shard_map/ppermute | solution.py:15
  90.9 9.3 %collective-permute-start.16 = (f32[128,256]{1,0:T(8,128)S(1)}, f32[128,256]{1,0:T(8,128)S(1)}, u32[]{:S(2)}, u32[]{:S(2)}) collective-permute-start(f32[128,256]{1,0:T(8,128)S(1)} %slice_subtract_fusion.1.refs_0_), channel_id=1, source_target_pairs={{0,16},{8,24},{16,0},{24,8},{1,17},{9,25},{17,1},{25,9},{2,18},{10... | collective-permute-start | bytes 393224 | tf_op jit(solution)/shard_map/ppermute | solution.py:15
  92.8 8.0 %collective-permute-start.17 = (f32[128,256]{1,0:T(8,128)S(1)}, f32[128,256]{1,0:T(8,128)S(1)}, u32[]{:S(2)}, u32[]{:S(2)}) collective-permute-start(f32[128,256]{1,0:T(8,128)S(1)} %slice_subtract_fusion.1.refs_0_), channel_id=1, source_target_pairs={{0,24},{8,0},{16,8},{24,16},{1,25},{9,1},{17,9},{25,17},{2,26},{10... | collective-permute-start | bytes 393224 | tf_op jit(solution)/shard_map/ppermute | solution.py:15
  95.4 9.5 %copy-start.11 = (f32[128,256]{1,0:T(8,128)}, f32[128,256]{1,0:T(8,128)S(1)}, u32[]{:S(2)}) copy-start(f32[128,256]{1,0:T(8,128)S(1)} %get-tuple-element.136) | copy-start | bytes 393220
  103.7 94.5 %copy-start.15 = (f32[32,256]{1,0:T(8,128)S(1)}, f32[32,256]{1,0:T(8,128)}, u32[]{:S(2)}) copy-start(f32[32,256]{1,0:T(8,128)} %copy-done.14) | copy-start | bytes 98308
  104.9 1.6 collective-permute-start.18
  105.0 20.0 %collective-permute-start.20 = (f32[1,128,1024]{2,1,0:T(8,128)}, f32[1,128,1024]{2,1,0:T(8,128)S(1)}, u32[]{:S(2)}, u32[]{:S(2)}) collective-permute-start(f32[1,128,1024]{2,1,0:T(8,128)} %get-tuple-element.134), channel_id=1, source_target_pairs={{0,4},{4,0},{1,5},{5,1},{2,6},{6,2},{3,7},{7,3},{8,12},{12,8},{9,1... | collective-permute-start | bytes 1572872 | tf_op jit(solution)/shard_map/ppermute | solution.py:15
  107.3 17.7 %all-to-all-start.2 = ((f32[8,32,256]{2,1,0:T(8,128)}), f32[8,32,256]{2,1,0:T(8,128)S(1)}, u32[]{:S(2)}, u32[]{:S(2)}) async-start(f32[8,32,256]{2,1,0:T(8,128)} %add.82), calls=%async_computation.2 | async-start | bytes 524288 | tf_op jit(solution)/shard_map/all_to_all | solution.py:293
  112.8 12.2 %collective-permute-start.19 = (f32[1,128,512]{2,1,0:T(8,128)}, f32[1,128,512]{2,1,0:T(8,128)S(1)}, u32[]{:S(2)}, u32[]{:S(2)}) collective-permute-start(f32[1,128,512]{2,1,0:T(8,128)} %get-tuple-element.130), channel_id=1, source_target_pairs={{0,16},{8,24},{16,0},{24,8},{1,17},{9,25},{17,1},{25,9},{2,18},{10... | collective-permute-start | bytes 786440 | tf_op jit(solution)/shard_map/ppermute | solution.py:15
  125.8 15.2 %all-to-all-start.3 = ((f32[8,32,256]{2,1,0:T(8,128)}), f32[8,32,256]{2,1,0:T(8,128)S(1)}, u32[]{:S(2)}, u32[]{:S(2)}) async-start(f32[8,32,256]{2,1,0:T(8,128)} %broadcast_in_dim.7), calls=%async_computation.3 | async-start | bytes 524288 | tf_op jit(solution)/shard_map/all_to_all | solution.py:296
  130.3 8.0 %collective-permute-start.21 = (f32[1,128,512]{2,1,0:T(8,128)}, f32[1,128,512]{2,1,0:T(8,128)S(1)}, u32[]{:S(2)}, u32[]{:S(2)}) collective-permute-start(f32[1,128,512]{2,1,0:T(8,128)} %get-tuple-element.139), channel_id=1, source_target_pairs={{0,8},{8,16},{16,24},{24,0},{1,9},{9,17},{17,25},{25,1},{2,10},{10... | collective-permute-start | bytes 786440 | tf_op jit(solution)/shard_map/ppermute | solution.py:15
  130.5 7.8 %collective-permute-start.22 = (f32[1,128,512]{2,1,0:T(8,128)}, f32[1,128,512]{2,1,0:T(8,128)S(1)}, u32[]{:S(2)}, u32[]{:S(2)}) collective-permute-start(f32[1,128,512]{2,1,0:T(8,128)} %get-tuple-element.140), channel_id=1, source_target_pairs={{0,24},{8,0},{16,8},{24,16},{1,25},{9,1},{17,9},{25,17},{2,26},{10... | collective-permute-start | bytes 786440 | tf_op jit(solution)/shard_map/ppermute | solution.py:15
  141.0 9.8 %collective-permute-start.23 = (f32[8,32,256]{2,1,0:T(8,128)S(1)}, f32[8,32,256]{2,1,0:T(8,128)S(1)}, u32[]{:S(2)}, u32[]{:S(2)}) collective-permute-start(f32[8,32,256]{2,1,0:T(8,128)S(1)} %all-to-all-done.3.refs_0_), channel_id=1, source_target_pairs={{0,8},{8,16},{16,24},{24,0},{1,9},{9,17},{17,25},{25,1},{2,10},{10... | collective-permute-start | bytes 786440 | tf_op jit(solution)/shard_map/ppermute | solution.py:15
  141.2 12.3 %collective-permute-start.24 = (f32[8,32,256]{2,1,0:T(8,128)S(1)}, f32[8,32,256]{2,1,0:T(8,128)S(1)}, u32[]{:S(2)}, u32[]{:S(2)}) collective-permute-start(f32[8,32,256]{2,1,0:T(8,128)S(1)} %all-to-all-done.3.refs_0_), channel_id=1, source_target_pairs={{0,16},{8,24},{16,0},{24,8},{1,17},{9,25},{17,1},{25,9},{2,18},{10... | collective-permute-start | bytes 786440 | tf_op jit(solution)/shard_map/ppermute | solution.py:15
  144.8 8.9 %collective-permute-start.25 = (f32[8,32,256]{2,1,0:T(8,128)S(1)}, f32[8,32,256]{2,1,0:T(8,128)S(1)}, u32[]{:S(2)}, u32[]{:S(2)}) collective-permute-start(f32[8,32,256]{2,1,0:T(8,128)S(1)} %all-to-all-done.3.refs_0_), channel_id=1, source_target_pairs={{0,24},{8,0},{16,8},{24,16},{1,25},{9,1},{17,9},{25,17},{2,26},{10... | collective-permute-start | bytes 786440 | tf_op jit(solution)/shard_map/ppermute | solution.py:15
  155.0 1.4 collective-permute-start.26
  157.4 8.0 %collective-permute-start.27 = (f32[128,256]{1,0:T(8,128)S(1)}, f32[128,256]{1,0:T(8,128)S(1)}, u32[]{:S(2)}, u32[]{:S(2)}) collective-permute-start(f32[128,256]{1,0:T(8,128)S(1)} %add_add_fusion), channel_id=1, source_target_pairs={{0,2},{1,3},{2,0},{3,1},{4,6},{5,7},{6,4},{7,5},{8,10},{9,11},{10,... | collective-permute-start | bytes 393224 | tf_op jit(solution)/shard_map/ppermute | solution.py:15
  159.1 6.8 %collective-permute-start.28 = (f32[128,256]{1,0:T(8,128)S(1)}, f32[128,256]{1,0:T(8,128)S(1)}, u32[]{:S(2)}, u32[]{:S(2)}) collective-permute-start(f32[128,256]{1,0:T(8,128)S(1)} %add_add_fusion), channel_id=1, source_target_pairs={{0,1},{1,2},{2,3},{3,0},{4,5},{5,6},{6,7},{7,4},{8,9},{9,10},{10,1... | collective-permute-start | bytes 393224 | tf_op jit(solution)/shard_map/ppermute | solution.py:15
  159.2 8.1 %collective-permute-start.29 = (f32[128,256]{1,0:T(8,128)S(1)}, f32[128,256]{1,0:T(8,128)S(1)}, u32[]{:S(2)}, u32[]{:S(2)}) collective-permute-start(f32[128,256]{1,0:T(8,128)S(1)} %add_add_fusion), channel_id=1, source_target_pairs={{0,3},{1,0},{2,1},{3,2},{4,7},{5,4},{6,5},{7,6},{8,11},{9,8},{10,9... | collective-permute-start | bytes 393224 | tf_op jit(solution)/shard_map/ppermute | solution.py:15
  168.3 6.8 %collective-permute-start.30 = (f32[128,256]{1,0:T(8,128)S(1)}, f32[128,256]{1,0:T(8,128)S(1)}, u32[]{:S(2)}, u32[]{:S(2)}) collective-permute-start(f32[128,256]{1,0:T(8,128)S(1)} %slice_subtract_fusion.refs_0_), channel_id=1, source_target_pairs={{0,8},{8,16},{16,24},{24,0},{1,9},{9,17},{17,25},{25,1},{2,10},{10... | collective-permute-start | bytes 393224 | tf_op jit(solution)/shard_map/ppermute | solution.py:15
  168.6 10.1 %collective-permute-start.31 = (f32[128,256]{1,0:T(8,128)S(1)}, f32[128,256]{1,0:T(8,128)S(1)}, u32[]{:S(2)}, u32[]{:S(2)}) collective-permute-start(f32[128,256]{1,0:T(8,128)S(1)} %slice_subtract_fusion.refs_0_), channel_id=1, source_target_pairs={{0,16},{8,24},{16,0},{24,8},{1,17},{9,25},{17,1},{25,9},{2,18},{10... | collective-permute-start | bytes 393224 | tf_op jit(solution)/shard_map/ppermute | solution.py:15
  172.4 6.2 %collective-permute-start.32 = (f32[128,256]{1,0:T(8,128)S(1)}, f32[128,256]{1,0:T(8,128)S(1)}, u32[]{:S(2)}, u32[]{:S(2)}) collective-permute-start(f32[128,256]{1,0:T(8,128)S(1)} %slice_subtract_fusion.refs_0_), channel_id=1, source_target_pairs={{0,24},{8,0},{16,8},{24,16},{1,25},{9,1},{17,9},{25,17},{2,26},{10... | collective-permute-start | bytes 393224 | tf_op jit(solution)/shard_map/ppermute | solution.py:15
  179.8 1.6 collective-permute-start.33
  (10 other events, 28.5 us)

commit v2 on v1

--- a/solution.py
+++ b/solution.py
@@ -145,7 +145,7 @@
         cost_estimate=pl.CostEstimate(
             flops=6 * Y * rows * columns * new, bytes_accessed=4 << 20, transcendentals=0
         ),
-        compiler_params=pltpu.CompilerParams(vmem_limit_bytes=32 << 20),
+        compiler_params=pltpu.CompilerParams(vmem_limit_bytes=60 << 20),
     )(place, *residuals, *blocks)
 
 

time: 200 us -> 208 us (1.040)
  Pallas kernels: 26.9 us -> 33.6 us
  waiting for transfers between devices: 76.8 us -> 79.9 us
    pallas_call x3, Pallas kernels: 3.66 us -> 10.5 us  [apply_inverse(): pl.pallas_call(inverse_kernel, out_shape=(out, out), grid_spec=pltpu.Pref...]
    add x3, other arithmetic: 1.53 us -> 4.36 us  [reduce(): chip = keep + shift(send, 'core', 1, CORE)]
    unnamed x40 -> x46, local copies, waits for them, and re-layouts: 4.32 us -> 1.96 us
  transfers between devices with their start and end apart: 38 -> 38, of which waited for: 26 -> 26; matrix products, arithmetic and copies ran while one was open for 3% -> 4% of each run, Pallas kernels for 9% -> 10%
where the time goes in v2:
time: 208 us; the launch traced here: 207 us
  waiting for transfers between devices  79.9 us (38%)
  starting transfers between devices  63.3 us (30%)
  Pallas kernels  33.6 us (16%)
  blocking collectives  16.7 us (8%)
  other arithmetic  6.13 us (3%)
  local copies, waits for them, and re-layouts  5.84 us (3%)
    ppermute x34, waiting for transfers between devices, shift(): lax.ppermute(value, axis, [(i, (i + by) % size) for i in range(size)])  57 us
    ppermute x34, starting transfers between devices, shift(): lax.ppermute(value, axis, [(i, (i + by) % size) for i in range(size)])  40.6 us
    all_to_all x2, waiting for transfers between devices, reduce(): return jnp.sum(lax.all_to_all(chip, 'z', 0, 0), axis=0)  17.7 us
    all_to_all x1, blocking collectives, reduce(): return jnp.sum(lax.all_to_all(chip, 'z', 0, 0), axis=0)  16.7 us
    all_to_all x2, starting transfers between devices, reduce(): return jnp.sum(lax.all_to_all(chip, 'z', 0, 0), axis=0)  13.7 us
    pallas_call x3, Pallas kernels, split_columns(): pl.pallas_call(functools.partial(split_kernel, len(blocks)), out_shape=[o...  10.7 us
    pallas_call x3, Pallas kernels, apply_inverse(): pl.pallas_call(inverse_kernel, out_shape=(out, out), grid_spec=pltpu.Pref...  10.5 us
    all_to_all x2, starting transfers between devices, gather_z(): lax.all_to_all(jnp.broadcast_to(rows[None], (Z,) + rows.shape), 'z', 0, 0)  8.93 us
  transfers between devices with their start and end apart: 38, of which 26 were waited for; matrix products, arithmetic and copies ran while one was open for 4% of the time, Pallas kernels for 10%

profile of v2, /device:TPU:2, one launch (start us, length us, event | category | flops | bytes accessed | tf_op | source)
XLA Modules:
  0.0 207.0 jit_solution(8389009908633058836)
XLA Ops:
  0.6 3.6 %shard_map.55 = (f32[1,136,512]{2,1,0:T(8,128)}, f32[1,136,512]{2,1,0:T(8,128)}, f32[1,136,512]{2,1,0:T(8,128)}, f32[1,136,512]{2,1,0:T(8,128)}) custom-call(s32[3]{0:T(128)} %pad_add_fusion.place, f32[3,1,128,1,2048]{4,3,2,1,0:T(1,128)} %refs_0_.8, f32[16,3,1,128]{3,2,1,0:T(1,128)} %refs_1_.2), custom_call_target="tpu_custom_call" | custom-call | flops 262144 | bytes 2097152 | tf_op jit(solution)/shard_map/pallas_call | solution.py:89
  4.2 1.6 collective-permute-start
  5.8 2.9 %collective-permute-start.1 = (f32[1,136,512]{2,1,0:T(8,128)}, f32[1,136,512]{2,1,0:T(8,128)S(1)}, u32[]{:S(2)}, u32[]{:S(2)}) collective-permute-start(f32[1,136,512]{2,1,0:T(8,128)} %get-tuple-element.80), channel_id=1, source_target_pairs={{0,16},{8,24},{16,0},{24,8},{1,17},{9,25},{17,1},{25,9},{2,18},{10... | collective-permute-start | bytes 835592 | tf_op jit(solution)/shard_map/ppermute | solution.py:15
  10.0 3.6 %shard_map.56 = (f32[1,128,512]{2,1,0:T(8,128)}, f32[1,128,512]{2,1,0:T(8,128)}, f32[1,128,512]{2,1,0:T(8,128)}, f32[1,128,512]{2,1,0:T(8,128)}) custom-call(s32[3]{0:T(128)} %pad_add_fusion.place, f32[3,1,128,1,2048]{4,3,2,1,0:T(1,128)} %refs_0_.8), custom_call_target="tpu_custom_call" | custom-call | flops 262144 | bytes 2097152 | tf_op jit(solution)/shard_map/pallas_call | solution.py:89
  14.3 4.9 %shard_map.57 = (f32[2,128,1024]{2,1,0:T(8,128)}, f32[2,128,1024]{2,1,0:T(8,128)}) custom-call(s32[3]{0:T(128)} %pad_add_fusion.place, f32[3,1,128,3,1,2048]{5,4,3,2,1,0:T(1,128)} %refs_0_.9, f32[3,1,128,3,1,2048]{5,4,3,2,1,0:T(1,128)} %refs_0_.9), custom_call_target="tpu_custom_call" | custom-call | flops 4194304 | bytes 4194304 | tf_op jit(solution)/shard_map/pallas_call | solution.py:183
  19.4 1.8 collective-permute-done.1.refs_6_
  23.7 3.5 %shard_map.58 = (f32[8,32,256]{2,1,0:T(8,128)}, f32[8,32,256]{2,1,0:T(8,128)}) custom-call(s32[3]{0:T(128)} %pad_add_fusion.place, f32[128,256]{1,0:T(8,128)} %get-tuple-element.156.refs_0_, f32[128,256]{1,0:T(8,128)} %get-tuple-element.155.refs_1_, f32[128,256]{1,0:T(8,128)} %get-tuple-element.154.refs_2_, f32[128,256]{1,0:T(8,128)} %get-tuple-element.153.refs_3_, ...), custom_call_target="tpu_custom_call" | custom-call | flops 402653184 | bytes 4194304 | tf_op jit(solution)/shard_map/pallas_call | solution.py:133
  29.1 1.7 add.73
  30.8 8.5 %all-to-all-start = ((f32[8,32,256]{2,1,0:T(8,128)}), f32[8,32,256]{2,1,0:T(8,128)S(1)}, u32[]{:S(2)}, u32[]{:S(2)}) async-start(f32[8,32,256]{2,1,0:T(8,128)} %add.73), calls=%async_computation | async-start | bytes 524288 | tf_op jit(solution)/shard_map/all_to_all | solution.py:293
  39.3 2.5 %collective-permute-start.4 = (f32[1,128,512]{2,1,0:T(8,128)}, f32[1,128,512]{2,1,0:T(8,128)S(1)}, u32[]{:S(2)}, u32[]{:S(2)}) collective-permute-start(f32[1,128,512]{2,1,0:T(8,128)} %get-tuple-element.94), channel_id=1, source_target_pairs={{0,16},{8,24},{16,0},{24,8},{1,17},{9,25},{17,1},{25,9},{2,18},{10... | collective-permute-start | bytes 786440 | tf_op jit(solution)/shard_map/ppermute | solution.py:15
  41.7 3.6 %shard_map.59 = (f32[1,128,512]{2,1,0:T(8,128)}, f32[1,128,512]{2,1,0:T(8,128)}, f32[1,128,512]{2,1,0:T(8,128)}, f32[1,128,512]{2,1,0:T(8,128)}) custom-call(s32[3]{0:T(128)} %pad_add_fusion.place, f32[3,1,128,1,2048]{4,3,2,1,0:T(1,128)} %refs_0_.8), custom_call_target="tpu_custom_call" | custom-call | flops 262144 | bytes 2097152 | tf_op jit(solution)/shard_map/pallas_call | solution.py:89
  45.3 6.4 %all-to-all-done = f32[8,32,256]{2,1,0:T(8,128)S(1)} async-done(((f32[8,32,256]{2,1,0:T(8,128)}), f32[8,32,256]{2,1,0:T(8,128)S(1)}, u32[]{:S(2)}, u32[]{:S(2)}) %all-to-all-start) | async-done | bytes 262176 | tf_op jit(solution)/shard_map/all_to_all | solution.py:293
  52.5 4.5 %all-to-all-start.1 = ((f32[8,32,256]{2,1,0:T(8,128)}), f32[8,32,256]{2,1,0:T(8,128)S(1)}, u32[]{:S(2)}, u32[]{:S(2)}) async-start(f32[8,32,256]{2,1,0:T(8,128)} %broadcast_in_dim.6), calls=%async_computation.1 | async-start | bytes 524288 | tf_op jit(solution)/shard_map/all_to_all | solution.py:296
  58.1 2.2 %collective-permute-start.7 = (f32[1,128,512]{2,1,0:T(8,128)}, f32[1,128,512]{2,1,0:T(8,128)}, u32[]{:S(2)}, u32[]{:S(2)}) collective-permute-start(f32[1,128,512]{2,1,0:T(8,128)} %get-tuple-element.107), channel_id=1, source_target_pairs={{0,24},{8,0},{16,8},{24,16},{1,25},{9,1},{17,9},{25,17},{2,26},{10... | collective-permute-start | bytes 786440 | tf_op jit(solution)/shard_map/ppermute | solution.py:15
  60.3 3.5 %shard_map.60 = (f32[1,128,1024]{2,1,0:T(8,128)}, f32[1,128,1024]{2,1,0:T(8,128)}) custom-call(s32[3]{0:T(128)} %pad_add_fusion.place, f32[3,1,128,3,1,2048]{5,4,3,2,1,0:T(1,128)} %refs_0_.9), custom_call_target="tpu_custom_call" | custom-call | flops 2097152 | bytes 2097152 | tf_op jit(solution)/shard_map/pallas_call | solution.py:183
  63.8 1.8 collective-permute-done.6.refs_5_
  65.6 2.5 %all-to-all-done.1.refs_0_ = f32[8,32,256]{2,1,0:T(8,128)S(1)} async-done(((f32[8,32,256]{2,1,0:T(8,128)}), f32[8,32,256]{2,1,0:T(8,128)S(1)}, u32[]{:S(2)}, u32[]{:S(2)}) %all-to-all-start.1) | async-done | bytes 262176 | tf_op jit(solution)/shard_map/all_to_all | solution.py:296
  68.1 2.0 collective-permute-start.10
  70.2 2.5 %collective-permute-start.9 = (f32[8,32,256]{2,1,0:T(8,128)S(1)}, f32[8,32,256]{2,1,0:T(8,128)S(1)}, u32[]{:S(2)}, u32[]{:S(2)}) collective-permute-start(f32[8,32,256]{2,1,0:T(8,128)S(1)} %all-to-all-done.1.refs_0_), channel_id=1, source_target_pairs={{0,16},{8,24},{16,0},{24,8},{1,17},{9,25},{17,1},{25,9},{2,18},{10... | collective-permute-start | bytes 786440 | tf_op jit(solution)/shard_map/ppermute | solution.py:15
  72.6 4.6 %collective-permute-done.10.refs_3_ = f32[8,32,256]{2,1,0:T(8,128)S(1)} collective-permute-done((f32[8,32,256]{2,1,0:T(8,128)S(1)}, f32[8,32,256]{2,1,0:T(8,128)S(1)}, u32[]{:S(2)}, u32[]{:S(2)}) %collective-permute-start.10) | collective-permute-done | bytes 262176 | tf_op jit(solution)/shard_map/ppermute | solution.py:15
  77.3 5.0 %collective-permute-done.8.refs_1_ = f32[8,32,256]{2,1,0:T(8,128)S(1)} collective-permute-done((f32[8,32,256]{2,1,0:T(8,128)S(1)}, f32[8,32,256]{2,1,0:T(8,128)S(1)}, u32[]{:S(2)}, u32[]{:S(2)}) %collective-permute-start.8) | collective-permute-done | bytes 262176 | tf_op jit(solution)/shard_map/ppermute | solution.py:15
  85.1 2.2 %collective-permute-start.12 = (f32[128,256]{1,0:T(8,128)S(1)}, f32[128,256]{1,0:T(8,128)S(1)}, u32[]{:S(2)}, u32[]{:S(2)}) collective-permute-start(f32[128,256]{1,0:T(8,128)S(1)} %add.78), channel_id=1, source_target_pairs={{0,2},{1,3},{2,0},{3,1},{4,6},{5,7},{6,4},{7,5},{8,10},{9,11},{10,... | collective-permute-start | bytes 393224 | tf_op jit(solution)/shard_map/ppermute | solution.py:15
  87.3 2.0 collective-permute-start.14
  89.9 3.2 %collective-permute-done.12 = f32[128,256]{1,0:T(8,128)S(1)} collective-permute-done((f32[128,256]{1,0:T(8,128)S(1)}, f32[128,256]{1,0:T(8,128)S(1)}, u32[]{:S(2)}, u32[]{:S(2)}) %collective-permute-start.12) | collective-permute-done | bytes 131104 | tf_op jit(solution)/shard_map/ppermute | solution.py:15
  93.1 2.1 collective-permute-done.13
  95.3 2.2 %collective-permute-start.16 = (f32[128,256]{1,0:T(8,128)S(1)}, f32[128,256]{1,0:T(8,128)S(1)}, u32[]{:S(2)}, u32[]{:S(2)}) collective-permute-start(f32[128,256]{1,0:T(8,128)S(1)} %slice_subtract_fusion.1.refs_0_), channel_id=1, source_target_pairs={{0,16},{8,24},{16,0},{24,8},{1,17},{9,25},{17,1},{25,9},{2,18},{10... | collective-permute-start | bytes 393224 | tf_op jit(solution)/shard_map/ppermute | solution.py:15
  99.8 4.8 %collective-permute-done.15.refs_1_ = f32[128,256]{1,0:T(8,128)S(1)} collective-permute-done((f32[128,256]{1,0:T(8,128)S(1)}, f32[128,256]{1,0:T(8,128)S(1)}, u32[]{:S(2)}, u32[]{:S(2)}) %collective-permute-start.15) | collective-permute-done | bytes 131104 | tf_op jit(solution)/shard_map/ppermute | solution.py:15
  105.9 3.5 %shard_map.63 = (f32[8,32,256]{2,1,0:T(8,128)}, f32[8,32,256]{2,1,0:T(8,128)}) custom-call(s32[3]{0:T(128)} %pad_add_fusion.place, f32[128,256]{1,0:T(8,128)} %copy-done.4, f32[128,256]{1,0:T(8,128)} %copy-done.14, f32[128,256]{1,0:T(8,128)} %copy-done.15, f32[128,256]{1,0:T(8,128)} %copy-done.16, f32[1,128,512]{2,1,0:T(8,128)} %get-tuple-element.124.refs_4_, ...), custom_call_target="tpu_custom_call" | custom-call | flops 402653184 | bytes 4194304 | tf_op jit(solution)/shard_map/pallas_call | solution.py:133
  111.2 1.7 add.82
  112.8 5.2 %all-to-all-start.2 = ((f32[8,32,256]{2,1,0:T(8,128)}), f32[8,32,256]{2,1,0:T(8,128)S(1)}, u32[]{:S(2)}, u32[]{:S(2)}) async-start(f32[8,32,256]{2,1,0:T(8,128)} %add.82), calls=%async_computation.2 | async-start | bytes 524288 | tf_op jit(solution)/shard_map/all_to_all | solution.py:293
  118.9 11.3 %all-to-all-done.2 = f32[8,32,256]{2,1,0:T(8,128)S(1)} async-done(((f32[8,32,256]{2,1,0:T(8,128)}), f32[8,32,256]{2,1,0:T(8,128)S(1)}, u32[]{:S(2)}, u32[]{:S(2)}) %all-to-all-start.2) | async-done | bytes 262176 | tf_op jit(solution)/shard_map/all_to_all | solution.py:293
  131.1 4.5 %all-to-all-start.3 = ((f32[8,32,256]{2,1,0:T(8,128)}), f32[8,32,256]{2,1,0:T(8,128)S(1)}, u32[]{:S(2)}, u32[]{:S(2)}) async-start(f32[8,32,256]{2,1,0:T(8,128)} %broadcast_in_dim.7), calls=%async_computation.3 | async-start | bytes 524288 | tf_op jit(solution)/shard_map/all_to_all | solution.py:296
  135.8 3.0 %collective-permute-start.22 = (f32[1,128,512]{2,1,0:T(8,128)}, f32[1,128,512]{2,1,0:T(8,128)S(1)}, u32[]{:S(2)}, u32[]{:S(2)}) collective-permute-start(f32[1,128,512]{2,1,0:T(8,128)} %get-tuple-element.140), channel_id=1, source_target_pairs={{0,24},{8,0},{16,8},{24,16},{1,25},{9,1},{17,9},{25,17},{2,26},{10... | collective-permute-start | bytes 786440 | tf_op jit(solution)/shard_map/ppermute | solution.py:15
  138.8 4.8 %collective-permute-done.21.refs_5_ = f32[1,128,512]{2,1,0:T(8,128)S(1)} collective-permute-done((f32[1,128,512]{2,1,0:T(8,128)}, f32[1,128,512]{2,1,0:T(8,128)S(1)}, u32[]{:S(2)}, u32[]{:S(2)}) %collective-permute-start.21) | collective-permute-done | bytes 262176 | tf_op jit(solution)/shard_map/ppermute | solution.py:15
  143.6 2.7 %all-to-all-done.3.refs_0_ = f32[8,32,256]{2,1,0:T(8,128)S(1)} async-done(((f32[8,32,256]{2,1,0:T(8,128)}), f32[8,32,256]{2,1,0:T(8,128)S(1)}, u32[]{:S(2)}, u32[]{:S(2)}) %all-to-all-start.3) | async-done | bytes 262176 | tf_op jit(solution)/shard_map/all_to_all | solution.py:296
  146.5 3.6 %collective-permute-start.24 = (f32[8,32,256]{2,1,0:T(8,128)S(1)}, f32[8,32,256]{2,1,0:T(8,128)S(1)}, u32[]{:S(2)}, u32[]{:S(2)}) collective-permute-start(f32[8,32,256]{2,1,0:T(8,128)S(1)} %all-to-all-done.3.refs_0_), channel_id=1, source_target_pairs={{0,16},{8,24},{16,0},{24,8},{1,17},{9,25},{17,1},{25,9},{2,18},{10... | collective-permute-start | bytes 786440 | tf_op jit(solution)/shard_map/ppermute | solution.py:15
  150.1 5.9 %collective-permute-done.23.refs_1_ = f32[8,32,256]{2,1,0:T(8,128)S(1)} collective-permute-done((f32[8,32,256]{2,1,0:T(8,128)S(1)}, f32[8,32,256]{2,1,0:T(8,128)S(1)}, u32[]{:S(2)}, u32[]{:S(2)}) %collective-permute-start.23) | collective-permute-done | bytes 262176 | tf_op jit(solution)/shard_map/ppermute | solution.py:15
  156.0 2.8 %collective-permute-done.24.refs_2_ = f32[8,32,256]{2,1,0:T(8,128)S(1)} collective-permute-done((f32[8,32,256]{2,1,0:T(8,128)S(1)}, f32[8,32,256]{2,1,0:T(8,128)S(1)}, u32[]{:S(2)}, u32[]{:S(2)}) %collective-permute-start.24) | collective-permute-done | bytes 262176 | tf_op jit(solution)/shard_map/ppermute | solution.py:15
  161.7 1.7 collective-permute-start.27
  163.6 1.9 collective-permute-start.29
  165.4 4.3 %collective-permute-done.27 = f32[128,256]{1,0:T(8,128)S(1)} collective-permute-done((f32[128,256]{1,0:T(8,128)S(1)}, f32[128,256]{1,0:T(8,128)S(1)}, u32[]{:S(2)}, u32[]{:S(2)}) %collective-permute-start.27) | collective-permute-done | bytes 131104 | tf_op jit(solution)/shard_map/ppermute | solution.py:15
  170.2 1.5 collective-permute-done.29
  172.0 3.8 %collective-permute-start.31 = (f32[128,256]{1,0:T(8,128)S(1)}, f32[128,256]{1,0:T(8,128)S(1)}, u32[]{:S(2)}, u32[]{:S(2)}) collective-permute-start(f32[128,256]{1,0:T(8,128)S(1)} %slice_subtract_fusion.refs_0_), channel_id=1, source_target_pairs={{0,16},{8,24},{16,0},{24,8},{1,17},{9,25},{17,1},{25,9},{2,18},{10... | collective-permute-start | bytes 393224 | tf_op jit(solution)/shard_map/ppermute | solution.py:15
  175.9 2.7 %collective-permute-done.30.refs_1_ = f32[128,256]{1,0:T(8,128)S(1)} collective-permute-done((f32[128,256]{1,0:T(8,128)S(1)}, f32[128,256]{1,0:T(8,128)S(1)}, u32[]{:S(2)}, u32[]{:S(2)}) %collective-permute-start.30) | collective-permute-done | bytes 131104 | tf_op jit(solution)/shard_map/ppermute | solution.py:15
  178.6 3.5 %collective-permute-done.31.refs_2_ = f32[128,256]{1,0:T(8,128)S(1)} collective-permute-done((f32[128,256]{1,0:T(8,128)S(1)}, f32[128,256]{1,0:T(8,128)S(1)}, u32[]{:S(2)}, u32[]{:S(2)}) %collective-permute-start.31) | collective-permute-done | bytes 131104 | tf_op jit(solution)/shard_map/ppermute | solution.py:15
  183.3 3.5 %shard_map.65 = (f32[8,32,256]{2,1,0:T(8,128)}, f32[8,32,256]{2,1,0:T(8,128)}) custom-call(s32[3]{0:T(128)} %pad_add_fusion.place, f32[128,256]{1,0:T(8,128)} %copy-done.5, f32[128,256]{1,0:T(8,128)} %copy-done.17, f32[128,256]{1,0:T(8,128)} %copy-done.18, f32[128,256]{1,0:T(8,128)} %copy-done.19, f32[1,128,512]{2,1,0:T(8,128)} %get-tuple-element.145.refs_4_, ...), custom_call_target="tpu_custom_call" | custom-call | flops 402653184 | bytes 4194304 | tf_op jit(solution)/shard_map/pallas_call | solution.py:133
  186.9 1.7 collective-permute-done.33
  189.6 16.7 %all_to_all.25 = f32[8,32,256]{2,1,0:T(8,128)S(1)} all-to-all(f32[8,32,256]{2,1,0:T(8,128)S(1)} %add.89), channel_id=1, replica_groups=mesh['z'=8,'y'=4,'core'=2,'col'=4] {'z'}, dimensions={0} | all-to-all | bytes 524288 | tf_op jit(solution)/shard_map/all_to_all | solution.py:293
  (110 shorter events, 26.9 us)
Async XLA Ops:
  4.2 15.2 %collective-permute-start = (f32[1,136,512]{2,1,0:T(8,128)}, f32[1,136,512]{2,1,0:T(8,128)S(1)}, u32[]{:S(2)}, u32[]{:S(2)}) collective-permute-start(f32[1,136,512]{2,1,0:T(8,128)} %get-tuple-element.79), channel_id=1, source_target_pairs={{0,8},{8,16},{16,24},{24,0},{1,9},{9,17},{17,25},{25,1},{2,10},{10... | collective-permute-start | bytes 835592 | tf_op jit(solution)/shard_map/ppermute | solution.py:15
  5.8 15.5 %collective-permute-start.1 = (f32[1,136,512]{2,1,0:T(8,128)}, f32[1,136,512]{2,1,0:T(8,128)S(1)}, u32[]{:S(2)}, u32[]{:S(2)}) collective-permute-start(f32[1,136,512]{2,1,0:T(8,128)} %get-tuple-element.80), channel_id=1, source_target_pairs={{0,16},{8,24},{16,0},{24,8},{1,17},{9,25},{17,1},{25,9},{2,18},{10... | collective-permute-start | bytes 835592 | tf_op jit(solution)/shard_map/ppermute | solution.py:15
  8.7 12.6 %collective-permute-start.2 = (f32[1,136,512]{2,1,0:T(8,128)}, f32[1,136,512]{2,1,0:T(8,128)S(1)}, u32[]{:S(2)}, u32[]{:S(2)}) collective-permute-start(f32[1,136,512]{2,1,0:T(8,128)} %get-tuple-element.81), channel_id=1, source_target_pairs={{0,24},{8,0},{16,8},{24,16},{1,25},{9,1},{17,9},{25,17},{2,26},{10... | collective-permute-start | bytes 835592 | tf_op jit(solution)/shard_map/ppermute | solution.py:15
  19.3 63.1 %copy-start = (f32[2,128,1024]{2,1,0:T(8,128)S(1)}, f32[2,128,1024]{2,1,0:T(8,128)}, u32[]{:S(2)}) copy-start(f32[2,128,1024]{2,1,0:T(8,128)} %get-tuple-element.104.own_ref) | copy-start | bytes 3145732
  19.3 63.1 %copy-start.2 = (s32[3]{0:T(128)S(1)}, s32[3]{0:T(128)}, u32[]{:S(2)}) copy-start(s32[3]{0:T(128)} %pad_add_fusion.place) | copy-start | bytes 40
  21.2 30.5 %collective-permute-start.5 = (f32[2,128,1024]{2,1,0:T(8,128)}, f32[2,128,1024]{2,1,0:T(8,128)S(1)}, u32[]{:S(2)}, u32[]{:S(2)}) collective-permute-start(f32[2,128,1024]{2,1,0:T(8,128)} %get-tuple-element.102), channel_id=1, source_target_pairs={{0,4},{4,0},{1,5},{5,1},{2,6},{6,2},{3,7},{7,3},{8,12},{12,8},{9,1... | collective-permute-start | bytes 3145736 | tf_op jit(solution)/shard_map/ppermute | solution.py:15
  27.2 56.5 %copy-start.20 = (f32[16,3,1,128]{3,2,1,0:T(1,128)S(1)}, f32[16,3,1,128]{3,2,1,0:T(1,128)}, u32[]{:S(2)}) copy-start(f32[16,3,1,128]{3,2,1,0:T(1,128)} %refs_1_.2) | copy-start | bytes 73732
  27.2 1.8 collective-permute-start.3
  30.8 20.9 %all-to-all-start = ((f32[8,32,256]{2,1,0:T(8,128)}), f32[8,32,256]{2,1,0:T(8,128)S(1)}, u32[]{:S(2)}, u32[]{:S(2)}) async-start(f32[8,32,256]{2,1,0:T(8,128)} %add.73), calls=%async_computation | async-start | bytes 524288 | tf_op jit(solution)/shard_map/all_to_all | solution.py:293
  39.3 12.4 %collective-permute-start.4 = (f32[1,128,512]{2,1,0:T(8,128)}, f32[1,128,512]{2,1,0:T(8,128)S(1)}, u32[]{:S(2)}, u32[]{:S(2)}) collective-permute-start(f32[1,128,512]{2,1,0:T(8,128)} %get-tuple-element.94), channel_id=1, source_target_pairs={{0,16},{8,24},{16,0},{24,8},{1,17},{9,25},{17,1},{25,9},{2,18},{10... | collective-permute-start | bytes 786440 | tf_op jit(solution)/shard_map/ppermute | solution.py:15
  52.5 15.6 %all-to-all-start.1 = ((f32[8,32,256]{2,1,0:T(8,128)}), f32[8,32,256]{2,1,0:T(8,128)S(1)}, u32[]{:S(2)}, u32[]{:S(2)}) async-start(f32[8,32,256]{2,1,0:T(8,128)} %broadcast_in_dim.6), calls=%async_computation.1 | async-start | bytes 524288 | tf_op jit(solution)/shard_map/all_to_all | solution.py:296
  57.0 101.9 %copy-start.3 = (s32[3]{0:T(128)S(1)}, s32[3]{0:T(128)}, u32[]{:S(2)}) copy-start(s32[3]{0:T(128)} %pad_add_fusion.place) | copy-start | bytes 40
  57.0 8.6 %collective-permute-start.6 = (f32[1,128,512]{2,1,0:T(8,128)}, f32[1,128,512]{2,1,0:T(8,128)S(1)}, u32[]{:S(2)}, u32[]{:S(2)}) collective-permute-start(f32[1,128,512]{2,1,0:T(8,128)} %get-tuple-element.106), channel_id=1, source_target_pairs={{0,8},{8,16},{16,24},{24,0},{1,9},{9,17},{17,25},{25,1},{2,10},{10... | collective-permute-start | bytes 786440 | tf_op jit(solution)/shard_map/ppermute | solution.py:15
  58.1 7.5 %collective-permute-start.7 = (f32[1,128,512]{2,1,0:T(8,128)}, f32[1,128,512]{2,1,0:T(8,128)}, u32[]{:S(2)}, u32[]{:S(2)}) collective-permute-start(f32[1,128,512]{2,1,0:T(8,128)} %get-tuple-element.107), channel_id=1, source_target_pairs={{0,24},{8,0},{16,8},{24,16},{1,25},{9,1},{17,9},{25,17},{2,26},{10... | collective-permute-start | bytes 786440 | tf_op jit(solution)/shard_map/ppermute | solution.py:15
  63.8 95.1 %copy-start.1 = (f32[1,128,1024]{2,1,0:T(8,128)S(1)}, f32[1,128,1024]{2,1,0:T(8,128)}, u32[]{:S(2)}) copy-start(f32[1,128,1024]{2,1,0:T(8,128)} %get-tuple-element.137.own_ref) | copy-start | bytes 1572868
  65.6 16.7 %copy-start.11 = (f32[1,128,512]{2,1,0:T(8,128)}, f32[1,128,512]{2,1,0:T(8,128)S(1)}, u32[]{:S(2)}) copy-start(f32[1,128,512]{2,1,0:T(8,128)S(1)} %collective-permute-done.6.refs_5_) | copy-start | bytes 786436
  68.1 9.2 %collective-permute-start.10 = (f32[8,32,256]{2,1,0:T(8,128)S(1)}, f32[8,32,256]{2,1,0:T(8,128)S(1)}, u32[]{:S(2)}, u32[]{:S(2)}) collective-permute-start(f32[8,32,256]{2,1,0:T(8,128)S(1)} %all-to-all-done.1.refs_0_), channel_id=1, source_target_pairs={{0,24},{8,0},{16,8},{24,16},{1,25},{9,1},{17,9},{25,17},{2,26},{10... | collective-permute-start | bytes 786440 | tf_op jit(solution)/shard_map/ppermute | solution.py:15
  70.1 12.2 %collective-permute-start.8 = (f32[8,32,256]{2,1,0:T(8,128)S(1)}, f32[8,32,256]{2,1,0:T(8,128)S(1)}, u32[]{:S(2)}, u32[]{:S(2)}) collective-permute-start(f32[8,32,256]{2,1,0:T(8,128)S(1)} %all-to-all-done.1.refs_0_), channel_id=1, source_target_pairs={{0,8},{8,16},{16,24},{24,0},{1,9},{9,17},{17,25},{25,1},{2,10},{10... | collective-permute-start | bytes 786440 | tf_op jit(solution)/shard_map/ppermute | solution.py:15
  70.2 12.2 %collective-permute-start.9 = (f32[8,32,256]{2,1,0:T(8,128)S(1)}, f32[8,32,256]{2,1,0:T(8,128)S(1)}, u32[]{:S(2)}, u32[]{:S(2)}) collective-permute-start(f32[8,32,256]{2,1,0:T(8,128)S(1)} %all-to-all-done.1.refs_0_), channel_id=1, source_target_pairs={{0,16},{8,24},{16,0},{24,8},{1,17},{9,25},{17,1},{25,9},{2,18},{10... | collective-permute-start | bytes 786440 | tf_op jit(solution)/shard_map/ppermute | solution.py:15
  83.7 1.4 collective-permute-start.11
  85.1 8.0 %collective-permute-start.12 = (f32[128,256]{1,0:T(8,128)S(1)}, f32[128,256]{1,0:T(8,128)S(1)}, u32[]{:S(2)}, u32[]{:S(2)}) collective-permute-start(f32[128,256]{1,0:T(8,128)S(1)} %add.78), channel_id=1, source_target_pairs={{0,2},{1,3},{2,0},{3,1},{4,6},{5,7},{6,4},{7,5},{8,10},{9,11},{10,... | collective-permute-start | bytes 393224 | tf_op jit(solution)/shard_map/ppermute | solution.py:15
  87.3 7.8 %collective-permute-start.13 = (f32[128,256]{1,0:T(8,128)S(1)}, f32[128,256]{1,0:T(8,128)S(1)}, u32[]{:S(2)}, u32[]{:S(2)}) collective-permute-start(f32[128,256]{1,0:T(8,128)S(1)} %add.78), channel_id=1, source_target_pairs={{0,1},{1,2},{2,3},{3,0},{4,5},{5,6},{6,7},{7,4},{8,9},{9,10},{10,1... | collective-permute-start | bytes 393224 | tf_op jit(solution)/shard_map/ppermute | solution.py:15
  87.3 7.8 %collective-permute-start.14 = (f32[128,256]{1,0:T(8,128)S(1)}, f32[128,256]{1,0:T(8,128)S(1)}, u32[]{:S(2)}, u32[]{:S(2)}) collective-permute-start(f32[128,256]{1,0:T(8,128)S(1)} %add.78), channel_id=1, source_target_pairs={{0,3},{1,0},{2,1},{3,2},{4,7},{5,4},{6,5},{7,6},{8,11},{9,8},{10,9... | collective-permute-start | bytes 393224 | tf_op jit(solution)/shard_map/ppermute | solution.py:15
  95.2 9.4 %collective-permute-start.15 = (f32[128,256]{1,0:T(8,128)S(1)}, f32[128,256]{1,0:T(8,128)S(1)}, u32[]{:S(2)}, u32[]{:S(2)}) collective-permute-start(f32[128,256]{1,0:T(8,128)S(1)} %slice_subtract_fusion.1.refs_0_), channel_id=1, source_target_pairs={{0,8},{8,16},{16,24},{24,0},{1,9},{9,17},{17,25},{25,1},{2,10},{10... | collective-permute-start | bytes 393224 | tf_op jit(solution)/shard_map/ppermute | solution.py:15
  95.3 9.4 %collective-permute-start.16 = (f32[128,256]{1,0:T(8,128)S(1)}, f32[128,256]{1,0:T(8,128)S(1)}, u32[]{:S(2)}, u32[]{:S(2)}) collective-permute-start(f32[128,256]{1,0:T(8,128)S(1)} %slice_subtract_fusion.1.refs_0_), channel_id=1, source_target_pairs={{0,16},{8,24},{16,0},{24,8},{1,17},{9,25},{17,1},{25,9},{2,18},{10... | collective-permute-start | bytes 393224 | tf_op jit(solution)/shard_map/ppermute | solution.py:15
  97.5 7.8 %collective-permute-start.17 = (f32[128,256]{1,0:T(8,128)S(1)}, f32[128,256]{1,0:T(8,128)S(1)}, u32[]{:S(2)}, u32[]{:S(2)}) collective-permute-start(f32[128,256]{1,0:T(8,128)S(1)} %slice_subtract_fusion.1.refs_0_), channel_id=1, source_target_pairs={{0,24},{8,0},{16,8},{24,16},{1,25},{9,1},{17,9},{25,17},{2,26},{10... | collective-permute-start | bytes 393224 | tf_op jit(solution)/shard_map/ppermute | solution.py:15
  109.4 1.7 collective-permute-start.18
  109.4 20.9 %collective-permute-start.20 = (f32[1,128,1024]{2,1,0:T(8,128)}, f32[1,128,1024]{2,1,0:T(8,128)S(1)}, u32[]{:S(2)}, u32[]{:S(2)}) collective-permute-start(f32[1,128,1024]{2,1,0:T(8,128)} %get-tuple-element.134), channel_id=1, source_target_pairs={{0,4},{4,0},{1,5},{5,1},{2,6},{6,2},{3,7},{7,3},{8,12},{12,8},{9,1... | collective-permute-start | bytes 1572872 | tf_op jit(solution)/shard_map/ppermute | solution.py:15
  112.8 17.4 %all-to-all-start.2 = ((f32[8,32,256]{2,1,0:T(8,128)}), f32[8,32,256]{2,1,0:T(8,128)S(1)}, u32[]{:S(2)}, u32[]{:S(2)}) async-start(f32[8,32,256]{2,1,0:T(8,128)} %add.82), calls=%async_computation.2 | async-start | bytes 524288 | tf_op jit(solution)/shard_map/all_to_all | solution.py:293
  118.1 12.2 %collective-permute-start.19 = (f32[1,128,512]{2,1,0:T(8,128)}, f32[1,128,512]{2,1,0:T(8,128)S(1)}, u32[]{:S(2)}, u32[]{:S(2)}) collective-permute-start(f32[1,128,512]{2,1,0:T(8,128)} %get-tuple-element.130), channel_id=1, source_target_pairs={{0,16},{8,24},{16,0},{24,8},{1,17},{9,25},{17,1},{25,9},{2,18},{10... | collective-permute-start | bytes 786440 | tf_op jit(solution)/shard_map/ppermute | solution.py:15
  130.3 51.8 %copy-start.10 = (f32[1,128,512]{2,1,0:T(8,128)}, f32[1,128,512]{2,1,0:T(8,128)S(1)}, u32[]{:S(2)}) copy-start(f32[1,128,512]{2,1,0:T(8,128)S(1)} %collective-permute-done.19.refs_6_) | copy-start | bytes 786436
  131.1 15.2 %all-to-all-start.3 = ((f32[8,32,256]{2,1,0:T(8,128)}), f32[8,32,256]{2,1,0:T(8,128)S(1)}, u32[]{:S(2)}, u32[]{:S(2)}) async-start(f32[8,32,256]{2,1,0:T(8,128)} %broadcast_in_dim.7), calls=%async_computation.3 | async-start | bytes 524288 | tf_op jit(solution)/shard_map/all_to_all | solution.py:296
  135.5 8.0 %collective-permute-start.21 = (f32[1,128,512]{2,1,0:T(8,128)}, f32[1,128,512]{2,1,0:T(8,128)S(1)}, u32[]{:S(2)}, u32[]{:S(2)}) collective-permute-start(f32[1,128,512]{2,1,0:T(8,128)} %get-tuple-element.139), channel_id=1, source_target_pairs={{0,8},{8,16},{16,24},{24,0},{1,9},{9,17},{17,25},{25,1},{2,10},{10... | collective-permute-start | bytes 786440 | tf_op jit(solution)/shard_map/ppermute | solution.py:15
  135.8 7.8 %collective-permute-start.22 = (f32[1,128,512]{2,1,0:T(8,128)}, f32[1,128,512]{2,1,0:T(8,128)S(1)}, u32[]{:S(2)}, u32[]{:S(2)}) collective-permute-start(f32[1,128,512]{2,1,0:T(8,128)} %get-tuple-element.140), channel_id=1, source_target_pairs={{0,24},{8,0},{16,8},{24,16},{1,25},{9,1},{17,9},{25,17},{2,26},{10... | collective-permute-start | bytes 786440 | tf_op jit(solution)/shard_map/ppermute | solution.py:15
  143.6 38.5 %copy-start.12 = (f32[1,128,512]{2,1,0:T(8,128)}, f32[1,128,512]{2,1,0:T(8,128)S(1)}, u32[]{:S(2)}) copy-start(f32[1,128,512]{2,1,0:T(8,128)S(1)} %collective-permute-done.21.refs_5_) | copy-start | bytes 786436
  143.6 38.5 %copy-start.13 = (f32[1,128,512]{2,1,0:T(8,128)}, f32[1,128,512]{2,1,0:T(8,128)S(1)}, u32[]{:S(2)}) copy-start(f32[1,128,512]{2,1,0:T(8,128)S(1)} %collective-permute-done.22.refs_7_) | copy-start | bytes 786436
  146.2 9.8 %collective-permute-start.23 = (f32[8,32,256]{2,1,0:T(8,128)S(1)}, f32[8,32,256]{2,1,0:T(8,128)S(1)}, u32[]{:S(2)}, u32[]{:S(2)}) collective-permute-start(f32[8,32,256]{2,1,0:T(8,128)S(1)} %all-to-all-done.3.refs_0_), channel_id=1, source_target_pairs={{0,8},{8,16},{16,24},{24,0},{1,9},{9,17},{17,25},{25,1},{2,10},{10... | collective-permute-start | bytes 786440 | tf_op jit(solution)/shard_map/ppermute | solution.py:15
  146.5 12.3 %collective-permute-start.24 = (f32[8,32,256]{2,1,0:T(8,128)S(1)}, f32[8,32,256]{2,1,0:T(8,128)S(1)}, u32[]{:S(2)}, u32[]{:S(2)}) collective-permute-start(f32[8,32,256]{2,1,0:T(8,128)S(1)} %all-to-all-done.3.refs_0_), channel_id=1, source_target_pairs={{0,16},{8,24},{16,0},{24,8},{1,17},{9,25},{17,1},{25,9},{2,18},{10... | collective-permute-start | bytes 786440 | tf_op jit(solution)/shard_map/ppermute | solution.py:15
  150.1 8.9 %collective-permute-start.25 = (f32[8,32,256]{2,1,0:T(8,128)S(1)}, f32[8,32,256]{2,1,0:T(8,128)S(1)}, u32[]{:S(2)}, u32[]{:S(2)}) collective-permute-start(f32[8,32,256]{2,1,0:T(8,128)S(1)} %all-to-all-done.3.refs_0_), channel_id=1, source_target_pairs={{0,24},{8,0},{16,8},{24,16},{1,25},{9,1},{17,9},{25,17},{2,26},{10... | collective-permute-start | bytes 786440 | tf_op jit(solution)/shard_map/ppermute | solution.py:15
  160.2 1.4 collective-permute-start.26
  161.7 8.0 %collective-permute-start.27 = (f32[128,256]{1,0:T(8,128)S(1)}, f32[128,256]{1,0:T(8,128)S(1)}, u32[]{:S(2)}, u32[]{:S(2)}) collective-permute-start(f32[128,256]{1,0:T(8,128)S(1)} %add_add_fusion), channel_id=1, source_target_pairs={{0,2},{1,3},{2,0},{3,1},{4,6},{5,7},{6,4},{7,5},{8,10},{9,11},{10,... | collective-permute-start | bytes 393224 | tf_op jit(solution)/shard_map/ppermute | solution.py:15
  163.4 6.8 %collective-permute-start.28 = (f32[128,256]{1,0:T(8,128)S(1)}, f32[128,256]{1,0:T(8,128)S(1)}, u32[]{:S(2)}, u32[]{:S(2)}) collective-permute-start(f32[128,256]{1,0:T(8,128)S(1)} %add_add_fusion), channel_id=1, source_target_pairs={{0,1},{1,2},{2,3},{3,0},{4,5},{5,6},{6,7},{7,4},{8,9},{9,10},{10,1... | collective-permute-start | bytes 393224 | tf_op jit(solution)/shard_map/ppermute | solution.py:15
  163.6 8.1 %collective-permute-start.29 = (f32[128,256]{1,0:T(8,128)S(1)}, f32[128,256]{1,0:T(8,128)S(1)}, u32[]{:S(2)}, u32[]{:S(2)}) collective-permute-start(f32[128,256]{1,0:T(8,128)S(1)} %add_add_fusion), channel_id=1, source_target_pairs={{0,3},{1,0},{2,1},{3,2},{4,7},{5,4},{6,5},{7,6},{8,11},{9,8},{10,9... | collective-permute-start | bytes 393224 | tf_op jit(solution)/shard_map/ppermute | solution.py:15
  171.7 10.4 %copy-start.5 = (f32[128,256]{1,0:T(8,128)}, f32[128,256]{1,0:T(8,128)S(1)}, u32[]{:S(2)}) copy-start(f32[128,256]{1,0:T(8,128)S(1)} %slice_subtract_fusion.refs_0_) | copy-start | bytes 393220
  171.7 6.8 %collective-permute-start.30 = (f32[128,256]{1,0:T(8,128)S(1)}, f32[128,256]{1,0:T(8,128)S(1)}, u32[]{:S(2)}, u32[]{:S(2)}) collective-permute-start(f32[128,256]{1,0:T(8,128)S(1)} %slice_subtract_fusion.refs_0_), channel_id=1, source_target_pairs={{0,8},{8,16},{16,24},{24,0},{1,9},{9,17},{17,25},{25,1},{2,10},{10... | collective-permute-start | bytes 393224 | tf_op jit(solution)/shard_map/ppermute | solution.py:15
  172.0 10.0 %collective-permute-start.31 = (f32[128,256]{1,0:T(8,128)S(1)}, f32[128,256]{1,0:T(8,128)S(1)}, u32[]{:S(2)}, u32[]{:S(2)}) collective-permute-start(f32[128,256]{1,0:T(8,128)S(1)} %slice_subtract_fusion.refs_0_), channel_id=1, source_target_pairs={{0,16},{8,24},{16,0},{24,8},{1,17},{9,25},{17,1},{25,9},{2,18},{10... | collective-permute-start | bytes 393224 | tf_op jit(solution)/shard_map/ppermute | solution.py:15
  175.8 6.2 %collective-permute-start.32 = (f32[128,256]{1,0:T(8,128)S(1)}, f32[128,256]{1,0:T(8,128)S(1)}, u32[]{:S(2)}, u32[]{:S(2)}) collective-permute-start(f32[128,256]{1,0:T(8,128)S(1)} %slice_subtract_fusion.refs_0_), channel_id=1, source_target_pairs={{0,24},{8,0},{16,8},{24,16},{1,25},{9,1},{17,9},{25,17},{2,26},{10... | collective-permute-start | bytes 393224 | tf_op jit(solution)/shard_map/ppermute | solution.py:15
  186.9 1.7 collective-permute-start.33
  (13 other events, 43.2 us)

commit v3 on v0

--- a/solution.py
+++ b/solution.py
@@ -183,7 +183,7 @@
 
 
 def factor_kernel(place, block_high, block_low, *refs):
-    pieces, rest, (out_ref, high, low) = refs[: Y + 1], refs[Y + 1], refs[Y + 2 :]
+    pieces, rest, (out_ref, high, low) = refs[: Y + 2], refs[Y + 2], refs[Y + 3 :]
     y, core = place[1], place[2]
     share = pieces[0].shape[1]
 
@@ -192,7 +192,7 @@
             for e in range(Y):
                 row = (z * Y + lax.rem(y + Y - e, Y)) * CORE + owner
                 where = pl.ds(pl.multiple_of(row * share, share), share)
-                piece = rest[e - 1, z] if at and e else pieces[at * Y + e][z]
+                piece = rest[e - 2, z] if at and e > 1 else pieces[at * Y + e][z]
                 high[where, :], low[where, :] = halves(piece)
         return carry
 
@@ -212,7 +212,7 @@
             num_scalar_prefetch=1,
             grid=(1,),
             in_specs=[pl.BlockSpec((rows, columns), lambda i, place: (0, 0))] * 2
-            + [pl.BlockSpec(pieces[0].shape, lambda i, place: (0, 0, 0))] * (Y + 1)
+            + [pl.BlockSpec(pieces[0].shape, lambda i, place: (0, 0, 0))] * (Y + 2)
             + [pl.BlockSpec(pieces[-1].shape, lambda i, place: (0, 0, 0, 0))],
             out_specs=pl.BlockSpec((rows, new), lambda i, place: (0, 0)),
             scratch_shapes=[pltpu.VMEM((columns, new), jnp.bfloat16)] * 2,
@@ -275,8 +275,8 @@
 
     def gather(line):
         mine = in_order(line, spread({e: line for e in range(1, Y)}))
-        rest = shift(jnp.stack(mine[1:]), "core", 1, CORE)
-        return mine + [shift(line, "core", 1, CORE), rest]
+        rest = shift(jnp.stack(mine[2:]), "core", 1, CORE)
+        return mine + [shift(piece, "core", 1, CORE) for piece in mine[:2]] + [rest]
 
     def residual_rows(panel, own):
         arrived = [shift(own, "col", by, N_COL) for by in (2, 1, 3)]

time: 197 us -> 199 us (1.010)
  local copies, waits for them, and re-layouts: 4.75 us -> 7.6 us
    unnamed x46, local copies, waits for them, and re-layouts: 2.47 us -> 5.32 us
    ppermute x34 -> x36, starting transfers between devices: 44.5 us -> 43.8 us  [shift(): lax.ppermute(value, axis, [(i, (i + by) % size) for i in range(size)])]
    ppermute x34 -> x36, waiting for transfers between devices: 54.7 us -> 54 us  [shift(): lax.ppermute(value, axis, [(i, (i + by) % size) for i in range(size)])]
  transfers between devices with their start and end apart: 38 -> 40, of which waited for: 25 -> 28; matrix products, arithmetic and copies ran while one was open for 1% -> 1% of each run, Pallas kernels for 8% -> 8%
where the time goes in v3:
time: 199 us; the launch traced here: 198 us
  waiting for transfers between devices  74.7 us (38%)
  starting transfers between devices  67 us (34%)
  Pallas kernels  26.7 us (13%)
  blocking collectives  16.9 us (8%)
  local copies, waits for them, and re-layouts  7.6 us (4%)
  other arithmetic  3.35 us (2%)
    ppermute x36, waiting for transfers between devices, shift(): lax.ppermute(value, axis, [(i, (i + by) % size) for i in range(size)])  54 us
    ppermute x36, starting transfers between devices, shift(): lax.ppermute(value, axis, [(i, (i + by) % size) for i in range(size)])  43.8 us
    all_to_all x1, blocking collectives, reduce(): return jnp.sum(lax.all_to_all(chip, 'z', 0, 0), axis=0)  16.9 us
    all_to_all x2, waiting for transfers between devices, reduce(): return jnp.sum(lax.all_to_all(chip, 'z', 0, 0), axis=0)  16.7 us
    all_to_all x2, starting transfers between devices, reduce(): return jnp.sum(lax.all_to_all(chip, 'z', 0, 0), axis=0)  14.4 us
    pallas_call x3, Pallas kernels, split_columns(): pl.pallas_call(functools.partial(split_kernel, len(blocks)), out_shape=[o...  10.9 us
    all_to_all x2, starting transfers between devices, gather_z(): lax.all_to_all(jnp.broadcast_to(rows[None], (Z,) + rows.shape), 'z', 0, 0)  8.87 us
    pallas_call x3, Pallas kernels, halve_block(): pl.pallas_call(halve_kernel, out_shape=(out, out), grid=(1,), in_specs=[p...  7.68 us
  transfers between devices with their start and end apart: 40, of which 28 were waited for; matrix products, arithmetic and copies ran while one was open for 1% of the time, Pallas kernels for 8%

profile of v3, /device:TPU:2, one launch (start us, length us, event | category | flops | bytes accessed | tf_op | source)
XLA Modules:
  0.0 197.8 jit_solution(16327056124067927490)
XLA Ops:
  0.7 3.7 %shard_map.55 = (f32[1,136,512]{2,1,0:T(8,128)}, f32[1,136,512]{2,1,0:T(8,128)}, f32[1,136,512]{2,1,0:T(8,128)}, f32[1,136,512]{2,1,0:T(8,128)}) custom-call(s32[3]{0:T(128)} %pad_add_fusion.place, f32[3,1,128,1,2048]{4,3,2,1,0:T(1,128)} %refs_0_.5, f32[16,3,1,128]{3,2,1,0:T(1,128)} %refs_1_.1), custom_call_target="tpu_custom_call" | custom-call | flops 262144 | bytes 2097152 | tf_op jit(solution)/shard_map/pallas_call | solution.py:89
  4.3 1.6 collective-permute-start
  5.9 2.9 %collective-permute-start.1 = (f32[1,136,512]{2,1,0:T(8,128)}, f32[1,136,512]{2,1,0:T(8,128)S(1)}, u32[]{:S(2)}, u32[]{:S(2)}) collective-permute-start(f32[1,136,512]{2,1,0:T(8,128)} %get-tuple-element.74), channel_id=1, source_target_pairs={{0,16},{8,24},{16,0},{24,8},{1,17},{9,25},{17,1},{25,9},{2,18},{10... | collective-permute-start | bytes 835592 | tf_op jit(solution)/shard_map/ppermute | solution.py:15
  10.2 3.6 %shard_map.56 = (f32[1,128,512]{2,1,0:T(8,128)}, f32[1,128,512]{2,1,0:T(8,128)}, f32[1,128,512]{2,1,0:T(8,128)}, f32[1,128,512]{2,1,0:T(8,128)}) custom-call(s32[3]{0:T(128)} %pad_add_fusion.place, f32[3,1,128,1,2048]{4,3,2,1,0:T(1,128)} %refs_0_.5), custom_call_target="tpu_custom_call" | custom-call | flops 262144 | bytes 2097152 | tf_op jit(solution)/shard_map/pallas_call | solution.py:89
  14.5 2.6 %shard_map.57 = (bf16[128,2048]{1,0:T(8,128)(2,1)}, bf16[128,2048]{1,0:T(8,128)(2,1)}) custom-call(f32[3,1,128,3,1,2048]{5,4,3,2,1,0:T(1,128)} %block_ref.5), custom_call_target="tpu_custom_call" | custom-call | flops 1048576 | bytes 2097152 | tf_op jit(solution)/shard_map/pallas_call | solution.py:167
  17.1 2.6 %shard_map.58 = (bf16[128,2048]{1,0:T(8,128)(2,1)}, bf16[128,2048]{1,0:T(8,128)(2,1)}) custom-call(f32[3,1,128,3,1,2048]{5,4,3,2,1,0:T(1,128)} %block_ref.5), custom_call_target="tpu_custom_call" | custom-call | flops 1048576 | bytes 2097152 | tf_op jit(solution)/shard_map/pallas_call | solution.py:167
  19.8 1.6 collective-permute-done.1.refs_6_
  23.7 1.5 collective-permute-done.3
  25.9 8.5 %all-to-all-start = ((f32[8,32,256]{2,1,0:T(8,128)}), f32[8,32,256]{2,1,0:T(8,128)S(1)}, u32[]{:S(2)}, u32[]{:S(2)}) async-start(f32[8,32,256]{2,1,0:T(8,128)} %add.64), calls=%async_computation | async-start | bytes 524288 | tf_op jit(solution)/shard_map/all_to_all | solution.py:271
  34.4 2.7 %collective-permute-start.4 = (f32[1,128,512]{2,1,0:T(8,128)S(1)}, f32[1,128,512]{2,1,0:T(8,128)S(1)}, u32[]{:S(2)}, u32[]{:S(2)}) collective-permute-start(f32[1,128,512]{2,1,0:T(8,128)S(1)} %copy-done.22), channel_id=1, source_target_pairs={{0,16},{8,24},{16,0},{24,8},{1,17},{9,25},{17,1},{25,9},{2,18},{10... | collective-permute-start | bytes 786440 | tf_op jit(solution)/shard_map/ppermute | solution.py:15
  37.1 3.6 %shard_map.60 = (f32[1,128,512]{2,1,0:T(8,128)}, f32[1,128,512]{2,1,0:T(8,128)}, f32[1,128,512]{2,1,0:T(8,128)}, f32[1,128,512]{2,1,0:T(8,128)}) custom-call(s32[3]{0:T(128)} %pad_add_fusion.place, f32[3,1,128,1,2048]{4,3,2,1,0:T(1,128)} %refs_0_.5), custom_call_target="tpu_custom_call" | custom-call | flops 262144 | bytes 2097152 | tf_op jit(solution)/shard_map/pallas_call | solution.py:89
  40.6 5.9 %all-to-all-done = f32[8,32,256]{2,1,0:T(8,128)S(1)} async-done(((f32[8,32,256]{2,1,0:T(8,128)}), f32[8,32,256]{2,1,0:T(8,128)S(1)}, u32[]{:S(2)}, u32[]{:S(2)}) %all-to-all-start) | async-done | bytes 262176 | tf_op jit(solution)/shard_map/all_to_all | solution.py:271
  47.4 4.4 %all-to-all-start.1 = ((f32[8,32,256]{2,1,0:T(8,128)}), f32[8,32,256]{2,1,0:T(8,128)S(1)}, u32[]{:S(2)}, u32[]{:S(2)}) async-start(f32[8,32,256]{2,1,0:T(8,128)} %broadcast_in_dim.6), calls=%async_computation.1 | async-start | bytes 524288 | tf_op jit(solution)/shard_map/all_to_all | solution.py:274
  52.9 2.1 %collective-permute-start.6 = (f32[1,128,512]{2,1,0:T(8,128)}, f32[1,128,512]{2,1,0:T(8,128)S(1)}, u32[]{:S(2)}, u32[]{:S(2)}) collective-permute-start(f32[1,128,512]{2,1,0:T(8,128)} %get-tuple-element.102), channel_id=1, source_target_pairs={{0,24},{8,0},{16,8},{24,16},{1,25},{9,1},{17,9},{25,17},{2,26},{10... | collective-permute-start | bytes 786440 | tf_op jit(solution)/shard_map/ppermute | solution.py:15
  55.0 2.5 %shard_map.61 = (bf16[128,2048]{1,0:T(8,128)(2,1)}, bf16[128,2048]{1,0:T(8,128)(2,1)}) custom-call(f32[3,1,128,3,1,2048]{5,4,3,2,1,0:T(1,128)} %block_ref.5), custom_call_target="tpu_custom_call" | custom-call | flops 1048576 | bytes 2097152 | tf_op jit(solution)/shard_map/pallas_call | solution.py:167
  57.5 2.3 %collective-permute-done.5.refs_5_ = f32[1,128,512]{2,1,0:T(8,128)S(1)} collective-permute-done((f32[1,128,512]{2,1,0:T(8,128)}, f32[1,128,512]{2,1,0:T(8,128)S(1)}, u32[]{:S(2)}, u32[]{:S(2)}) %collective-permute-start.5) | collective-permute-done | bytes 262176 | tf_op jit(solution)/shard_map/ppermute | solution.py:15
  62.5 2.6 %collective-permute-start.8 = (f32[8,32,256]{2,1,0:T(8,128)S(1)}, f32[8,32,256]{2,1,0:T(8,128)S(1)}, u32[]{:S(2)}, u32[]{:S(2)}) collective-permute-start(f32[8,32,256]{2,1,0:T(8,128)S(1)} %all-to-all-done.1.refs_0_), channel_id=1, source_target_pairs={{0,16},{8,24},{16,0},{24,8},{1,17},{9,25},{17,1},{25,9},{2,18},{10... | collective-permute-start | bytes 786440 | tf_op jit(solution)/shard_map/ppermute | solution.py:15
  67.1 5.0 %collective-permute-done.8.refs_2_ = f32[8,32,256]{2,1,0:T(8,128)S(1)} collective-permute-done((f32[8,32,256]{2,1,0:T(8,128)S(1)}, f32[8,32,256]{2,1,0:T(8,128)S(1)}, u32[]{:S(2)}, u32[]{:S(2)}) %collective-permute-start.8) | collective-permute-done | bytes 262176 | tf_op jit(solution)/shard_map/ppermute | solution.py:15
  72.1 2.1 %collective-permute-done.9.refs_3_ = f32[8,32,256]{2,1,0:T(8,128)S(1)} collective-permute-done((f32[8,32,256]{2,1,0:T(8,128)S(1)}, f32[8,32,256]{2,1,0:T(8,128)S(1)}, u32[]{:S(2)}, u32[]{:S(2)}) %collective-permute-start.9) | collective-permute-done | bytes 262176 | tf_op jit(solution)/shard_map/ppermute | solution.py:15
  77.0 1.5 shard_map.62
  78.5 2.2 %collective-permute-start.13 = (f32[128,256]{1,0:T(8,128)S(1)}, f32[128,256]{1,0:T(8,128)S(1)}, u32[]{:S(2)}, u32[]{:S(2)}) collective-permute-start(f32[128,256]{1,0:T(8,128)S(1)} %shard_map.62), channel_id=1, source_target_pairs={{0,2},{1,3},{2,0},{3,1},{4,6},{5,7},{6,4},{7,5},{8,10},{9,11},{10,... | collective-permute-start | bytes 393224 | tf_op jit(solution)/shard_map/ppermute | solution.py:15
  80.8 2.0 %collective-permute-start.15 = (f32[128,256]{1,0:T(8,128)S(1)}, f32[128,256]{1,0:T(8,128)S(1)}, u32[]{:S(2)}, u32[]{:S(2)}) collective-permute-start(f32[128,256]{1,0:T(8,128)S(1)} %shard_map.62), channel_id=1, source_target_pairs={{0,3},{1,0},{2,1},{3,2},{4,7},{5,4},{6,5},{7,6},{8,11},{9,8},{10,9... | collective-permute-start | bytes 393224 | tf_op jit(solution)/shard_map/ppermute | solution.py:15
  83.3 3.2 %collective-permute-done.13 = f32[128,256]{1,0:T(8,128)S(1)} collective-permute-done((f32[128,256]{1,0:T(8,128)S(1)}, f32[128,256]{1,0:T(8,128)S(1)}, u32[]{:S(2)}, u32[]{:S(2)}) %collective-permute-start.13) | collective-permute-done | bytes 131104 | tf_op jit(solution)/shard_map/ppermute | solution.py:15
  86.5 2.0 %collective-permute-done.14 = f32[128,256]{1,0:T(8,128)S(1)} collective-permute-done((f32[128,256]{1,0:T(8,128)S(1)}, f32[128,256]{1,0:T(8,128)S(1)}, u32[]{:S(2)}, u32[]{:S(2)}) %collective-permute-start.14) | collective-permute-done | bytes 131104 | tf_op jit(solution)/shard_map/ppermute | solution.py:15
  88.6 1.8 collective-permute-start.16
  90.4 2.4 %collective-permute-start.17 = (f32[128,256]{1,0:T(8,128)S(1)}, f32[128,256]{1,0:T(8,128)S(1)}, u32[]{:S(2)}, u32[]{:S(2)}) collective-permute-start(f32[128,256]{1,0:T(8,128)S(1)} %slice_subtract_fusion.1.refs_0_), channel_id=1, source_target_pairs={{0,16},{8,24},{16,0},{24,8},{1,17},{9,25},{17,1},{25,9},{2,18},{10... | collective-permute-start | bytes 393224 | tf_op jit(solution)/shard_map/ppermute | solution.py:15
  95.4 3.5 %collective-permute-done.17.refs_2_ = f32[128,256]{1,0:T(8,128)S(1)} collective-permute-done((f32[128,256]{1,0:T(8,128)S(1)}, f32[128,256]{1,0:T(8,128)S(1)}, u32[]{:S(2)}, u32[]{:S(2)}) %collective-permute-start.17) | collective-permute-done | bytes 131104 | tf_op jit(solution)/shard_map/ppermute | solution.py:15
  104.0 1.5 collective-permute-done.19
  106.3 5.9 %all-to-all-start.2 = ((f32[8,32,256]{2,1,0:T(8,128)}), f32[8,32,256]{2,1,0:T(8,128)S(1)}, u32[]{:S(2)}, u32[]{:S(2)}) async-start(f32[8,32,256]{2,1,0:T(8,128)} %add.72), calls=%async_computation.2 | async-start | bytes 524288 | tf_op jit(solution)/shard_map/all_to_all | solution.py:271
  113.6 10.8 %all-to-all-done.2 = f32[8,32,256]{2,1,0:T(8,128)S(1)} async-done(((f32[8,32,256]{2,1,0:T(8,128)}), f32[8,32,256]{2,1,0:T(8,128)S(1)}, u32[]{:S(2)}, u32[]{:S(2)}) %all-to-all-start.2) | async-done | bytes 262176 | tf_op jit(solution)/shard_map/all_to_all | solution.py:271
  125.1 4.5 %all-to-all-start.3 = ((f32[8,32,256]{2,1,0:T(8,128)}), f32[8,32,256]{2,1,0:T(8,128)S(1)}, u32[]{:S(2)}, u32[]{:S(2)}) async-start(f32[8,32,256]{2,1,0:T(8,128)} %broadcast_in_dim.7), calls=%async_computation.3 | async-start | bytes 524288 | tf_op jit(solution)/shard_map/all_to_all | solution.py:274
  130.4 2.4 %collective-permute-start.22 = (f32[1,128,512]{2,1,0:T(8,128)}, f32[1,128,512]{2,1,0:T(8,128)S(1)}, u32[]{:S(2)}, u32[]{:S(2)}) collective-permute-start(f32[1,128,512]{2,1,0:T(8,128)} %get-tuple-element.131), channel_id=1, source_target_pairs={{0,24},{8,0},{16,8},{24,16},{1,25},{9,1},{17,9},{25,17},{2,26},{10... | collective-permute-start | bytes 786440 | tf_op jit(solution)/shard_map/ppermute | solution.py:15
  132.9 4.8 %collective-permute-done.21.refs_5_ = f32[1,128,512]{2,1,0:T(8,128)S(1)} collective-permute-done((f32[1,128,512]{2,1,0:T(8,128)}, f32[1,128,512]{2,1,0:T(8,128)S(1)}, u32[]{:S(2)}, u32[]{:S(2)}) %collective-permute-start.21) | collective-permute-done | bytes 262176 | tf_op jit(solution)/shard_map/ppermute | solution.py:15
  137.6 2.7 %all-to-all-done.3.refs_0_ = f32[8,32,256]{2,1,0:T(8,128)S(1)} async-done(((f32[8,32,256]{2,1,0:T(8,128)}), f32[8,32,256]{2,1,0:T(8,128)S(1)}, u32[]{:S(2)}, u32[]{:S(2)}) %all-to-all-start.3) | async-done | bytes 262176 | tf_op jit(solution)/shard_map/all_to_all | solution.py:274
  141.7 2.1 %collective-permute-start.25 = (f32[8,32,256]{2,1,0:T(8,128)S(1)}, f32[8,32,256]{2,1,0:T(8,128)S(1)}, u32[]{:S(2)}, u32[]{:S(2)}) collective-permute-start(f32[8,32,256]{2,1,0:T(8,128)S(1)} %all-to-all-done.3.refs_0_), channel_id=1, source_target_pairs={{0,24},{8,0},{16,8},{24,16},{1,25},{9,1},{17,9},{25,17},{2,26},{10... | collective-permute-start | bytes 786440 | tf_op jit(solution)/shard_map/ppermute | solution.py:15
  143.8 6.1 %collective-permute-done.24.refs_2_ = f32[8,32,256]{2,1,0:T(8,128)S(1)} collective-permute-done((f32[8,32,256]{2,1,0:T(8,128)S(1)}, f32[8,32,256]{2,1,0:T(8,128)S(1)}, u32[]{:S(2)}, u32[]{:S(2)}) %collective-permute-start.24) | collective-permute-done | bytes 262176 | tf_op jit(solution)/shard_map/ppermute | solution.py:15
  149.9 2.6 %collective-permute-done.25.refs_3_ = f32[8,32,256]{2,1,0:T(8,128)S(1)} collective-permute-done((f32[8,32,256]{2,1,0:T(8,128)S(1)}, f32[8,32,256]{2,1,0:T(8,128)S(1)}, u32[]{:S(2)}, u32[]{:S(2)}) %collective-permute-start.25) | collective-permute-done | bytes 262176 | tf_op jit(solution)/shard_map/ppermute | solution.py:15
  153.4 1.7 collective-permute-done.26.refs_4_
  155.5 1.5 shard_map.65
  157.0 1.7 collective-permute-start.29
  158.8 1.9 collective-permute-start.31
  160.7 4.3 %collective-permute-done.29 = f32[128,256]{1,0:T(8,128)S(1)} collective-permute-done((f32[128,256]{1,0:T(8,128)S(1)}, f32[128,256]{1,0:T(8,128)S(1)}, u32[]{:S(2)}, u32[]{:S(2)}) %collective-permute-start.29) | collective-permute-done | bytes 131104 | tf_op jit(solution)/shard_map/ppermute | solution.py:15
  165.4 1.5 collective-permute-done.31
  168.0 3.1 %collective-permute-start.33 = (f32[128,256]{1,0:T(8,128)S(1)}, f32[128,256]{1,0:T(8,128)S(1)}, u32[]{:S(2)}, u32[]{:S(2)}) collective-permute-start(f32[128,256]{1,0:T(8,128)S(1)} %slice_subtract_fusion.refs_0_), channel_id=1, source_target_pairs={{0,16},{8,24},{16,0},{24,8},{1,17},{9,25},{17,1},{25,9},{2,18},{10... | collective-permute-start | bytes 393224 | tf_op jit(solution)/shard_map/ppermute | solution.py:15
  171.3 2.5 %collective-permute-done.32.refs_1_ = f32[128,256]{1,0:T(8,128)S(1)} collective-permute-done((f32[128,256]{1,0:T(8,128)S(1)}, f32[128,256]{1,0:T(8,128)S(1)}, u32[]{:S(2)}, u32[]{:S(2)}) %collective-permute-start.32) | collective-permute-done | bytes 131104 | tf_op jit(solution)/shard_map/ppermute | solution.py:15
  173.8 3.5 %collective-permute-done.33.refs_2_ = f32[128,256]{1,0:T(8,128)S(1)} collective-permute-done((f32[128,256]{1,0:T(8,128)S(1)}, f32[128,256]{1,0:T(8,128)S(1)}, u32[]{:S(2)}, u32[]{:S(2)}) %collective-permute-start.33) | collective-permute-done | bytes 131104 | tf_op jit(solution)/shard_map/ppermute | solution.py:15
  178.7 1.5 collective-permute-done.35
  180.2 16.9 %all_to_all.25 = f32[8,32,256]{2,1,0:T(8,128)S(1)} all-to-all(f32[8,32,256]{2,1,0:T(8,128)S(1)} %add.77), channel_id=1, replica_groups=mesh['z'=8,'y'=4,'core'=2,'col'=4] {'z'}, dimensions={0} | all-to-all | bytes 524288 | tf_op jit(solution)/shard_map/all_to_all | solution.py:271
  (115 shorter events, 34.0 us)
Async XLA Ops:
  4.3 15.4 %collective-permute-start = (f32[1,136,512]{2,1,0:T(8,128)}, f32[1,136,512]{2,1,0:T(8,128)S(1)}, u32[]{:S(2)}, u32[]{:S(2)}) collective-permute-start(f32[1,136,512]{2,1,0:T(8,128)} %get-tuple-element.73), channel_id=1, source_target_pairs={{0,8},{8,16},{16,24},{24,0},{1,9},{9,17},{17,25},{25,1},{2,10},{10... | collective-permute-start | bytes 835592 | tf_op jit(solution)/shard_map/ppermute | solution.py:15
  5.9 15.5 %collective-permute-start.1 = (f32[1,136,512]{2,1,0:T(8,128)}, f32[1,136,512]{2,1,0:T(8,128)S(1)}, u32[]{:S(2)}, u32[]{:S(2)}) collective-permute-start(f32[1,136,512]{2,1,0:T(8,128)} %get-tuple-element.74), channel_id=1, source_target_pairs={{0,16},{8,24},{16,0},{24,8},{1,17},{9,25},{17,1},{25,9},{2,18},{10... | collective-permute-start | bytes 835592 | tf_op jit(solution)/shard_map/ppermute | solution.py:15
  8.8 12.6 %collective-permute-start.2 = (f32[1,136,512]{2,1,0:T(8,128)}, f32[1,136,512]{2,1,0:T(8,128)S(1)}, u32[]{:S(2)}, u32[]{:S(2)}) collective-permute-start(f32[1,136,512]{2,1,0:T(8,128)} %get-tuple-element.75), channel_id=1, source_target_pairs={{0,24},{8,0},{16,8},{24,16},{1,25},{9,1},{17,9},{25,17},{2,26},{10... | collective-permute-start | bytes 835592 | tf_op jit(solution)/shard_map/ppermute | solution.py:15
  22.3 54.8 %copy-start.4 = (bf16[128,2048]{1,0:T(8,128)(2,1)S(1)}, bf16[128,2048]{1,0:T(8,128)(2,1)}, u32[]{:S(2)}) copy-start(bf16[128,2048]{1,0:T(8,128)(2,1)} %get-tuple-element.99.block_high) | copy-start | bytes 1572868
  22.3 54.7 %copy-start.5 = (bf16[128,2048]{1,0:T(8,128)(2,1)S(1)}, bf16[128,2048]{1,0:T(8,128)(2,1)}, u32[]{:S(2)}) copy-start(bf16[128,2048]{1,0:T(8,128)(2,1)} %get-tuple-element.100.block_low) | copy-start | bytes 1572868
  23.6 1.6 collective-permute-start.3
  25.9 20.6 %all-to-all-start = ((f32[8,32,256]{2,1,0:T(8,128)}), f32[8,32,256]{2,1,0:T(8,128)S(1)}, u32[]{:S(2)}, u32[]{:S(2)}) async-start(f32[8,32,256]{2,1,0:T(8,128)} %add.64), calls=%async_computation | async-start | bytes 524288 | tf_op jit(solution)/shard_map/all_to_all | solution.py:271
  34.4 59.3 %copy-start.2 = (bf16[128,2048]{1,0:T(8,128)(2,1)S(1)}, bf16[128,2048]{1,0:T(8,128)(2,1)}, u32[]{:S(2)}) copy-start(bf16[128,2048]{1,0:T(8,128)(2,1)} %get-tuple-element.110.block_high) | copy-start | bytes 1572868
  34.4 59.3 %copy-start.3 = (bf16[128,2048]{1,0:T(8,128)(2,1)S(1)}, bf16[128,2048]{1,0:T(8,128)(2,1)}, u32[]{:S(2)}) copy-start(bf16[128,2048]{1,0:T(8,128)(2,1)} %get-tuple-element.111.block_low) | copy-start | bytes 1572868
  34.4 12.2 %collective-permute-start.4 = (f32[1,128,512]{2,1,0:T(8,128)S(1)}, f32[1,128,512]{2,1,0:T(8,128)S(1)}, u32[]{:S(2)}, u32[]{:S(2)}) collective-permute-start(f32[1,128,512]{2,1,0:T(8,128)S(1)} %copy-done.22), channel_id=1, source_target_pairs={{0,16},{8,24},{16,0},{24,8},{1,17},{9,25},{17,1},{25,9},{2,18},{10... | collective-permute-start | bytes 786440 | tf_op jit(solution)/shard_map/ppermute | solution.py:15
  47.4 15.1 %all-to-all-start.1 = ((f32[8,32,256]{2,1,0:T(8,128)}), f32[8,32,256]{2,1,0:T(8,128)S(1)}, u32[]{:S(2)}, u32[]{:S(2)}) async-start(f32[8,32,256]{2,1,0:T(8,128)} %broadcast_in_dim.6), calls=%async_computation.1 | async-start | bytes 524288 | tf_op jit(solution)/shard_map/all_to_all | solution.py:274
  51.8 8.0 %collective-permute-start.5 = (f32[1,128,512]{2,1,0:T(8,128)}, f32[1,128,512]{2,1,0:T(8,128)S(1)}, u32[]{:S(2)}, u32[]{:S(2)}) collective-permute-start(f32[1,128,512]{2,1,0:T(8,128)} %get-tuple-element.101), channel_id=1, source_target_pairs={{0,8},{8,16},{16,24},{24,0},{1,9},{9,17},{17,25},{25,1},{2,10},{10... | collective-permute-start | bytes 786440 | tf_op jit(solution)/shard_map/ppermute | solution.py:15
  52.9 7.6 %collective-permute-start.6 = (f32[1,128,512]{2,1,0:T(8,128)}, f32[1,128,512]{2,1,0:T(8,128)S(1)}, u32[]{:S(2)}, u32[]{:S(2)}) collective-permute-start(f32[1,128,512]{2,1,0:T(8,128)} %get-tuple-element.102), channel_id=1, source_target_pairs={{0,24},{8,0},{16,8},{24,16},{1,25},{9,1},{17,9},{25,17},{2,26},{10... | collective-permute-start | bytes 786440 | tf_op jit(solution)/shard_map/ppermute | solution.py:15
  57.5 98.0 %copy-start = (bf16[128,2048]{1,0:T(8,128)(2,1)S(1)}, bf16[128,2048]{1,0:T(8,128)(2,1)}, u32[]{:S(2)}) copy-start(bf16[128,2048]{1,0:T(8,128)(2,1)} %get-tuple-element.128.block_high) | copy-start | bytes 1572868
  57.5 98.0 %copy-start.1 = (bf16[128,2048]{1,0:T(8,128)(2,1)S(1)}, bf16[128,2048]{1,0:T(8,128)(2,1)}, u32[]{:S(2)}) copy-start(bf16[128,2048]{1,0:T(8,128)(2,1)} %get-tuple-element.129.block_low) | copy-start | bytes 1572868
  62.5 9.6 %collective-permute-start.8 = (f32[8,32,256]{2,1,0:T(8,128)S(1)}, f32[8,32,256]{2,1,0:T(8,128)S(1)}, u32[]{:S(2)}, u32[]{:S(2)}) collective-permute-start(f32[8,32,256]{2,1,0:T(8,128)S(1)} %all-to-all-done.1.refs_0_), channel_id=1, source_target_pairs={{0,16},{8,24},{16,0},{24,8},{1,17},{9,25},{17,1},{25,9},{2,18},{10... | collective-permute-start | bytes 786440 | tf_op jit(solution)/shard_map/ppermute | solution.py:15
  65.0 9.2 %collective-permute-start.9 = (f32[8,32,256]{2,1,0:T(8,128)S(1)}, f32[8,32,256]{2,1,0:T(8,128)S(1)}, u32[]{:S(2)}, u32[]{:S(2)}) collective-permute-start(f32[8,32,256]{2,1,0:T(8,128)S(1)} %all-to-all-done.1.refs_0_), channel_id=1, source_target_pairs={{0,24},{8,0},{16,8},{24,16},{1,25},{9,1},{17,9},{25,17},{2,26},{10... | collective-permute-start | bytes 786440 | tf_op jit(solution)/shard_map/ppermute | solution.py:15
  66.3 8.6 %collective-permute-start.7 = (f32[8,32,256]{2,1,0:T(8,128)S(1)}, f32[8,32,256]{2,1,0:T(8,128)S(1)}, u32[]{:S(2)}, u32[]{:S(2)}) collective-permute-start(f32[8,32,256]{2,1,0:T(8,128)S(1)} %all-to-all-done.1.refs_0_), channel_id=1, source_target_pairs={{0,8},{8,16},{16,24},{24,0},{1,9},{9,17},{17,25},{25,1},{2,10},{10... | collective-permute-start | bytes 786440 | tf_op jit(solution)/shard_map/ppermute | solution.py:15
  74.3 2.8 %collective-permute-start.12 = (f32[2,8,32,256]{3,2,1,0:T(8,128)S(1)}, f32[2,8,32,256]{3,2,1,0:T(8,128)S(1)}, u32[]{:S(2)}, u32[]{:S(2)}) collective-permute-start(f32[2,8,32,256]{3,2,1,0:T(8,128)S(1)} %pad_maximum_fusion), channel_id=1, source_target_pairs={{0,4},{4,0},{1,5},{5,1},{2,6},{6,2},{3,7},{7,3},{8,12},{12,8},{9,1... | collective-permute-start | bytes 1572872 | tf_op jit(solution)/shard_map/ppermute | solution.py:15
  74.4 2.3 %collective-permute-start.10 = (f32[8,32,256]{2,1,0:T(8,128)S(1)}, f32[8,32,256]{2,1,0:T(8,128)S(1)}, u32[]{:S(2)}, u32[]{:S(2)}) collective-permute-start(f32[8,32,256]{2,1,0:T(8,128)S(1)} %all-to-all-done.1.refs_0_), channel_id=1, source_target_pairs={{0,4},{4,0},{1,5},{5,1},{2,6},{6,2},{3,7},{7,3},{8,12},{12,8},{9,1... | collective-permute-start | bytes 786440 | tf_op jit(solution)/shard_map/ppermute | solution.py:15
  74.9 2.1 %collective-permute-start.11 = (f32[8,32,256]{2,1,0:T(8,128)S(1)}, f32[8,32,256]{2,1,0:T(8,128)S(1)}, u32[]{:S(2)}, u32[]{:S(2)}) collective-permute-start(f32[8,32,256]{2,1,0:T(8,128)S(1)} %collective-permute-done.7.refs_1_), channel_id=1, source_target_pairs={{0,4},{4,0},{1,5},{5,1},{2,6},{6,2},{3,7},{7,3},{8,12},{12,8},{9,1... | collective-permute-start | bytes 786440 | tf_op jit(solution)/shard_map/ppermute | solution.py:15
  78.5 98.8 %copy-start.7 = (f32[1,128,512]{2,1,0:T(8,128)S(1)}, f32[1,128,512]{2,1,0:T(8,128)}, u32[]{:S(2)}) copy-start(f32[1,128,512]{2,1,0:T(8,128)} %get-tuple-element.133.refs_4_) | copy-start | bytes 786436
  78.5 118.6 %copy-start.18 = (f32[32,256]{1,0:T(8,128)S(1)}, f32[32,256]{1,0:T(8,128)}, u32[]{:S(2)}) copy-start(f32[32,256]{1,0:T(8,128)} %copy-done.17) | copy-start | bytes 98308
  78.5 8.0 %collective-permute-start.13 = (f32[128,256]{1,0:T(8,128)S(1)}, f32[128,256]{1,0:T(8,128)S(1)}, u32[]{:S(2)}, u32[]{:S(2)}) collective-permute-start(f32[128,256]{1,0:T(8,128)S(1)} %shard_map.62), channel_id=1, source_target_pairs={{0,2},{1,3},{2,0},{3,1},{4,6},{5,7},{6,4},{7,5},{8,10},{9,11},{10,... | collective-permute-start | bytes 393224 | tf_op jit(solution)/shard_map/ppermute | solution.py:15
  80.8 7.8 %collective-permute-start.14 = (f32[128,256]{1,0:T(8,128)S(1)}, f32[128,256]{1,0:T(8,128)S(1)}, u32[]{:S(2)}, u32[]{:S(2)}) collective-permute-start(f32[128,256]{1,0:T(8,128)S(1)} %shard_map.62), channel_id=1, source_target_pairs={{0,1},{1,2},{2,3},{3,0},{4,5},{5,6},{6,7},{7,4},{8,9},{9,10},{10,1... | collective-permute-start | bytes 393224 | tf_op jit(solution)/shard_map/ppermute | solution.py:15
  80.8 7.8 %collective-permute-start.15 = (f32[128,256]{1,0:T(8,128)S(1)}, f32[128,256]{1,0:T(8,128)S(1)}, u32[]{:S(2)}, u32[]{:S(2)}) collective-permute-start(f32[128,256]{1,0:T(8,128)S(1)} %shard_map.62), channel_id=1, source_target_pairs={{0,3},{1,0},{2,1},{3,2},{4,7},{5,4},{6,5},{7,6},{8,11},{9,8},{10,9... | collective-permute-start | bytes 393224 | tf_op jit(solution)/shard_map/ppermute | solution.py:15
  88.6 6.8 %collective-permute-start.16 = (f32[128,256]{1,0:T(8,128)S(1)}, f32[128,256]{1,0:T(8,128)S(1)}, u32[]{:S(2)}, u32[]{:S(2)}) collective-permute-start(f32[128,256]{1,0:T(8,128)S(1)} %slice_subtract_fusion.1.refs_0_), channel_id=1, source_target_pairs={{0,8},{8,16},{16,24},{24,0},{1,9},{9,17},{17,25},{25,1},{2,10},{10... | collective-permute-start | bytes 393224 | tf_op jit(solution)/shard_map/ppermute | solution.py:15
  90.4 8.5 %collective-permute-start.17 = (f32[128,256]{1,0:T(8,128)S(1)}, f32[128,256]{1,0:T(8,128)S(1)}, u32[]{:S(2)}, u32[]{:S(2)}) collective-permute-start(f32[128,256]{1,0:T(8,128)S(1)} %slice_subtract_fusion.1.refs_0_), channel_id=1, source_target_pairs={{0,16},{8,24},{16,0},{24,8},{1,17},{9,25},{17,1},{25,9},{2,18},{10... | collective-permute-start | bytes 393224 | tf_op jit(solution)/shard_map/ppermute | solution.py:15
  92.8 6.1 %collective-permute-start.18 = (f32[128,256]{1,0:T(8,128)S(1)}, f32[128,256]{1,0:T(8,128)S(1)}, u32[]{:S(2)}, u32[]{:S(2)}) collective-permute-start(f32[128,256]{1,0:T(8,128)S(1)} %slice_subtract_fusion.1.refs_0_), channel_id=1, source_target_pairs={{0,24},{8,0},{16,8},{24,16},{1,25},{9,1},{17,9},{25,17},{2,26},{10... | collective-permute-start | bytes 393224 | tf_op jit(solution)/shard_map/ppermute | solution.py:15
  103.9 1.6 collective-permute-start.19
  106.3 18.1 %all-to-all-start.2 = ((f32[8,32,256]{2,1,0:T(8,128)}), f32[8,32,256]{2,1,0:T(8,128)S(1)}, u32[]{:S(2)}, u32[]{:S(2)}) async-start(f32[8,32,256]{2,1,0:T(8,128)} %add.72), calls=%async_computation.2 | async-start | bytes 524288 | tf_op jit(solution)/shard_map/all_to_all | solution.py:271
  112.2 12.2 %collective-permute-start.20 = (f32[1,128,512]{2,1,0:T(8,128)}, f32[1,128,512]{2,1,0:T(8,128)S(1)}, u32[]{:S(2)}, u32[]{:S(2)}) collective-permute-start(f32[1,128,512]{2,1,0:T(8,128)} %get-tuple-element.122), channel_id=1, source_target_pairs={{0,16},{8,24},{16,0},{24,8},{1,17},{9,25},{17,1},{25,9},{2,18},{10... | collective-permute-start | bytes 786440 | tf_op jit(solution)/shard_map/ppermute | solution.py:15
  125.1 15.2 %all-to-all-start.3 = ((f32[8,32,256]{2,1,0:T(8,128)}), f32[8,32,256]{2,1,0:T(8,128)S(1)}, u32[]{:S(2)}, u32[]{:S(2)}) async-start(f32[8,32,256]{2,1,0:T(8,128)} %broadcast_in_dim.7), calls=%async_computation.3 | async-start | bytes 524288 | tf_op jit(solution)/shard_map/all_to_all | solution.py:274
  129.6 8.0 %collective-permute-start.21 = (f32[1,128,512]{2,1,0:T(8,128)}, f32[1,128,512]{2,1,0:T(8,128)S(1)}, u32[]{:S(2)}, u32[]{:S(2)}) collective-permute-start(f32[1,128,512]{2,1,0:T(8,128)} %get-tuple-element.130), channel_id=1, source_target_pairs={{0,8},{8,16},{16,24},{24,0},{1,9},{9,17},{17,25},{25,1},{2,10},{10... | collective-permute-start | bytes 786440 | tf_op jit(solution)/shard_map/ppermute | solution.py:15
  130.4 7.2 %collective-permute-start.22 = (f32[1,128,512]{2,1,0:T(8,128)}, f32[1,128,512]{2,1,0:T(8,128)S(1)}, u32[]{:S(2)}, u32[]{:S(2)}) collective-permute-start(f32[1,128,512]{2,1,0:T(8,128)} %get-tuple-element.131), channel_id=1, source_target_pairs={{0,24},{8,0},{16,8},{24,16},{1,25},{9,1},{17,9},{25,17},{2,26},{10... | collective-permute-start | bytes 786440 | tf_op jit(solution)/shard_map/ppermute | solution.py:15
  140.3 9.6 %collective-permute-start.24 = (f32[8,32,256]{2,1,0:T(8,128)S(1)}, f32[8,32,256]{2,1,0:T(8,128)S(1)}, u32[]{:S(2)}, u32[]{:S(2)}) collective-permute-start(f32[8,32,256]{2,1,0:T(8,128)S(1)} %all-to-all-done.3.refs_0_), channel_id=1, source_target_pairs={{0,16},{8,24},{16,0},{24,8},{1,17},{9,25},{17,1},{25,9},{2,18},{10... | collective-permute-start | bytes 786440 | tf_op jit(solution)/shard_map/ppermute | solution.py:15
  141.7 10.7 %collective-permute-start.25 = (f32[8,32,256]{2,1,0:T(8,128)S(1)}, f32[8,32,256]{2,1,0:T(8,128)S(1)}, u32[]{:S(2)}, u32[]{:S(2)}) collective-permute-start(f32[8,32,256]{2,1,0:T(8,128)S(1)} %all-to-all-done.3.refs_0_), channel_id=1, source_target_pairs={{0,24},{8,0},{16,8},{24,16},{1,25},{9,1},{17,9},{25,17},{2,26},{10... | collective-permute-start | bytes 786440 | tf_op jit(solution)/shard_map/ppermute | solution.py:15
  143.8 9.5 %collective-permute-start.23 = (f32[8,32,256]{2,1,0:T(8,128)S(1)}, f32[8,32,256]{2,1,0:T(8,128)S(1)}, u32[]{:S(2)}, u32[]{:S(2)}) collective-permute-start(f32[8,32,256]{2,1,0:T(8,128)S(1)} %all-to-all-done.3.refs_0_), channel_id=1, source_target_pairs={{0,8},{8,16},{16,24},{24,0},{1,9},{9,17},{17,25},{25,1},{2,10},{10... | collective-permute-start | bytes 786440 | tf_op jit(solution)/shard_map/ppermute | solution.py:15
  152.5 3.0 %collective-permute-start.28 = (f32[2,8,32,256]{3,2,1,0:T(8,128)S(1)}, f32[2,8,32,256]{3,2,1,0:T(8,128)S(1)}, u32[]{:S(2)}, u32[]{:S(2)}) collective-permute-start(f32[2,8,32,256]{3,2,1,0:T(8,128)S(1)} %pad_maximum_fusion.1), channel_id=1, source_target_pairs={{0,4},{4,0},{1,5},{5,1},{2,6},{6,2},{3,7},{7,3},{8,12},{12,8},{9,1... | collective-permute-start | bytes 1572872 | tf_op jit(solution)/shard_map/ppermute | solution.py:15
  152.8 2.3 %collective-permute-start.26 = (f32[8,32,256]{2,1,0:T(8,128)S(1)}, f32[8,32,256]{2,1,0:T(8,128)S(1)}, u32[]{:S(2)}, u32[]{:S(2)}) collective-permute-start(f32[8,32,256]{2,1,0:T(8,128)S(1)} %all-to-all-done.3.refs_0_), channel_id=1, source_target_pairs={{0,4},{4,0},{1,5},{5,1},{2,6},{6,2},{3,7},{7,3},{8,12},{12,8},{9,1... | collective-permute-start | bytes 786440 | tf_op jit(solution)/shard_map/ppermute | solution.py:15
  153.3 2.1 %collective-permute-start.27 = (f32[8,32,256]{2,1,0:T(8,128)S(1)}, f32[8,32,256]{2,1,0:T(8,128)S(1)}, u32[]{:S(2)}, u32[]{:S(2)}) collective-permute-start(f32[8,32,256]{2,1,0:T(8,128)S(1)} %collective-permute-done.23.refs_1_), channel_id=1, source_target_pairs={{0,4},{4,0},{1,5},{5,1},{2,6},{6,2},{3,7},{7,3},{8,12},{12,8},{9,1... | collective-permute-start | bytes 786440 | tf_op jit(solution)/shard_map/ppermute | solution.py:15
  157.0 8.0 %collective-permute-start.29 = (f32[128,256]{1,0:T(8,128)S(1)}, f32[128,256]{1,0:T(8,128)S(1)}, u32[]{:S(2)}, u32[]{:S(2)}) collective-permute-start(f32[128,256]{1,0:T(8,128)S(1)} %add.73), channel_id=1, source_target_pairs={{0,2},{1,3},{2,0},{3,1},{4,6},{5,7},{6,4},{7,5},{8,10},{9,11},{10,... | collective-permute-start | bytes 393224 | tf_op jit(solution)/shard_map/ppermute | solution.py:15
  158.7 6.8 %collective-permute-start.30 = (f32[128,256]{1,0:T(8,128)S(1)}, f32[128,256]{1,0:T(8,128)S(1)}, u32[]{:S(2)}, u32[]{:S(2)}) collective-permute-start(f32[128,256]{1,0:T(8,128)S(1)} %add.73), channel_id=1, source_target_pairs={{0,1},{1,2},{2,3},{3,0},{4,5},{5,6},{6,7},{7,4},{8,9},{9,10},{10,1... | collective-permute-start | bytes 393224 | tf_op jit(solution)/shard_map/ppermute | solution.py:15
  158.8 8.1 %collective-permute-start.31 = (f32[128,256]{1,0:T(8,128)S(1)}, f32[128,256]{1,0:T(8,128)S(1)}, u32[]{:S(2)}, u32[]{:S(2)}) collective-permute-start(f32[128,256]{1,0:T(8,128)S(1)} %add.73), channel_id=1, source_target_pairs={{0,3},{1,0},{2,1},{3,2},{4,7},{5,4},{6,5},{7,6},{8,11},{9,8},{10,9... | collective-permute-start | bytes 393224 | tf_op jit(solution)/shard_map/ppermute | solution.py:15
  167.0 6.8 %collective-permute-start.32 = (f32[128,256]{1,0:T(8,128)S(1)}, f32[128,256]{1,0:T(8,128)S(1)}, u32[]{:S(2)}, u32[]{:S(2)}) collective-permute-start(f32[128,256]{1,0:T(8,128)S(1)} %slice_subtract_fusion.refs_0_), channel_id=1, source_target_pairs={{0,8},{8,16},{16,24},{24,0},{1,9},{9,17},{17,25},{25,1},{2,10},{10... | collective-permute-start | bytes 393224 | tf_op jit(solution)/shard_map/ppermute | solution.py:15
  168.0 9.3 %collective-permute-start.33 = (f32[128,256]{1,0:T(8,128)S(1)}, f32[128,256]{1,0:T(8,128)S(1)}, u32[]{:S(2)}, u32[]{:S(2)}) collective-permute-start(f32[128,256]{1,0:T(8,128)S(1)} %slice_subtract_fusion.refs_0_), channel_id=1, source_target_pairs={{0,16},{8,24},{16,0},{24,8},{1,17},{9,25},{17,1},{25,9},{2,18},{10... | collective-permute-start | bytes 393224 | tf_op jit(solution)/shard_map/ppermute | solution.py:15
  171.1 6.2 %collective-permute-start.34 = (f32[128,256]{1,0:T(8,128)S(1)}, f32[128,256]{1,0:T(8,128)S(1)}, u32[]{:S(2)}, u32[]{:S(2)}) collective-permute-start(f32[128,256]{1,0:T(8,128)S(1)} %slice_subtract_fusion.refs_0_), channel_id=1, source_target_pairs={{0,24},{8,0},{16,8},{24,16},{1,25},{9,1},{17,9},{25,17},{2,26},{10... | collective-permute-start | bytes 393224 | tf_op jit(solution)/shard_map/ppermute | solution.py:15
  178.6 1.6 collective-permute-start.35
  (15 other events, 164.5 us)
